TPU v7x, 256 devices: a whole 4x4x8 slice. The times are simulated.
256 devices in a mesh: pb: 4 (over y), neg: 64 (over z, x, core).
Axes of the slice: x: 4, y: 4, z: 8, core: 2. Of those that a mesh axis runs over, the one named last changes fastest.
Arguments:
- hidden: bfloat16 [4, 256, 128, 1024], P('pb', 'neg'), may hold values from -6 to 6
- lengths: int32 [4, 256], P('pb', 'neg'), may hold values from 32 to 128
- teacher: float32 [4, 256], P('pb', 'neg'), may hold values from -8 to 8
- norm_gain: float32 [1024], replicated, may hold values from 0.1 to 1.9
- final_gain: float32 [1024], replicated, may hold values from 0.1 to 1.9
- score_vector: float32 [1024], replicated, may hold values from -0.1875 to 0.1875
- query_weight: bfloat16 [1024, 1024], P(('pb', 'neg')), may hold values from -0.1875 to 0.1875
- key_matrix: bfloat16 [1024, 512], P(('pb', 'neg')), may hold values from -0.1875 to 0.1875
- value_matrix: bfloat16 [1024, 512], P(('pb', 'neg')), may hold values from -0.1875 to 0.1875
- out_weight: bfloat16 [1024, 1024], P(None, ('pb', 'neg')), may hold values from -0.1875 to 0.1875
Outputs:
- scores: float32 [4, 256], P('pb', 'neg')
- loss: float32 [], replicated
- grad_hidden: bfloat16 [4, 256, 128, 1024], P('pb', 'neg')
- grad_query: float32 [1024, 1024], P(('pb', 'neg'))
- grad_key: float32 [1024, 512], P(('pb', 'neg'))
- grad_value: float32 [1024, 512], P(('pb', 'neg'))
- grad_out: float32 [1024, 1024], P(None, ('pb', 'neg'))
Inputs may be any that keep to these rules, and one draw needn't show every extreme that they name: `lengths`: the number of real tokens of the pair; its other positions out of 128 are padding.
All inputs are finite; a program needn't handle non-finite values.
Results may differ from a plain program's by a relative error of at most 0.013.
Values may be sent and summed in bfloat16 or wider, within the bound.
No kernel may reach another device: no remote copies, remote signals or barrier semaphores. Data moves between devices by JAX's collectives and lax.ppermute only.
A program may use at most 64 MiB of HBM per device.

v0:
```python
import jax
import jax.numpy as jnp
import numpy as np
from jax import lax
from jax.experimental import pallas as pl
from jax.experimental.pallas import tpu as pltpu
from jax.sharding import Mesh
from jax.sharding import PartitionSpec as P

HW = 128
AXES = ("pb", "z", "x", "c")
NEG = ("z", "x", "c")
EPS = 1e-06
ROPE_BASE = 1000000.0
GRAD_SCALE = 512.0
PAIRS = 4
SEQ = 128
D = 1024
ROWS = PAIRS * SEQ
F32 = jnp.float32
BF16 = jnp.bfloat16
SM = pl.BlockSpec(memory_space=pltpu.SMEM)
LAST = (((1,), (1,)), ((), ()))
FIRST = (((0,), (0,)), ((), ()))
SCALE = HW ** (-0.5)


def rope_consts():
    freqs = np.float32(ROPE_BASE) ** (-(np.arange(HW // 2, dtype=np.float32) * 2.0) / HW)
    angles = np.arange(SEQ, dtype=np.float32)[:, None] * freqs.astype(np.float32)[None, :]
    angles = np.concatenate([angles, angles], axis=1)
    sign = np.where(np.arange(HW) < HW // 2, -1.0, 1.0)
    return (
        np.cos(angles).astype(np.float32),
        (np.sin(angles) * sign[None, :]).astype(np.float32),
    )


def whole(shape):
    return pl.BlockSpec(shape, lambda i: (0,) * len(shape), pipeline_mode=pl.Buffered(1))


def call(body, scalars, arrays, outs, scratch=(), flops=0, grant=52):
    moved = sum(a.size * a.dtype.itemsize for a in arrays)
    moved += sum(int(np.prod(o)) * np.dtype(d).itemsize for o, d in outs)
    return pl.pallas_call(
        body,
        grid=(1,),
        out_shape=[jax.ShapeDtypeStruct(o, d) for o, d in outs],
        in_specs=[SM] * len(scalars) + [whole(a.shape) for a in arrays],
        out_specs=[whole(o) for o, _ in outs],
        scratch_shapes=[pltpu.VMEM(o, d) for o, d in scratch],
        compiler_params=pltpu.CompilerParams(vmem_limit_bytes=grant << 20),
        cost_estimate=pl.CostEstimate(flops=flops, bytes_accessed=moved, transcendentals=0),
    )(*scalars, *arrays)


def block_at(me, step, width):
    return pl.ds(pl.multiple_of(lax.rem(me + step + 4, 4) * width, width), width)


def dot(a, b, dims=(((1,), (0,)), ((), ()))):
    return lax.dot_general(a, b, dims, preferred_element_type=F32)


def half_turn(v):
    return pltpu.roll(v, HW // 2, 1)


def heads(v, n):
    return [v[:, i * HW : (i + 1) * HW] for i in range(n)]


def block_mask():
    row = lax.broadcasted_iota(jnp.int32, (8, 512), 0)
    lane = lax.broadcasted_iota(jnp.int32, (8, 512), 1)
    return (lane // HW) == (row // 2), (row % 2) == 0


def to_blocks(row, mask, even):
    h = heads(row, 8)
    e = jnp.broadcast_to(jnp.concatenate(h[0::2], axis=1), (8, 512))
    o = jnp.broadcast_to(jnp.concatenate(h[1::2], axis=1), (8, 512))
    return jnp.where(mask, jnp.where(even, e, o), 0.0)


def from_blocks(blocks, mask, even):
    e = jnp.sum(jnp.where(mask & even, blocks, 0.0), axis=0, keepdims=True)
    o = jnp.sum(jnp.where(mask & (~even), blocks, 0.0), axis=0, keepdims=True)
    parts = []
    for g in range(4):
        parts += [e[:, g * HW : (g + 1) * HW], o[:, g * HW : (g + 1) * HW]]
    return jnp.concatenate(parts, axis=1)


def prep_body(len_ref, h_ref, gain_ref, normed_ref, turned_ref, nlast_ref, xlast_ref):
    row = lax.broadcasted_iota(jnp.int32, (8, SEQ), 0)
    lane = lax.broadcasted_iota(jnp.int32, (8, SEQ), 1)
    nl = jnp.zeros((8, D), F32)
    xl = jnp.zeros((8, D), F32)
    for p in range(PAIRS):
        raw = h_ref[p * SEQ : (p + 1) * SEQ, :]
        x = raw.astype(F32)
        inv = lax.rsqrt(jnp.mean(x * x, axis=-1, keepdims=True) + EPS)
        n = (x * inv * gain_ref[...]).astype(BF16)
        normed_ref[p * SEQ : (p + 1) * SEQ, :] = n
        turned_ref[:, p * SEQ : (p + 1) * SEQ] = n.T
        e = len_ref[p] - 1
        hot = jnp.where((row == p) & (lane == e), 1.0, 0.0).astype(BF16)
        nl = nl + dot(hot, n)
        xl = xl + dot(hot, raw)
    nlast_ref[...] = nl.astype(BF16)
    xlast_ref[...] = xl


def arrange_body(at_ref, *refs):
    a_refs, out_ref = refs[0:4], refs[4]
    x = at_ref[1]
    for d in range(4):
        out_ref[:, pl.ds(lax.rem(x - d + 4, 4), 1)] = a_refs[d][...].reshape(8, 1, 8, 1024)


def attend_body(at_ref, len_ref, normed_ref, nlast_ref, cos_ref, sin_ref, *refs):
    kv_refs, q_refs = refs[0:2], (refs[2:6], refs[6:10])
    kproj_ref, krot_ref, vcast_ref, qproj_ref, qrot_ref, attn_ref, ctx_ref, qr_scr, ctx_scr = refs[10:]
    x = at_ref[1]
    mask, even = block_mask()
    lane = lax.broadcasted_iota(jnp.int32, (8, SEQ), 1)
    for half in range(2):
        kv_ref = kv_refs[half]

        @pl.loop(0, PAIRS)
        def _(p):
            rows = pl.ds(pl.multiple_of(p * SEQ, SEQ), SEQ)
            kv = dot(normed_ref[rows, :], kv_ref[...])
            kproj_ref[rows, half * 256 : half * 256 + 256] = kv[:, 0:256]
            vcast_ref[rows, half * 256 : half * 256 + 256] = kv[:, 256:512].astype(BF16)

        q = jnp.zeros((8, 512), F32)
        for d in range(4):
            q = q + dot(nlast_ref[:, block_at(x, -d, 256)], q_refs[half][d][...])
        qproj_ref[:, half * 512 : half * 512 + 512] = q
    cos_q = jnp.concatenate(
        [cos_ref[pl.ds(len_ref[p] - 1, 1), :] for p in range(PAIRS)] * 2, axis=0
    )
    sin_q = jnp.concatenate(
        [sin_ref[pl.ds(len_ref[p] - 1, 1), :] for p in range(PAIRS)] * 2, axis=0
    )
    for h in range(8):
        q = qproj_ref[:, h * HW : (h + 1) * HW]
        u = q * lax.rsqrt(jnp.mean(q * q, axis=-1, keepdims=True) + EPS)
        r = u * cos_q + half_turn(u) * sin_q
        qr_scr[:, h * HW : (h + 1) * HW] = r
        qrot_ref[:, h * HW : (h + 1) * HW] = r.astype(BF16)
    ctx_scr[...] = jnp.zeros((8, D), F32)
    for p in range(PAIRS):
        rows = slice(p * SEQ, (p + 1) * SEQ)
        for g in range(4):
            k = kproj_ref[rows, g * HW : (g + 1) * HW]
            u = k * lax.rsqrt(jnp.mean(k * k, axis=-1, keepdims=True) + EPS)
            r = u * cos_ref[...] + half_turn(u) * sin_ref[...]
            krot_ref[rows, g * HW : (g + 1) * HW] = r.astype(BF16)
        qb = to_blocks(qr_scr[p : p + 1, :], mask, even).astype(BF16)
        logits = dot(qb, krot_ref[rows, :], LAST) * SCALE
        ex = jnp.where(lane <= len_ref[p] - 1, jnp.exp(logits), 0.0)
        w = ex / jnp.sum(ex, axis=-1, keepdims=True)
        attn_ref[p * 8 : (p + 1) * 8, :] = w
        c = dot(w.astype(BF16), vcast_ref[rows, :])
        ctx_scr[p : p + 1, :] = from_blocks(c, mask, even)
    ctx_ref[...] = ctx_scr[...].astype(BF16)


def score_body(teach_ref, ctx_ref, xlast_ref, fg_ref, sv_ref, oa_ref, ob_ref, *refs):
    unit_ref, oscale_ref, score_ref, tot_ref, line_ref = refs
    res = xlast_ref[...] + (
        dot(ctx_ref[:, 0:512], oa_ref[...], LAST) + dot(ctx_ref[:, 512:1024], ob_ref[...], LAST)
    )
    sc = lax.rsqrt(jnp.mean(res * res, axis=-1, keepdims=True) + EPS)
    unit = res * sc
    unit_ref[...] = unit
    oscale_ref[...] = jnp.broadcast_to(sc, (8, HW))
    s = jnp.sum(unit * fg_ref[...] * sv_ref[...], axis=-1, keepdims=True)
    s = jnp.broadcast_to(s, (8, HW))
    score_ref[...] = s
    row = lax.broadcasted_iota(jnp.int32, (8, HW), 0)
    lane = lax.broadcasted_iota(jnp.int32, (8, HW), 1)
    line_ref[...] = jnp.sum(jnp.where(row == lane, s, 0.0), axis=0, keepdims=True)[:, 0:PAIRS]
    scaled = teach_ref[...] / 2.0
    es = jnp.exp(s)
    et = jnp.exp(scaled)
    v = jnp.where(lane == 0, es, jnp.where(lane == 1, et, et * (scaled - s)))
    v = jnp.where((row < PAIRS) & (lane < 3), v, 0.0)
    tot_ref[...] = jnp.broadcast_to(jnp.sum(v, axis=0, keepdims=True), (8, HW))


def unit_back_body(
    len_ref,
    krot_ref,
    vcast_ref,
    kproj_ref,
    qproj_ref,
    qrot_ref,
    attn_ref,
    unit_ref,
    oscale_ref,
    fg_ref,
    sv_ref,
    cos_ref,
    sin_ref,
    *refs,
):
    oa_ref, ob_ref, gkva_ref, gkvb_ref, gq_ref, gr_ref, gc_scr, gq_scr, qr_scr = refs
    mask, even = block_mask()
    unit = unit_ref[...]
    gu = sv_ref[...] * fg_ref[...]
    gr = oscale_ref[:, 0:1] * (gu - unit * jnp.mean(gu * unit, axis=-1, keepdims=True))
    gr_ref[...] = gr
    grb = gr.astype(BF16)
    gc_scr[:, 0:512] = dot(grb, oa_ref[...])
    gc_scr[:, 512:1024] = dot(grb, ob_ref[...])
    qr_scr[...] = qrot_ref[...].astype(F32)
    gq_scr[...] = jnp.zeros((8, D), F32)
    for p in range(PAIRS):
        rows = slice(p * SEQ, (p + 1) * SEQ)
        gb = to_blocks(gc_scr[p : p + 1, :], mask, even).astype(BF16)
        qb = to_blocks(qr_scr[p : p + 1, :], mask, even).astype(BF16)
        w = attn_ref[p * 8 : (p + 1) * 8, :]
        gp = dot(gb, vcast_ref[rows, :], LAST)
        gv = dot(w.astype(BF16), gb, FIRST)
        gkva_ref[rows, 256:512] = gv[:, 0:256]
        gkvb_ref[rows, 256:512] = gv[:, 256:512]
        spread = jnp.sum(w * gp, axis=-1, keepdims=True)
        dl = (w * (gp - spread)).astype(BF16)
        gq_scr[p : p + 1, :] = from_blocks(dot(dl, krot_ref[rows, :]) * SCALE, mask, even)
        gk = dot(dl, qb, FIRST) * SCALE
        for g in range(4):
            k = kproj_ref[rows, g * HW : (g + 1) * HW]
            sc = lax.rsqrt(jnp.mean(k * k, axis=-1, keepdims=True) + EPS)
            u = k * sc
            r = gk[:, g * HW : (g + 1) * HW]
            t = r * cos_ref[...] + half_turn(r * sin_ref[...])
            out = sc * (t - u * jnp.mean(t * u, axis=-1, keepdims=True))
            ref = gkva_ref if g < 2 else gkvb_ref
            ref[rows, (g % 2) * HW : (g % 2 + 1) * HW] = out
    cos_q = jnp.concatenate(
        [cos_ref[pl.ds(len_ref[p] - 1, 1), :] for p in range(PAIRS)] * 2, axis=0
    )
    sin_q = jnp.concatenate(
        [sin_ref[pl.ds(len_ref[p] - 1, 1), :] for p in range(PAIRS)] * 2, axis=0
    )
    for h in range(8):
        q = qproj_ref[:, h * HW : (h + 1) * HW]
        sc = lax.rsqrt(jnp.mean(q * q, axis=-1, keepdims=True) + EPS)
        u = q * sc
        r = gq_scr[:, h * HW : (h + 1) * HW]
        t = r * cos_q + half_turn(r * sin_q)
        gq_ref[:, h * HW : (h + 1) * HW] = sc * (
            t - u * jnp.mean(t * u, axis=-1, keepdims=True)
        )


def weight_pieces(x, half, turned_ref, nlast_ref, skv_ref, sq_ref, srow_ref, sturn_ref, ctx_ref, store):
    low = slice(half * 512, half * 512 + 256)
    high = slice(half * 512 + 256, half * 512 + 512)

    @pl.loop(0, 4)
    def _(i):
        rows = pl.ds(pl.multiple_of(i * 256, 256), 256)
        kv = dot(turned_ref[rows, :], skv_ref[...])
        o_low = dot(srow_ref[:, rows], ctx_ref[:, low], FIRST)
        rows_x = block_at(x, i, 256)
        q = dot(nlast_ref[:, rows_x], sq_ref[:, half * 512 : half * 512 + 512], FIRST)
        o_high = dot(sturn_ref[:, rows_x], ctx_ref[:, high], FIRST)
        store(pl.ds(i, 1), kv, o_low, q, o_high)


def weight_body(
    at_ref,
    tot_ref,
    score_ref,
    teach_ref,
    gkva_ref,
    gkvb_ref,
    gq_ref,
    gr_ref,
    grturn_ref,
    turned_ref,
    nlast_ref,
    ctx_ref,
    *refs,
):
    out_a, out_b, loss_ref, skva_ref, skvb_ref, sq_ref, sr_ref, srow_ref, sturn_ref = refs
    pb, x = at_ref[0], at_ref[1]
    lane = lax.broadcasted_iota(jnp.int32, (1, HW), 1)

    def pick(v, i):
        return jnp.sum(jnp.where(lane == i, v, 0.0), axis=-1, keepdims=True)

    loss = jnp.zeros((1, 1), F32)
    mine = jnp.zeros((1, HW), F32)
    for q in range(4):
        t = jnp.sum(tot_ref[q * 64 : (q + 1) * 64, :], axis=0, keepdims=True)
        ts, tt, cr = pick(t, 0), pick(t, 1), pick(t, 2)
        loss = loss + (cr / tt - jnp.log(tt) + jnp.log(ts))
        mine = mine + jnp.where(pb == q, t, 0.0)
    loss_ref[...] = loss
    ts, tt = pick(mine, 0), pick(mine, 1)
    row = lax.broadcasted_iota(jnp.int32, (8, HW), 0)
    g = GRAD_SCALE * (jnp.exp(score_ref[...]) / ts - jnp.exp(teach_ref[...] / 2.0) / tt)
    g = jnp.where(row < PAIRS, g, 0.0)
    gcol = g[:, 0:1]
    sr = gr_ref[...] * gcol
    sr_ref[...] = sr
    sq = (gq_ref[...] * gcol).astype(BF16)
    sq_ref[...] = sq
    for gkv_ref, s_ref in ((gkvb_ref, skvb_ref), (gkva_ref, skva_ref)):
        for p in range(PAIRS):
            rows = slice(p * SEQ, (p + 1) * SEQ)
            s_ref[rows, :] = (gkv_ref[rows, :] * gcol[p : p + 1, :]).astype(BF16)
    srow_ref[...] = sr.astype(BF16)
    sturn_ref[...] = (grturn_ref[...] * gcol).astype(BF16)

    def store(at, kv, o_low, q, o_high):
        out_a[at, :, 0:512] = kv.astype(BF16)[None]
        out_a[at, :, 512:768] = o_low.astype(BF16)[None]
        out_b[at, :, 0:512] = q.astype(BF16)[None]
        out_b[at, :, 512:768] = o_high.astype(BF16)[None]

    weight_pieces(
        x, 1, turned_ref, nlast_ref, skvb_ref, sq_ref, srow_ref, sturn_ref, ctx_ref, store
    )


def own_weight_body(
    at_ref,
    skva_ref,
    sq_ref,
    srow_ref,
    sturn_ref,
    turned_ref,
    nlast_ref,
    ctx_ref,
    add_a,
    add_b,
    out_a,
    *refs,
):
    outs_b, b_scr = refs[0:4], refs[4]

    def store(at, kv, o_low, q, o_high):
        out_a[at, :, 0:512] = (kv[None] + add_a[at, :, 0:512].astype(F32)).astype(BF16)
        out_a[at, :, 512:768] = (o_low[None] + add_a[at, :, 512:768].astype(F32)).astype(BF16)
        b_scr[at, :, 0:512] = (q[None] + add_b[at, :, 0:512].astype(F32)).astype(BF16)
        b_scr[at, :, 512:768] = (o_high[None] + add_b[at, :, 512:768].astype(F32)).astype(BF16)

    weight_pieces(
        at_ref[1], 0, turned_ref, nlast_ref, skva_ref, sq_ref, srow_ref, sturn_ref, ctx_ref, store
    )
    for d in range(4):
        outs_b[d][...] = b_scr[d]


def middle_body(at_ref, got_a_ref, *refs):
    b_refs, out_a, out_b, a_scr = refs[0:4], refs[4:8], refs[8], refs[9]
    x = at_ref[1]
    total_a = got_a_ref[0].astype(F32)
    total_b = b_refs[0][...].astype(F32)
    for d in range(1, 4):
        total_a = total_a + got_a_ref[d].astype(F32)
        total_b = total_b + b_refs[d][...].astype(F32)
    out_b[...] = total_b.astype(BF16)
    a_scr[...] = total_a.reshape(8, 4, 8, 768)
    for d in range(4):
        out_a[d][...] = a_scr[:, pl.ds(lax.rem(x + d, 4), 1)].reshape(64, 768).astype(BF16)


def last_body(at_ref, sq_ref, *refs):
    q_refs, out_ref = (refs[0:4], refs[4:8]), refs[8]
    x = at_ref[1]
    for d in range(4):
        out_ref[:, block_at(x, -d, 256)] = dot(sq_ref[:, 0:512], q_refs[0][d][...], LAST) + dot(
            sq_ref[:, 512:1024], q_refs[1][d][...], LAST
        )


def hidden_body(
    len_ref, h_ref, gain_ref, skva_ref, skvb_ref, last_ref, sr_ref, kva_ref, kvb_ref, out_ref
):
    pos = lax.broadcasted_iota(jnp.int32, (SEQ, 1), 0)

    @pl.loop(0, PAIRS)
    def _(p):
        rows = pl.ds(pl.multiple_of(p * SEQ, SEQ), SEQ)
        gn = dot(skva_ref[rows, :], kva_ref[...], LAST) + dot(
            skvb_ref[rows, :], kvb_ref[...], LAST
        )
        at = pos == len_ref[p] - 1
        gn = gn + jnp.where(at, last_ref[pl.ds(p, 1), :], 0.0)
        x = h_ref[rows, :].astype(F32)
        inv = lax.rsqrt(jnp.mean(x * x, axis=-1, keepdims=True) + EPS)
        s = gn * gain_ref[...]
        gi = inv * s - x * (inv * inv * inv * jnp.mean(s * x, axis=-1, keepdims=True))
        gi = gi + jnp.where(at, sr_ref[pl.ds(p, 1), :], 0.0)
        out_ref[rows, :] = gi.astype(BF16)


def everyone(x, axes, count):
    return lax.all_to_all(
        jnp.broadcast_to(x[None], (count, *x.shape)), axes, 0, 0, tiled=True
    )


def from_ring(x, axis):
    return [x] + [
        lax.ppermute(x, axis, [(i, (i + d) % 4) for i in range(4)]) for d in range(1, 4)
    ]


def along_ring(pieces, axis):
    return [pieces[0]] + [
        lax.ppermute(pieces[d], axis, [(i, (i + d) % 4) for i in range(4)]) for d in range(1, 4)
    ]


def chunk_turn(v):
    return jnp.transpose(v.reshape(8, 32, 4, 8), (0, 2, 1, 3)).reshape(8, D)


def chunk_back(v):
    return jnp.transpose(v.reshape(8, 4, 32, 8), (0, 2, 1, 3)).reshape(8, D)


def swap(x):
    return lax.ppermute(x, "c", [(0, 1), (1, 0)])


def shards(
    hidden,
    lengths,
    teacher,
    norm_gain,
    final_gain,
    score_vector,
    query_weight,
    key_matrix,
    value_matrix,
    out_weight,
):
    c = lax.axis_index("c")
    first = c == 0
    at = jnp.stack([lax.axis_index("pb"), lax.axis_index("x")]).astype(jnp.int32)
    tokens = hidden.reshape(ROWS, D)
    lens = lengths[0]
    gain = norm_gain[None]
    fg = final_gain[None]
    sv = score_vector[None]
    cos_np, sin_np = rope_consts()
    cos, sin = jnp.asarray(cos_np), jnp.asarray(sin_np)
    teach = jnp.broadcast_to(jnp.pad(teacher[0], (0, 4))[:, None], (8, HW))

    turned_out = out_weight.T
    halves = [
        jnp.concatenate(
            [
                key_matrix[:, h * 256 : h * 256 + 256],
                value_matrix[:, h * 256 : h * 256 + 256],
                query_weight[:, h * 512 : h * 512 + 512],
                turned_out[:, h * 512 : h * 512 + 512],
            ],
            axis=1,
        )
        for h in range(2)
    ]
    mine = jnp.where(first, halves[0], halves[1])
    theirs = swap(jnp.where(first, halves[1], halves[0]))
    block = jnp.concatenate(
        [jnp.where(first, mine, theirs), jnp.where(first, theirs, mine)], axis=0
    )
    wide = jnp.concatenate([block[:, 0:512], block[:, 1024:1536], block[:, 512:1024]], axis=1)
    column = everyone(wide, "z", 8).reshape(64, 1536)

    normed, turned, nlast, xlast = call(
        prep_body,
        [lens],
        [tokens, gain],
        [((ROWS, D), BF16), ((D, ROWS), BF16), ((8, D), BF16), ((8, D), F32)],
        flops=10_000_000,
    )
    nlast = chunk_turn(nlast)
    column, normed, turned, nlast, xlast = lax.optimization_barrier(
        (column, normed, turned, nlast, xlast)
    )
    (slab_a,) = call(
        arrange_body,
        [at],
        from_ring(column[:, 0:1024], "x"),
        [((8, 4, 8, 1024), BF16)],
    )
    slab_a = slab_a.reshape(256, 1024)
    slab_b = everyone(column[:, 1024:1536], "pb", 4).reshape(256, 512)
    slab_a, slab_b = lax.optimization_barrier((slab_a, slab_b))
    qa = from_ring(slab_b, "x")
    kva = everyone(slab_a[:, 0:512], "pb", 4).reshape(1024, 512)
    kva, qa, slab_o = lax.optimization_barrier((kva, qa, slab_a[:, 512:1024]))
    planes_o = everyone(slab_o, "pb", 4)
    kvb = swap(kva)
    qb = [swap(v) for v in qa]

    kproj, krot, vcast, qproj, qrot, attn, ctx = call(
        attend_body,
        [at, lens],
        [normed, nlast, cos, sin, kva, kvb, *qa, *qb],
        [
            ((ROWS, 512), F32),
            ((ROWS, 512), BF16),
            ((ROWS, 512), BF16),
            ((8, D), F32),
            ((8, D), BF16),
            ((32, SEQ), F32),
            ((8, D), BF16),
        ],
        [((8, D), F32), ((8, D), F32)],
        flops=1_100_000_000,
    )
    ctx, planes_o = lax.optimization_barrier((ctx, planes_o))
    oa = planes_o.reshape(1024, 512)
    ob = swap(oa)
    unit, oscale, score, tot, line = call(
        score_body,
        [],
        [teach, ctx, xlast, fg, sv, oa, ob],
        [((8, D), F32), ((8, HW), F32), ((8, HW), F32), ((8, HW), F32), ((1, PAIRS), F32)],
        flops=20_000_000,
    )

    totals = everyone(tot[0:1], AXES, 256).reshape(256, HW)

    gkva, gkvb, gq, gr = call(
        unit_back_body,
        [lens],
        [krot, vcast, kproj, qproj, qrot, attn, unit, oscale, fg, sv, cos, sin, oa, ob],
        [((ROWS, 512), F32), ((ROWS, 512), F32), ((8, D), F32), ((8, D), F32)],
        [((8, D), F32), ((8, D), F32), ((8, D), F32)],
        flops=200_000_000,
    )
    grturn = chunk_turn(gr)

    pieces = ((4, 256, 768), BF16)
    back_a, back_b, loss, skva, skvb, sq, sr, srow, sturn = call(
        weight_body,
        [at],
        [totals, score, teach, gkva, gkvb, gq, gr, grturn, turned, nlast, ctx],
        [
            pieces,
            pieces,
            ((1, 1), F32),
            ((ROWS, 512), BF16),
            ((ROWS, 512), BF16),
            ((8, D), BF16),
            ((8, D), F32),
            ((8, D), BF16),
            ((8, D), BF16),
        ],
        flops=600_000_000,
    )
    chip_a, *chip_b = call(
        own_weight_body,
        [at],
        [skva, sq, srow, sturn, turned, nlast, ctx, swap(back_a), swap(back_b)],
        [pieces] + [((256, 768), BF16)] * 4,
        [pieces],
        flops=600_000_000,
    )
    got_a = lax.all_to_all(chip_a, "pb", 0, 0, tiled=True)
    got_b = along_ring(chip_b, "x")
    (last,) = call(last_body, [at], [sq, *qa, *qb], [((8, D), F32)], flops=20_000_000)
    (grad_hidden,) = call(
        hidden_body,
        [lens],
        [tokens, gain, skva, skvb, chunk_back(last), sr, kva, kvb],
        [((ROWS, D), BF16)],
        flops=1_100_000_000,
    )
    got_a, got_b, grad_hidden = lax.optimization_barrier((got_a, got_b, grad_hidden))
    *mid_a, mid_b = call(
        middle_body,
        [at],
        [got_a, *got_b],
        [((64, 768), BF16)] * 4 + [((256, 768), BF16)],
        [((8, 4, 8, 768), F32)],
    )
    done_a = along_ring(mid_a, "x")
    done_b = lax.all_to_all(mid_b.reshape(4, 64, 768), "pb", 0, 0, tiled=True)

    def added(parts):
        total = parts[0].astype(F32)
        for part in parts[1:]:
            total = total + part.astype(F32)
        return total.astype(BF16)

    part = jnp.concatenate([added(done_a), added(done_b)], axis=1)
    rec = lax.all_to_all(part.reshape(8, 8, 1536), "z", 0, 0, tiled=True)
    rec = jnp.sum(rec.astype(F32), axis=0)
    reduced = jnp.concatenate(
        [rec[:, 0:512], rec[:, 768:1280], rec[:, 512:768], rec[:, 1280:1536]], axis=1
    )

    keep = jnp.where(first, reduced[0:4], reduced[4:8])
    got = swap(jnp.where(first, reduced[4:8], reduced[0:4]))
    low = jnp.where(first, keep, got)
    high = jnp.where(first, got, keep)

    def both(a, b):
        return jnp.concatenate([low[:, a:b], high[:, a:b]], axis=1)

    return (
        line,
        loss.reshape(()),
        grad_hidden.reshape(hidden.shape),
        both(512, 1024),
        both(0, 256),
        both(256, 512),
        both(1024, 1536).T,
    )


def solution(mesh):
    torus = Mesh(mesh.devices.reshape(mesh.shape["pb"], 8, 4, 2), AXES)
    placed = (
        P("pb", NEG, None, None),
        P("pb", NEG),
        P("pb", NEG),
        P(),
        P(),
        P(),
        P(AXES, None),
        P(AXES, None),
        P(AXES, None),
        P(None, AXES),
    )
    return jax.shard_map(
        shards,
        mesh=torus,
        in_specs=placed,
        out_specs=(
            P("pb", NEG),
            P(),
            P("pb", NEG, None, None),
            P(AXES, None),
            P(AXES, None),
            P(AXES, None),
            P(None, AXES),
        ),
        check_vma=False,
    )
```

profile of v0, /device:TPU:1, one launch (start us, length us, event | category | flops | bytes accessed | tf_op | source)
XLA Modules:
  0.0 195.3 jit_solution(12586501145794044740)
XLA Ops:
  2.1 3.3 %collective-permute-start = (bf16[4,1536]{1,0:T(4,128)(2,1)S(1)}, bf16[4,1536]{1,0:T(4,128)(2,1)S(1)}, u32[]{:S(2)}, u32[]{:S(2)}) collective-permute-start(bf16[4,1536]{1,0:T(4,128)(2,1)S(1)} %broadcast_select_fusion.4), channel_id=1, source_target_pairs={{0,1},{1,0},{2,3},{3,2},{4,5},{5,4},{6,7},{7,6},{8,9},{9,8},{10,11... | collective-permute-start | bytes 36872 | tf_op jit(solution)/shard_map/ppermute | solution.py:434
  7.1 6.5 %all-to-all-start = ((bf16[8,8,1536]{2,1,0:T(8,128)(2,1)}), bf16[8,8,1536]{2,1,0:T(8,128)(2,1)S(1)}, u32[]{:S(2)}, u32[]{:S(2)}) async-start(bf16[8,8,1536]{2,1,0:T(8,128)(2,1)} %broadcast_in_dim.21), calls=%async_computation | async-start | bytes 393216 | tf_op jit(solution)/shard_map/all_to_all | solution.py:408
  19.4 3.6 %all-to-all-done = bf16[8,8,1536]{2,1,0:T(8,128)(2,1)S(1)} async-done(((bf16[8,8,1536]{2,1,0:T(8,128)(2,1)}), bf16[8,8,1536]{2,1,0:T(8,128)(2,1)S(1)}, u32[]{:S(2)}, u32[]{:S(2)}) %all-to-all-start) | async-done | bytes 196640 | tf_op jit(solution)/shard_map/all_to_all | solution.py:408
  23.7 4.2 %all-to-all-start.1 = ((bf16[4,64,512]{2,1,0:T(8,128)(2,1)}), bf16[4,64,512]{2,1,0:T(8,128)(2,1)S(1)}, u32[]{:S(2)}, u32[]{:S(2)}) async-start(bf16[4,64,512]{2,1,0:T(8,128)(2,1)} %broadcast_in_dim.23), calls=%async_computation.1 | async-start | bytes 524288 | tf_op jit(solution)/shard_map/all_to_all | solution.py:408
  38.9 4.2 %all-to-all-start.2 = ((bf16[4,256,512]{2,1,0:T(8,128)(2,1)}), bf16[4,256,512]{2,1,0:T(8,128)(2,1)}, u32[]{:S(2)}, u32[]{:S(2)}) async-start(bf16[4,256,512]{2,1,0:T(8,128)(2,1)} %broadcast_in_dim.24), calls=%async_computation.2 | async-start | bytes 2097152 | tf_op jit(solution)/shard_map/all_to_all | solution.py:408
  44.9 3.5 %collective-permute-done.6.refs_5_.refs_3_ = bf16[256,512]{1,0:T(8,128)(2,1)S(1)} collective-permute-done((bf16[256,512]{1,0:T(8,128)(2,1)S(1)}, bf16[256,512]{1,0:T(8,128)(2,1)S(1)}, u32[]{:S(2)}, u32[]{:S(2)}) %collective-permute-start.6) | collective-permute-done | bytes 262176 | tf_op jit(solution)/shard_map/ppermute | solution.py:415
  50.6 6.5 %collective-permute-done.4.refs_3_.refs_1_ = bf16[256,512]{1,0:T(8,128)(2,1)S(1)} collective-permute-done((bf16[256,512]{1,0:T(8,128)(2,1)S(1)}, bf16[256,512]{1,0:T(8,128)(2,1)S(1)}, u32[]{:S(2)}, u32[]{:S(2)}) %collective-permute-start.4) | collective-permute-done | bytes 262176 | tf_op jit(solution)/shard_map/ppermute | solution.py:415
  60.8 4.2 %all-to-all-start.3 = ((bf16[4,256,512]{2,1,0:T(8,128)(2,1)}), bf16[4,256,512]{2,1,0:T(8,128)(2,1)S(1)}, u32[]{:S(2)}, u32[]{:S(2)}) async-start(bf16[4,256,512]{2,1,0:T(8,128)(2,1)} %broadcast_in_dim.25), calls=%async_computation.3 | async-start | bytes 2097152 | tf_op jit(solution)/shard_map/all_to_all | solution.py:408
  68.4 7.4 %shard_map.173 = (f32[512,512]{1,0:T(8,128)}, bf16[512,512]{1,0:T(8,128)(2,1)}, bf16[512,512]{1,0:T(8,128)(2,1)}, f32[8,1024]{1,0:T(8,128)S(1)}, bf16[8,1024]{1,...) custom-call(s32[2]{0:T(128)S(1)} %pad_add_fusion.at_ref, s32[4]{0:T(128)S(1)} %bitcast.51, ...), custom_call_target="tpu_custom_call" | custom-call | flops 1100000000 | bytes 7569408 | tf_op jit(solution)/shard_map/pallas_call | solution.py:46
  75.8 4.2 %all-to-all-done.3 = bf16[4,256,512]{2,1,0:T(8,128)(2,1)S(1)} async-done(((bf16[4,256,512]{2,1,0:T(8,128)(2,1)}), bf16[4,256,512]{2,1,0:T(8,128)(2,1)S(1)}, u32[]{:S(2)}, u32[]{:S(2)}) %all-to-all-start.3) | async-done | bytes 1048608 | tf_op jit(solution)/shard_map/all_to_all | solution.py:408
  88.8 7.1 %all-to-all-start.4 = ((f32[256,1,128]{2,1,0:T(1,128)}), f32[256,1,128]{2,1,0:T(1,128)S(1)}, u32[]{:S(2)}, u32[]{:S(2)}) async-start(f32[256,1,128]{2,1,0:T(1,128)} %broadcast_in_dim.56), calls=%async_computation.4 | async-start | bytes 262144 | tf_op jit(solution)/shard_map/all_to_all | solution.py:408
  100.6 5.5 %shard_map.175 = (f32[512,512]{1,0:T(8,128)}, f32[512,512]{1,0:T(8,128)}, f32[8,1024]{1,0:T(8,128)S(1)}, f32[8,1024]{1,0:T(8,128)S(1)}) custom-call(s32[4]{0:T(128)S(1)} %bitcast.52, bf16[512,512]{1,0:T(8,128)(2,1)S(1)} %copy-done.6, bf16[512,512]{1,0:T(8,128)(2,1)S(1)} %copy-done.7, f32[512,512]{1,0:T(8,128)} %get-tuple-element.91.kproj_ref, ...), custom_call_target="tpu_custom_call" | custom-call | flops 200000000 | bytes 6598656 | tf_op jit(solution)/shard_map/pallas_call | solution.py:46
  108.8 5.5 %shard_map.176 = (bf16[4,256,768]{2,1,0:T(8,128)(2,1)}, bf16[4,256,768]{2,1,0:T(8,128)(2,1)}, f32[1,1]{1,0:T(1,128)}, bf16[512,512]{1,0:T(8,128)(2,1)S(1)}, bf16...) custom-call(s32[2]{0:T(128)S(1)} %pad_add_fusion.at_ref, ...), custom_call_target="tpu_custom_call" | custom-call | flops 600000000 | bytes 7692292 | tf_op jit(solution)/shard_map/pallas_call | solution.py:46
  115.8 3.2 %collective-permute-done.13.add_a = bf16[4,256,768]{2,1,0:T(8,128)(2,1)S(1)} collective-permute-done((bf16[4,256,768]{2,1,0:T(8,128)(2,1)}, bf16[4,256,768]{2,1,0:T(8,128)(2,1)S(1)}, u32[]{:S(2)}, u32[]{:S(2)}) %collective-permute-start.13) | collective-permute-done | bytes 1572896 | tf_op jit(solution)/shard_map/ppermute | solution.py:434
  122.5 5.2 %shard_map.177 = (bf16[4,256,768]{2,1,0:T(8,128)(2,1)}, bf16[256,768]{1,0:T(8,128)(2,1)S(1)}, bf16[256,768]{1,0:T(8,128)(2,1)S(1)}, bf16[256,768]{1,0:T(8,128)(2,1)S(1)}, bf16[256,768]{1,0:T(8,128)(2,1)S(1)}) custom-call(s32[2]{0:T(128)S(1)} %pad_add_fusion.at_ref, bf16[512,512]{1,0:T(8,128)(2,1)} %copy-done.1, ...), custom_call_target="tpu_custom_call" | custom-call | flops 600000000 | bytes 7946240 | tf_op jit(solution)/shard_map/pallas_call | solution.py:46
  129.2 4.5 %all-to-all-start.5 = ((bf16[4,256,768]{2,1,0:T(8,128)(2,1)}), bf16[4,256,768]{2,1,0:T(8,128)(2,1)}, u32[]{:S(2)}, u32[]{:S(2)}) async-start(bf16[4,256,768]{2,1,0:T(8,128)(2,1)} %get-tuple-element.109), calls=%async_computation.5 | async-start | bytes 3145728 | tf_op jit(solution)/shard_map/all_to_all | solution.py:574
  140.0 6.6 %shard_map.179 = bf16[512,1024]{1,0:T(8,128)(2,1)} custom-call(s32[4]{0:T(128)S(1)} %bitcast.53, bf16[512,1024]{1,0:T(8,128)(2,1)} %bitcast.55, f32[1,1024]{1,0:T(1,128)S(1)} %bitcast.45, bf16[512,512]{1,0:T(8,128)(2,1)S(1)} %copy-done.2, bf16[512,512]{1,0:T(8,128)(2,1)S(1)} %get-tuple-element.114.skvb_ref, f32[8,1024]{1,0:T(8,128)S(1)} %reshape.94.last_ref, ...), custom_call_target="tpu_custom_call" | custom-call | flops 1100000000 | bytes 5312512 | tf_op jit(solution)/shard_map/pallas_call | solution.py:46
  146.6 7.2 %collective-permute-done.16.refs_2_ = bf16[256,768]{1,0:T(8,128)(2,1)} collective-permute-done((bf16[256,768]{1,0:T(8,128)(2,1)}, bf16[256,768]{1,0:T(8,128)(2,1)}, u32[]{:S(2)}, u32[]{:S(2)}) %collective-permute-start.16) | collective-permute-done | bytes 393248 | tf_op jit(solution)/shard_map/ppermute | solution.py:421
  154.4 3.0 %shard_map.180 = (bf16[64,768]{1,0:T(8,128)(2,1)S(1)}, bf16[64,768]{1,0:T(8,128)(2,1)S(1)}, bf16[64,768]{1,0:T(8,128)(2,1)S(1)}, bf16[64,768]{1,0:T(8,128)(2,1)S(1)}, bf16[256,768]{1,0:T(8,128)(2,1)}) custom-call(s32[2]{0:T(128)S(1)} %pad_add_fusion.at_ref, bf16[4,256,768]{2,1,0:T(8,128)(2,1)} %all-to-all-done.5.got_a_ref, ...), custom_call_target="tpu_custom_call" | custom-call | bytes 3932160 | tf_op jit(solution)/shard_map/pallas_call | solution.py:46
  159.0 2.9 %collective-permute-start.19 = (bf16[64,768]{1,0:T(8,128)(2,1)S(1)}, bf16[64,768]{1,0:T(8,128)(2,1)S(1)}, u32[]{:S(2)}, u32[]{:S(2)}) collective-permute-start(bf16[64,768]{1,0:T(8,128)(2,1)S(1)} %get-tuple-element.124), channel_id=1, source_target_pairs={{0,4},{2,6},{4,0},{6,2},{1,5},{3,7},{5,1},{7,3},{8,12},{10,14},{12... | collective-permute-start | bytes 294920 | tf_op jit(solution)/shard_map/ppermute | solution.py:421
  161.9 4.1 %all-to-all-start.6 = ((bf16[4,64,768]{2,1,0:T(8,128)(2,1)}), bf16[4,64,768]{2,1,0:T(8,128)(2,1)S(1)}, u32[]{:S(2)}, u32[]{:S(2)}) async-start(bf16[4,64,768]{2,1,0:T(8,128)(2,1)} %bitcast.21), calls=%async_computation.6 | async-start | bytes 786432 | tf_op jit(solution)/shard_map/all_to_all | solution.py:593
  166.5 6.0 %all-to-all-done.6 = bf16[4,64,768]{2,1,0:T(8,128)(2,1)S(1)} async-done(((bf16[4,64,768]{2,1,0:T(8,128)(2,1)}), bf16[4,64,768]{2,1,0:T(8,128)(2,1)S(1)}, u32[]{:S(2)}, u32[]{:S(2)}) %all-to-all-start.6) | async-done | bytes 393248 | tf_op jit(solution)/shard_map/all_to_all | solution.py:593
  172.6 13.8 %all_to_all.40 = bf16[8,8,1536]{2,1,0:T(8,128)(2,1)S(1)} all-to-all(bf16[8,8,1536]{2,1,0:T(8,128)(2,1)S(1)} %maximum_bitcast_fusion), channel_id=1, replica_groups=mesh['pb'=4,'z'=8,'x'=4,'c'=2] {'z'}, dimensions={0} | all-to-all | bytes 393216 | tf_op jit(solution)/shard_map/all_to_all | solution.py:602
  186.5 5.5 %collective-permute-start.21 = (f32[4,1536]{1,0:T(4,128)S(1)}, f32[4,1536]{1,0:T(4,128)S(1)}, u32[]{:S(2)}, u32[]{:S(2)}) collective-permute-start(f32[4,1536]{1,0:T(4,128)S(1)} %slice_select_fusion), channel_id=1, source_target_pairs={{0,1},{1,0},{2,3},{3,2},{4,5},{5,4},{6,7},{7,6},{8,9},{9,8},{10,11... | collective-permute-start | bytes 73736 | tf_op jit(solution)/shard_map/ppermute | solution.py:434
  (159 shorter events, 66.5 us)
Async XLA Ops:
  2.1 4.2 %collective-permute-start = (bf16[4,1536]{1,0:T(4,128)(2,1)S(1)}, bf16[4,1536]{1,0:T(4,128)(2,1)S(1)}, u32[]{:S(2)}, u32[]{:S(2)}) collective-permute-start(bf16[4,1536]{1,0:T(4,128)(2,1)S(1)} %broadcast_select_fusion.4), channel_id=1, source_target_pairs={{0,1},{1,0},{2,3},{3,2},{4,5},{5,4},{6,7},{7,6},{8,9},{9,8},{10,11... | collective-permute-start | bytes 36872 | tf_op jit(solution)/shard_map/ppermute | solution.py:434
  7.1 15.9 %all-to-all-start = ((bf16[8,8,1536]{2,1,0:T(8,128)(2,1)}), bf16[8,8,1536]{2,1,0:T(8,128)(2,1)S(1)}, u32[]{:S(2)}, u32[]{:S(2)}) async-start(bf16[8,8,1536]{2,1,0:T(8,128)(2,1)} %broadcast_in_dim.21), calls=%async_computation | async-start | bytes 393216 | tf_op jit(solution)/shard_map/all_to_all | solution.py:408
  23.7 14.1 %all-to-all-start.1 = ((bf16[4,64,512]{2,1,0:T(8,128)(2,1)}), bf16[4,64,512]{2,1,0:T(8,128)(2,1)S(1)}, u32[]{:S(2)}, u32[]{:S(2)}) async-start(bf16[4,64,512]{2,1,0:T(8,128)(2,1)} %broadcast_in_dim.23), calls=%async_computation.1 | async-start | bytes 524288 | tf_op jit(solution)/shard_map/all_to_all | solution.py:408
  27.9 5.4 %collective-permute-start.3 = (bf16[64,1024]{1,0:T(8,128)(2,1)S(1)}, bf16[64,1024]{1,0:T(8,128)(2,1)S(1)}, u32[]{:S(2)}, u32[]{:S(2)}) collective-permute-start(bf16[64,1024]{1,0:T(8,128)(2,1)S(1)} %slice.110.refs_0_), channel_id=1, source_target_pairs={{0,6},{2,0},{4,2},{6,4},{1,7},{3,1},{5,3},{7,5},{8,14},{10,8},{12,... | collective-permute-start | bytes 393224 | tf_op jit(solution)/shard_map/ppermute | solution.py:415
  30.5 5.6 %collective-permute-start.2 = (bf16[64,1024]{1,0:T(8,128)(2,1)S(1)}, bf16[64,1024]{1,0:T(8,128)(2,1)S(1)}, u32[]{:S(2)}, u32[]{:S(2)}) collective-permute-start(bf16[64,1024]{1,0:T(8,128)(2,1)S(1)} %slice.110.refs_0_), channel_id=1, source_target_pairs={{0,4},{2,6},{4,0},{6,2},{1,5},{3,7},{5,1},{7,3},{8,12},{10,14},{12... | collective-permute-start | bytes 393224 | tf_op jit(solution)/shard_map/ppermute | solution.py:415
  31.0 6.2 %collective-permute-start.1 = (bf16[64,1024]{1,0:T(8,128)(2,1)S(1)}, bf16[64,1024]{1,0:T(8,128)(2,1)S(1)}, u32[]{:S(2)}, u32[]{:S(2)}) collective-permute-start(bf16[64,1024]{1,0:T(8,128)(2,1)S(1)} %slice.110.refs_0_), channel_id=1, source_target_pairs={{0,2},{2,4},{4,6},{6,0},{1,3},{3,5},{5,7},{7,1},{8,10},{10,12},{12... | collective-permute-start | bytes 393224 | tf_op jit(solution)/shard_map/ppermute | solution.py:415
  38.9 18.3 %all-to-all-start.2 = ((bf16[4,256,512]{2,1,0:T(8,128)(2,1)}), bf16[4,256,512]{2,1,0:T(8,128)(2,1)}, u32[]{:S(2)}, u32[]{:S(2)}) async-start(bf16[4,256,512]{2,1,0:T(8,128)(2,1)} %broadcast_in_dim.24), calls=%async_computation.2 | async-start | bytes 2097152 | tf_op jit(solution)/shard_map/all_to_all | solution.py:408
  43.1 5.3 %collective-permute-start.6 = (bf16[256,512]{1,0:T(8,128)(2,1)S(1)}, bf16[256,512]{1,0:T(8,128)(2,1)S(1)}, u32[]{:S(2)}, u32[]{:S(2)}) collective-permute-start(bf16[256,512]{1,0:T(8,128)(2,1)S(1)} %bitcast.36), channel_id=1, source_target_pairs={{0,6},{2,0},{4,2},{6,4},{1,7},{3,1},{5,3},{7,5},{8,14},{10,8},{12,... | collective-permute-start | bytes 786440 | tf_op jit(solution)/shard_map/ppermute | solution.py:415
  43.8 6.8 %collective-permute-start.5 = (bf16[256,512]{1,0:T(8,128)(2,1)S(1)}, bf16[256,512]{1,0:T(8,128)(2,1)S(1)}, u32[]{:S(2)}, u32[]{:S(2)}) collective-permute-start(bf16[256,512]{1,0:T(8,128)(2,1)S(1)} %bitcast.37), channel_id=1, source_target_pairs={{0,4},{2,6},{4,0},{6,2},{1,5},{3,7},{5,1},{7,3},{8,12},{10,14},{12... | collective-permute-start | bytes 786440 | tf_op jit(solution)/shard_map/ppermute | solution.py:415
  44.3 12.8 %collective-permute-start.4 = (bf16[256,512]{1,0:T(8,128)(2,1)S(1)}, bf16[256,512]{1,0:T(8,128)(2,1)S(1)}, u32[]{:S(2)}, u32[]{:S(2)}) collective-permute-start(bf16[256,512]{1,0:T(8,128)(2,1)S(1)} %bitcast.38), channel_id=1, source_target_pairs={{0,2},{2,4},{4,6},{6,0},{1,3},{3,5},{5,7},{7,1},{8,10},{10,12},{12... | collective-permute-start | bytes 786440 | tf_op jit(solution)/shard_map/ppermute | solution.py:415
  57.2 10.5 %collective-permute-start.7 = (bf16[1024,512]{1,0:T(8,128)(2,1)}, bf16[1024,512]{1,0:T(8,128)(2,1)}, u32[]{:S(2)}, u32[]{:S(2)}) collective-permute-start(bf16[1024,512]{1,0:T(8,128)(2,1)} %bitcast.11.refs_0_.kva_ref), channel_id=1, source_target_pairs={{0,1},{1,0},{2,3},{3,2},{4,5},{5,4},{6,7},{7,6},{8,9},{9,8},{10,11... | collective-permute-start | bytes 3145736 | tf_op jit(solution)/shard_map/ppermute | solution.py:434
  60.8 19.2 %all-to-all-start.3 = ((bf16[4,256,512]{2,1,0:T(8,128)(2,1)}), bf16[4,256,512]{2,1,0:T(8,128)(2,1)S(1)}, u32[]{:S(2)}, u32[]{:S(2)}) async-start(bf16[4,256,512]{2,1,0:T(8,128)(2,1)} %broadcast_in_dim.25), calls=%async_computation.3 | async-start | bytes 2097152 | tf_op jit(solution)/shard_map/all_to_all | solution.py:408
  88.8 19.9 %all-to-all-start.4 = ((f32[256,1,128]{2,1,0:T(1,128)}), f32[256,1,128]{2,1,0:T(1,128)S(1)}, u32[]{:S(2)}, u32[]{:S(2)}) async-start(f32[256,1,128]{2,1,0:T(1,128)} %broadcast_in_dim.56), calls=%async_computation.4 | async-start | bytes 262144 | tf_op jit(solution)/shard_map/all_to_all | solution.py:408
  115.1 3.9 %collective-permute-start.13 = (bf16[4,256,768]{2,1,0:T(8,128)(2,1)}, bf16[4,256,768]{2,1,0:T(8,128)(2,1)S(1)}, u32[]{:S(2)}, u32[]{:S(2)}) collective-permute-start(bf16[4,256,768]{2,1,0:T(8,128)(2,1)} %get-tuple-element.107), channel_id=1, source_target_pairs={{0,1},{1,0},{2,3},{3,2},{4,5},{5,4},{6,7},{7,6},{8,9},{9,8},{10,11... | collective-permute-start | bytes 4718600 | tf_op jit(solution)/shard_map/ppermute | solution.py:434
  115.8 5.5 %collective-permute-start.14 = (bf16[4,256,768]{2,1,0:T(8,128)(2,1)}, bf16[4,256,768]{2,1,0:T(8,128)(2,1)S(1)}, u32[]{:S(2)}, u32[]{:S(2)}) collective-permute-start(bf16[4,256,768]{2,1,0:T(8,128)(2,1)} %get-tuple-element.108), channel_id=1, source_target_pairs={{0,1},{1,0},{2,3},{3,2},{4,5},{5,4},{6,7},{7,6},{8,9},{9,8},{10,11... | collective-permute-start | bytes 4718600 | tf_op jit(solution)/shard_map/ppermute | solution.py:434
  129.2 25.2 %all-to-all-start.5 = ((bf16[4,256,768]{2,1,0:T(8,128)(2,1)}), bf16[4,256,768]{2,1,0:T(8,128)(2,1)}, u32[]{:S(2)}, u32[]{:S(2)}) async-start(bf16[4,256,768]{2,1,0:T(8,128)(2,1)} %get-tuple-element.109), calls=%async_computation.5 | async-start | bytes 3145728 | tf_op jit(solution)/shard_map/all_to_all | solution.py:574
  133.7 12.9 %collective-permute-start.15 = (bf16[256,768]{1,0:T(8,128)(2,1)}, bf16[256,768]{1,0:T(8,128)(2,1)S(1)}, u32[]{:S(2)}, u32[]{:S(2)}) collective-permute-start(bf16[256,768]{1,0:T(8,128)(2,1)} %copy-done.30), channel_id=1, source_target_pairs={{0,2},{2,4},{4,6},{6,0},{1,3},{3,5},{5,7},{7,1},{8,10},{10,12},{12... | collective-permute-start | bytes 1179656 | tf_op jit(solution)/shard_map/ppermute | solution.py:421
  134.0 19.7 %collective-permute-start.16 = (bf16[256,768]{1,0:T(8,128)(2,1)}, bf16[256,768]{1,0:T(8,128)(2,1)}, u32[]{:S(2)}, u32[]{:S(2)}) collective-permute-start(bf16[256,768]{1,0:T(8,128)(2,1)} %copy-done.29), channel_id=1, source_target_pairs={{0,4},{2,6},{4,0},{6,2},{1,5},{3,7},{5,1},{7,3},{8,12},{10,14},{12... | collective-permute-start | bytes 1179656 | tf_op jit(solution)/shard_map/ppermute | solution.py:421
  136.1 18.3 %collective-permute-start.17 = (bf16[256,768]{1,0:T(8,128)(2,1)}, bf16[256,768]{1,0:T(8,128)(2,1)}, u32[]{:S(2)}, u32[]{:S(2)}) collective-permute-start(bf16[256,768]{1,0:T(8,128)(2,1)} %copy-done.28), channel_id=1, source_target_pairs={{0,6},{2,0},{4,2},{6,4},{1,7},{3,1},{5,3},{7,5},{8,14},{10,8},{12,... | collective-permute-start | bytes 1179656 | tf_op jit(solution)/shard_map/ppermute | solution.py:421
  157.4 8.7 %collective-permute-start.18 = (bf16[64,768]{1,0:T(8,128)(2,1)S(1)}, bf16[64,768]{1,0:T(8,128)(2,1)S(1)}, u32[]{:S(2)}, u32[]{:S(2)}) collective-permute-start(bf16[64,768]{1,0:T(8,128)(2,1)S(1)} %get-tuple-element.123), channel_id=1, source_target_pairs={{0,2},{2,4},{4,6},{6,0},{1,3},{3,5},{5,7},{7,1},{8,10},{10,12},{12... | collective-permute-start | bytes 294920 | tf_op jit(solution)/shard_map/ppermute | solution.py:421
  159.0 7.5 %collective-permute-start.19 = (bf16[64,768]{1,0:T(8,128)(2,1)S(1)}, bf16[64,768]{1,0:T(8,128)(2,1)S(1)}, u32[]{:S(2)}, u32[]{:S(2)}) collective-permute-start(bf16[64,768]{1,0:T(8,128)(2,1)S(1)} %get-tuple-element.124), channel_id=1, source_target_pairs={{0,4},{2,6},{4,0},{6,2},{1,5},{3,7},{5,1},{7,3},{8,12},{10,14},{12... | collective-permute-start | bytes 294920 | tf_op jit(solution)/shard_map/ppermute | solution.py:421
  161.9 4.5 %collective-permute-start.20 = (bf16[64,768]{1,0:T(8,128)(2,1)S(1)}, bf16[64,768]{1,0:T(8,128)(2,1)S(1)}, u32[]{:S(2)}, u32[]{:S(2)}) collective-permute-start(bf16[64,768]{1,0:T(8,128)(2,1)S(1)} %get-tuple-element.125), channel_id=1, source_target_pairs={{0,6},{2,0},{4,2},{6,4},{1,7},{3,1},{5,3},{7,5},{8,14},{10,8},{12,... | collective-permute-start | bytes 294920 | tf_op jit(solution)/shard_map/ppermute | solution.py:421
  161.9 10.5 %all-to-all-start.6 = ((bf16[4,64,768]{2,1,0:T(8,128)(2,1)}), bf16[4,64,768]{2,1,0:T(8,128)(2,1)S(1)}, u32[]{:S(2)}, u32[]{:S(2)}) async-start(bf16[4,64,768]{2,1,0:T(8,128)(2,1)} %bitcast.21), calls=%async_computation.6 | async-start | bytes 786432 | tf_op jit(solution)/shard_map/all_to_all | solution.py:593
  186.5 6.4 %collective-permute-start.21 = (f32[4,1536]{1,0:T(4,128)S(1)}, f32[4,1536]{1,0:T(4,128)S(1)}, u32[]{:S(2)}, u32[]{:S(2)}) collective-permute-start(f32[4,1536]{1,0:T(4,128)S(1)} %slice_select_fusion), channel_id=1, source_target_pairs={{0,1},{1,0},{2,3},{3,2},{4,5},{5,4},{6,7},{7,6},{8,9},{9,8},{10,11... | collective-permute-start | bytes 73736 | tf_op jit(solution)/shard_map/ppermute | solution.py:434
  (40 other events, 194.8 us)
where the time goes:
time: 197 us; the launch traced here: 195 us
  starting transfers between devices  62.4 us (32%)
  waiting for transfers between devices  51.8 us (26%)
  Pallas kernels  40.9 us (21%)
  local copies, waits for them, and re-layouts  22.6 us (11%)
  blocking collectives  13.8 us (7%)
  other arithmetic  2.74 us (1%)
    pallas_call x10, Pallas kernels, call(): pl.pallas_call(body, grid=(1,), out_shape=[jax.ShapeDtypeStruct(o, d) for...  40.9 us
    all_to_all x5, starting transfers between devices, everyone(): lax.all_to_all(jnp.broadcast_to(x[None], (count, *x.shape)), axes, 0, 0,...  26.2 us
    ppermute x6, waiting for transfers between devices, from_ring(): lax.ppermute(x, axis, [(i, (i + d) % 4) for i in range(4)])  17.8 us
    ppermute x10, starting transfers between devices, swap(): return lax.ppermute(x, 'c', [(0, 1), (1, 0)])  14.2 us
    all_to_all x1, blocking collectives, shards(): rec = lax.all_to_all(part.reshape(8, 8, 1536), 'z', 0, 0, tiled=True)  13.8 us
    unnamed x70, local copies, waits for them, and re-layouts  13.3 us
    ppermute x10, waiting for transfers between devices, swap(): return lax.ppermute(x, 'c', [(0, 1), (1, 0)])  10.4 us
    all_to_all x5, waiting for transfers between devices, everyone(): lax.all_to_all(jnp.broadcast_to(x[None], (count, *x.shape)), axes, 0, 0,...  9.43 us
  transfers between devices with their start and end apart: 29, of which 22 were waited for; matrix products, arithmetic and copies ran while one was open for 2% of the time, Pallas kernels for 13%

commit v1 on v0

v1 whole, which is shorter than its diff:
```python
import jax
import jax.numpy as jnp
import numpy as np
from jax import lax
from jax.experimental import pallas as pl
from jax.experimental.pallas import tpu as pltpu
from jax.sharding import Mesh
from jax.sharding import PartitionSpec as P

HW = 128
AXES = ("pb", "z", "x", "c")
NEG = ("z", "x", "c")
EPS = 1e-06
ROPE_BASE = 1000000.0
GRAD_SCALE = 512.0
PAIRS = 4
SEQ = 128
D = 1024
ROWS = PAIRS * SEQ
BOTH = 2 * PAIRS
F32 = jnp.float32
BF16 = jnp.bfloat16
SM = pl.BlockSpec(memory_space=pltpu.SMEM)
LAST = (((1,), (1,)), ((), ()))
FIRST = (((0,), (0,)), ((), ()))
SCALE = HW ** (-0.5)


def rope_consts():
    freqs = np.float32(ROPE_BASE) ** (-(np.arange(HW // 2, dtype=np.float32) * 2.0) / HW)
    angles = np.arange(SEQ, dtype=np.float32)[:, None] * freqs.astype(np.float32)[None, :]
    angles = np.concatenate([angles, angles], axis=1)
    sign = np.where(np.arange(HW) < HW // 2, -1.0, 1.0)
    return (
        np.cos(angles).astype(np.float32),
        (np.sin(angles) * sign[None, :]).astype(np.float32),
    )


def whole(shape):
    return pl.BlockSpec(shape, lambda i: (0,) * len(shape), pipeline_mode=pl.Buffered(1))


def call(body, scalars, arrays, outs, scratch=(), flops=0, grant=52, light=False):
    moved = sum(a.size * a.dtype.itemsize for a in arrays)
    moved += sum(int(np.prod(o)) * np.dtype(d).itemsize for o, d in outs)
    if light:
        moved = flops = 1024
    return pl.pallas_call(
        body,
        grid=(1,),
        out_shape=[jax.ShapeDtypeStruct(o, d) for o, d in outs],
        in_specs=[SM] * len(scalars) + [whole(a.shape) for a in arrays],
        out_specs=[whole(o) for o, _ in outs],
        scratch_shapes=[pltpu.VMEM(o, d) for o, d in scratch],
        compiler_params=pltpu.CompilerParams(vmem_limit_bytes=grant << 20),
        cost_estimate=pl.CostEstimate(flops=flops, bytes_accessed=moved, transcendentals=0),
    )(*scalars, *arrays)


def block_at(me, step, width):
    return pl.ds(pl.multiple_of(lax.rem(me + step + 4, 4) * width, width), width)


def dot(a, b, dims=(((1,), (0,)), ((), ()))):
    return lax.dot_general(a, b, dims, preferred_element_type=F32)


def half_turn(v):
    return pltpu.roll(v, HW // 2, 1)


def heads(v, n):
    return [v[:, i * HW : (i + 1) * HW] for i in range(n)]


def block_mask():
    row = lax.broadcasted_iota(jnp.int32, (8, 256), 0)
    lane = lax.broadcasted_iota(jnp.int32, (8, 256), 1)
    return (lane // HW) == (row // 2), (row % 2) == 0


def to_blocks(row, mask, even):
    h = heads(row, 4)
    e = jnp.broadcast_to(jnp.concatenate(h[0::2], axis=1), (8, 256))
    o = jnp.broadcast_to(jnp.concatenate(h[1::2], axis=1), (8, 256))
    return jnp.where(mask, jnp.where(even, e, o), 0.0)


def from_blocks(blocks, mask, even):
    e = jnp.sum(jnp.where(mask & even, blocks, 0.0), axis=0, keepdims=True)
    o = jnp.sum(jnp.where(mask & (~even), blocks, 0.0), axis=0, keepdims=True)
    return jnp.concatenate([e[:, 0:HW], o[:, 0:HW], e[:, HW:], o[:, HW:]], axis=1)


def query_tables(len_ref, cos_ref, sin_ref):
    return [
        jnp.concatenate([t[pl.ds(len_ref[p] - 1, 1), :] for p in range(BOTH)], axis=0)
        for t in (cos_ref, sin_ref)
    ]


def prep_body(len_ref, h_ref, gain_ref, normed_ref, turned_ref, nlast_ref, xlast_ref):
    row = lax.broadcasted_iota(jnp.int32, (8, SEQ), 0)
    lane = lax.broadcasted_iota(jnp.int32, (8, SEQ), 1)
    nl = jnp.zeros((8, D), F32)
    xl = jnp.zeros((8, D), F32)
    for p in range(PAIRS):
        raw = h_ref[p * SEQ : (p + 1) * SEQ, :]
        x = raw.astype(F32)
        inv = lax.rsqrt(jnp.mean(x * x, axis=-1, keepdims=True) + EPS)
        n = (x * inv * gain_ref[...]).astype(BF16)
        normed_ref[p * SEQ : (p + 1) * SEQ, :] = n
        turned_ref[:, p * SEQ : (p + 1) * SEQ] = n.T
        e = len_ref[p] - 1
        hot = jnp.where((row == p) & (lane == e), 1.0, 0.0).astype(BF16)
        nl = nl + dot(hot, n)
        xl = xl + dot(hot, raw)
    nlast_ref[...] = nl.astype(BF16)
    xlast_ref[...] = xl


def arrange_body(at_ref, *refs):
    a_refs, out_ref = refs[0:4], refs[4]
    x = at_ref[1]
    for d in range(4):
        out_ref[:, pl.ds(lax.rem(x - d + 4, 4), 1)] = a_refs[d][...].reshape(8, 1, 8, 1024)


def attend_body(
    at_ref, len_ref, normed_ref, other_ref, nlast_ref, cos_ref, sin_ref, kv_ref, *refs
):
    q_refs = refs[0:4]
    kproj_ref, krot_ref, vcast_ref, qproj_ref, qrot_ref, attn_ref, ctx_ref, qr_scr, ctx_scr = refs[4:]
    x = at_ref[1]
    mask, even = block_mask()
    lane = lax.broadcasted_iota(jnp.int32, (8, SEQ), 1)
    for side, rows_ref in enumerate((normed_ref, other_ref)):

        @pl.loop(0, 2)
        def _(i):
            src = pl.ds(pl.multiple_of(i * 256, 256), 256)
            dst = pl.ds(pl.multiple_of(side * ROWS + i * 256, 256), 256)
            kv = dot(rows_ref[src, :], kv_ref[...])
            kproj_ref[dst, :] = kv[:, 0:256]
            vcast_ref[dst, :] = kv[:, 256:512].astype(BF16)

    q = jnp.zeros((8, 512), F32)
    for d in range(4):
        q = q + dot(nlast_ref[:, block_at(x, -d, 256)], q_refs[d][...])
    qproj_ref[...] = q
    cos_q, sin_q = query_tables(len_ref, cos_ref, sin_ref)
    for h in range(4):
        q = qproj_ref[:, h * HW : (h + 1) * HW]
        u = q * lax.rsqrt(jnp.mean(q * q, axis=-1, keepdims=True) + EPS)
        r = u * cos_q + half_turn(u) * sin_q
        qr_scr[:, h * HW : (h + 1) * HW] = r
        qrot_ref[:, h * HW : (h + 1) * HW] = r.astype(BF16)
    for p in range(BOTH):
        rows = slice(p * SEQ, (p + 1) * SEQ)
        for g in range(2):
            k = kproj_ref[rows, g * HW : (g + 1) * HW]
            u = k * lax.rsqrt(jnp.mean(k * k, axis=-1, keepdims=True) + EPS)
            r = u * cos_ref[...] + half_turn(u) * sin_ref[...]
            krot_ref[rows, g * HW : (g + 1) * HW] = r.astype(BF16)
        qb = to_blocks(qr_scr[p : p + 1, :], mask, even).astype(BF16)
        logits = dot(qb, krot_ref[rows, :], LAST) * SCALE
        ex = jnp.where(lane <= len_ref[p] - 1, jnp.exp(logits), 0.0)
        w = ex / jnp.sum(ex, axis=-1, keepdims=True)
        attn_ref[p * 8 : (p + 1) * 8, :] = w
        c = dot(w.astype(BF16), vcast_ref[rows, :])
        ctx_scr[p : p + 1, :] = from_blocks(c, mask, even)
    ctx_ref[...] = ctx_scr[...].astype(BF16)


def attended_body(at_ref, ctx_ref, *refs):
    o_refs, out_ref = refs[0:4], refs[4]
    for d in range(4):
        out_ref[:, block_at(at_ref[0], -d, 256)] = dot(ctx_ref[...], o_refs[d][...], LAST)


def score_body(teach_ref, mine_ref, theirs_ref, xlast_ref, fg_ref, sv_ref, *refs):
    unit_ref, oscale_ref, score_ref, tot_ref, line_ref = refs
    res = xlast_ref[...] + (mine_ref[...] + pltpu.roll(theirs_ref[...], PAIRS, 0))
    sc = lax.rsqrt(jnp.mean(res * res, axis=-1, keepdims=True) + EPS)
    unit = res * sc
    unit_ref[...] = unit
    oscale_ref[...] = jnp.broadcast_to(sc, (8, HW))
    s = jnp.sum(unit * fg_ref[...] * sv_ref[...], axis=-1, keepdims=True)
    s = jnp.broadcast_to(s, (8, HW))
    score_ref[...] = s
    row = lax.broadcasted_iota(jnp.int32, (8, HW), 0)
    lane = lax.broadcasted_iota(jnp.int32, (8, HW), 1)
    line_ref[...] = jnp.sum(jnp.where(row == lane, s, 0.0), axis=0, keepdims=True)[:, 0:PAIRS]
    scaled = teach_ref[...] / 2.0
    es = jnp.exp(s)
    et = jnp.exp(scaled)
    v = jnp.where(lane == 0, es, jnp.where(lane == 1, et, et * (scaled - s)))
    v = jnp.where((row < PAIRS) & (lane < 3), v, 0.0)
    tot_ref[...] = jnp.broadcast_to(jnp.sum(v, axis=0, keepdims=True), (8, HW))


def unit_back_body(
    at_ref,
    len_ref,
    krot_ref,
    vcast_ref,
    kproj_ref,
    qproj_ref,
    qrot_ref,
    attn_ref,
    unit_ref,
    oscale_ref,
    fg_ref,
    sv_ref,
    cos_ref,
    sin_ref,
    *refs,
):
    o_refs, q_refs, kv_ref = refs[0:4], refs[4:8], refs[8]
    gkv_ref, gq_ref, gr_ref, last_ref, send_ref, gc_scr, gq_scr, qr_scr, gr_scr = refs[9:]
    mask, even = block_mask()
    unit = unit_ref[...]
    gu = sv_ref[...] * fg_ref[...]
    gr = oscale_ref[:, 0:1] * (gu - unit * jnp.mean(gu * unit, axis=-1, keepdims=True))
    gr_ref[...] = gr
    gr_scr[...] = gr.astype(BF16)
    gc = jnp.zeros((8, 512), F32)
    for d in range(4):
        gc = gc + dot(gr_scr[:, block_at(at_ref[0], -d, 256)], o_refs[d][...])
    gc_scr[...] = gc
    qr_scr[...] = qrot_ref[...].astype(F32)
    for p in range(BOTH):
        rows = slice(p * SEQ, (p + 1) * SEQ)
        gb = to_blocks(gc_scr[p : p + 1, :], mask, even).astype(BF16)
        qb = to_blocks(qr_scr[p : p + 1, :], mask, even).astype(BF16)
        w = attn_ref[p * 8 : (p + 1) * 8, :]
        gp = dot(gb, vcast_ref[rows, :], LAST)
        gkv_ref[rows, 256:512] = dot(w.astype(BF16), gb, FIRST)
        spread = jnp.sum(w * gp, axis=-1, keepdims=True)
        dl = (w * (gp - spread)).astype(BF16)
        gq_scr[p : p + 1, :] = from_blocks(dot(dl, krot_ref[rows, :]) * SCALE, mask, even)
        gk = dot(dl, qb, FIRST) * SCALE
        for g in range(2):
            cols = slice(g * HW, (g + 1) * HW)
            k = kproj_ref[rows, cols]
            sc = lax.rsqrt(jnp.mean(k * k, axis=-1, keepdims=True) + EPS)
            u = k * sc
            r = gk[:, cols]
            t = r * cos_ref[...] + half_turn(r * sin_ref[...])
            gkv_ref[rows, cols] = sc * (t - u * jnp.mean(t * u, axis=-1, keepdims=True))
    cos_q, sin_q = query_tables(len_ref, cos_ref, sin_ref)
    for h in range(4):
        q = qproj_ref[:, h * HW : (h + 1) * HW]
        sc = lax.rsqrt(jnp.mean(q * q, axis=-1, keepdims=True) + EPS)
        u = q * sc
        r = gq_scr[:, h * HW : (h + 1) * HW]
        t = r * cos_q + half_turn(r * sin_q)
        gq_ref[:, h * HW : (h + 1) * HW] = sc * (
            t - u * jnp.mean(t * u, axis=-1, keepdims=True)
        )
    gqb = gq_ref[...].astype(BF16)
    for d in range(4):
        last_ref[:, block_at(at_ref[1], -d, 256)] = dot(gqb, q_refs[d][...], LAST)

    @pl.loop(0, 2)
    def _(i):
        src = pl.ds(pl.multiple_of(ROWS + i * 256, 256), 256)
        gn = dot(gkv_ref[src, :].astype(BF16), kv_ref[...], LAST)
        send_ref[pl.ds(pl.multiple_of(i * 256, 256), 256), :] = gn.astype(BF16)


def weight_body(
    at_ref,
    tot_ref,
    score_ref,
    teach_ref,
    gkv_ref,
    gq_ref,
    gr_ref,
    grturn_ref,
    turned_ref,
    turned_other_ref,
    nlast_ref,
    ctx_ref,
    *refs,
):
    out_a, outs_b, loss_ref, skv_ref, g_ref, sr_ref = refs[0], refs[1:5], *refs[5:9]
    srow_scr, sturn_scr, b_scr, sq_scr = refs[9:]
    pb, x = at_ref[0], at_ref[1]
    lane = lax.broadcasted_iota(jnp.int32, (1, HW), 1)

    def pick(v, i):
        return jnp.sum(jnp.where(lane == i, v, 0.0), axis=-1, keepdims=True)

    loss = jnp.zeros((1, 1), F32)
    mine = jnp.zeros((1, HW), F32)
    for q in range(4):
        t = jnp.sum(tot_ref[q * 64 : (q + 1) * 64, :], axis=0, keepdims=True)
        ts, tt, cr = pick(t, 0), pick(t, 1), pick(t, 2)
        loss = loss + (cr / tt - jnp.log(tt) + jnp.log(ts))
        mine = mine + jnp.where(pb == q, t, 0.0)
    loss_ref[...] = loss
    ts, tt = pick(mine, 0), pick(mine, 1)
    row = lax.broadcasted_iota(jnp.int32, (8, HW), 0)
    g = GRAD_SCALE * (jnp.exp(score_ref[...]) / ts - jnp.exp(teach_ref[...] / 2.0) / tt)
    gcol = g[:, 0:1]
    sr = gr_ref[...] * gcol
    sr_ref[...] = sr
    g_ref[...] = g
    sq_scr[...] = (gq_ref[...] * gcol).astype(BF16)
    srow_scr[...] = sr.astype(BF16)
    sturn_scr[...] = (grturn_ref[...] * gcol).astype(BF16)
    for p in range(BOTH):
        rows = slice(p * SEQ, (p + 1) * SEQ)
        skv_ref[rows, :] = (gkv_ref[rows, :] * gcol[p : p + 1, :]).astype(BF16)

    @pl.loop(0, 4)
    def _(i):
        rows = pl.ds(pl.multiple_of(i * 256, 256), 256)
        kv = dot(turned_ref[rows, :], skv_ref[0:ROWS, :]) + dot(
            turned_other_ref[rows, :], skv_ref[ROWS : 2 * ROWS, :]
        )
        o_low = dot(srow_scr[:, rows], ctx_ref[:, 0:256], FIRST)
        rows_x = block_at(x, i, 256)
        q = dot(nlast_ref[:, rows_x], sq_scr[...], FIRST)
        o_high = dot(sturn_scr[:, rows_x], ctx_ref[:, 256:512], FIRST)
        here = pl.ds(i, 1)
        out_a[here, :, 0:512] = kv.astype(BF16)[None]
        out_a[here, :, 512:768] = o_low.astype(BF16)[None]
        b_scr[here, :, 0:512] = q.astype(BF16)[None]
        b_scr[here, :, 512:768] = o_high.astype(BF16)[None]

    for d in range(4):
        outs_b[d][...] = b_scr[d]


def middle_body(at_ref, got_a_ref, *refs):
    b_refs, out_a, out_b, a_scr = refs[0:4], refs[4:8], refs[8], refs[9]
    x = at_ref[1]
    total_a = got_a_ref[0].astype(F32)
    total_b = b_refs[0][...].astype(F32)
    for d in range(1, 4):
        total_a = total_a + got_a_ref[d].astype(F32)
        total_b = total_b + b_refs[d][...].astype(F32)
    out_b[...] = total_b.astype(BF16)
    a_scr[...] = total_a.reshape(8, 4, 8, 768)
    for d in range(4):
        out_a[d][...] = a_scr[:, pl.ds(lax.rem(x + d, 4), 1)].reshape(64, 768).astype(BF16)


def hidden_body(len_ref, h_ref, gain_ref, skv_ref, g_ref, last_ref, other_ref, sr_ref, kv_ref, got_ref, out_ref):
    pos = lax.broadcasted_iota(jnp.int32, (SEQ, 1), 0)

    @pl.loop(0, PAIRS)
    def _(p):
        rows = pl.ds(pl.multiple_of(p * SEQ, SEQ), SEQ)
        at = pos == len_ref[p] - 1
        last = last_ref[pl.ds(p, 1), :] + other_ref[pl.ds(PAIRS + p, 1), :]
        unit = got_ref[rows, :].astype(F32) + jnp.where(at, last, 0.0)
        gn = dot(skv_ref[rows, :], kv_ref[...], LAST) + g_ref[pl.ds(p, 1), 0:1] * unit
        x = h_ref[rows, :].astype(F32)
        inv = lax.rsqrt(jnp.mean(x * x, axis=-1, keepdims=True) + EPS)
        s = gn * gain_ref[...]
        gi = inv * s - x * (inv * inv * inv * jnp.mean(s * x, axis=-1, keepdims=True))
        gi = gi + jnp.where(at, sr_ref[pl.ds(p, 1), :], 0.0)
        out_ref[rows, :] = gi.astype(BF16)


def everyone(x, axes, count):
    return lax.all_to_all(
        jnp.broadcast_to(x[None], (count, *x.shape)), axes, 0, 0, tiled=True
    )


def from_ring(x, axis):
    return [x] + [
        lax.ppermute(x, axis, [(i, (i + d) % 4) for i in range(4)]) for d in range(1, 4)
    ]


def along_ring(pieces, axis):
    return [pieces[0]] + [
        lax.ppermute(pieces[d], axis, [(i, (i + d) % 4) for i in range(4)]) for d in range(1, 4)
    ]


def chunk_turn(v):
    return jnp.transpose(v.reshape(8, 32, 4, 8), (0, 2, 1, 3)).reshape(8, D)


def chunk_back(v):
    return jnp.transpose(v.reshape(8, 4, 32, 8), (0, 2, 1, 3)).reshape(8, D)


def swap(x):
    return lax.ppermute(x, "c", [(0, 1), (1, 0)])


def shards(
    hidden,
    lengths,
    teacher,
    norm_gain,
    final_gain,
    score_vector,
    query_weight,
    key_matrix,
    value_matrix,
    out_weight,
):
    c = lax.axis_index("c")
    first = c == 0
    at = jnp.stack([lax.axis_index("pb"), lax.axis_index("x")]).astype(jnp.int32)
    tokens = hidden.reshape(ROWS, D)
    lens = lengths[0]
    gain = norm_gain[None]
    fg = final_gain[None]
    sv = score_vector[None]
    cos_np, sin_np = rope_consts()
    cos, sin = jnp.asarray(cos_np), jnp.asarray(sin_np)
    turned_out = out_weight.T
    halves = [
        jnp.concatenate(
            [
                key_matrix[:, h * 256 : h * 256 + 256],
                value_matrix[:, h * 256 : h * 256 + 256],
                query_weight[:, h * 512 : h * 512 + 512],
                turned_out[:, h * 512 : h * 512 + 512],
            ],
            axis=1,
        )
        for h in range(2)
    ]
    mine = jnp.where(first, halves[0], halves[1])
    theirs = swap(jnp.where(first, halves[1], halves[0]))
    block = jnp.concatenate(
        [jnp.where(first, mine, theirs), jnp.where(first, theirs, mine)], axis=0
    )
    wide = jnp.concatenate([block[:, 0:512], block[:, 1024:1536], block[:, 512:1024]], axis=1)
    column = everyone(wide, "z", 8).reshape(64, 1536)
    normed, turned, nlast, xlast = call(
        prep_body,
        [lens],
        [tokens, gain],
        [((ROWS, D), BF16), ((D, ROWS), BF16), ((8, D), BF16), ((8, D), F32)],
        flops=10_000_000,
    )
    column, normed, turned, nlast, xlast, lens_late, teach_late = lax.optimization_barrier(
        (column, normed, turned, nlast, xlast, lens, teacher[0])
    )
    lens_both = jnp.concatenate([lens_late, swap(lens_late)])
    teach = jnp.concatenate([teach_late, swap(teach_late)])
    teach = jnp.broadcast_to(teach[:, None], (8, HW))
    other, turned_other = swap(normed), swap(turned)
    nlast = chunk_turn(jnp.concatenate([nlast[0:PAIRS], swap(nlast)[0:PAIRS]], axis=0))
    xlast = jnp.concatenate([xlast[0:PAIRS], swap(xlast)[0:PAIRS]], axis=0)
    slab_b = everyone(column[:, 1024:1536], "pb", 4).reshape(256, 512)
    ring_a = from_ring(column[:, 0:1024], "x")
    (slab_a,) = call(arrange_body, [at], ring_a, [((8, 4, 8, 1024), BF16)])
    slab_a, slab_b = lax.optimization_barrier((slab_a, slab_b))
    slab_a = slab_a.reshape(256, 1024)
    qa = from_ring(slab_b, "x")
    kva = everyone(slab_a[:, 0:512], "pb", 4).reshape(1024, 512)
    oa = from_ring(slab_a[:, 512:1024], "pb")

    kproj, krot, vcast, qproj, qrot, attn, ctx = call(
        attend_body,
        [at, lens_both],
        [normed, other, nlast, cos, sin, kva, *qa],
        [
            ((2 * ROWS, 256), F32),
            ((2 * ROWS, 256), BF16),
            ((2 * ROWS, 256), BF16),
            ((8, 512), F32),
            ((8, 512), BF16),
            ((64, SEQ), F32),
            ((8, 512), BF16),
        ],
        [((8, 512), F32), ((8, 512), F32)],
        flops=1_100_000_000,
    )
    (attended,) = call(attended_body, [at], [ctx, *oa], [((8, D), F32)], flops=10_000_000)
    unit, oscale, score, tot, line = call(
        score_body,
        [],
        [teach, attended, swap(attended), xlast, fg, sv],
        [((8, D), F32), ((8, HW), F32), ((8, HW), F32), ((8, HW), F32), ((1, PAIRS), F32)],
        flops=1_000_000,
    )

    totals = everyone(tot[0:1], AXES, 256).reshape(256, HW)

    gkv, gq, gr, last, send = call(
        unit_back_body,
        [at, lens_both],
        [krot, vcast, kproj, qproj, qrot, attn, unit, oscale, fg, sv, cos, sin, *oa, *qa, kva],
        [((2 * ROWS, 512), F32), ((8, 512), F32), ((8, D), F32), ((8, D), F32), ((ROWS, D), BF16)],
        [((8, 512), F32), ((8, 512), F32), ((8, 512), F32), ((8, D), BF16)],
        flops=200_000_000,
    )
    grturn = chunk_turn(gr)
    last = chunk_back(last)
    got = swap(send)

    pieces = ((4, 256, 768), BF16)
    chip_a, *rest = call(
        weight_body,
        [at],
        [totals, score, teach, gkv, gq, gr, grturn, turned, turned_other, nlast, ctx],
        [pieces]
        + [((256, 768), BF16)] * 4
        + [((1, 1), F32), ((ROWS * 2, 512), BF16), ((8, HW), F32), ((8, D), F32)],
        [((8, D), BF16), ((8, D), BF16), pieces, ((8, 512), BF16)],
        flops=1_100_000_000,
    )
    chip_b, (loss, skv, g, sr) = rest[0:4], rest[4:]
    got_a = lax.all_to_all(chip_a, "pb", 0, 0, tiled=True)
    got_b = along_ring(chip_b, "x")
    (grad_hidden,) = call(
        hidden_body,
        [lens_both],
        [tokens, gain, skv, g, last, swap(last), sr, kva, got],
        [((ROWS, D), BF16)],
        flops=600_000_000,
    )
    got_a, got_b, grad_hidden = lax.optimization_barrier((got_a, got_b, grad_hidden))
    *mid_a, mid_b = call(
        middle_body,
        [at],
        [got_a, *got_b],
        [((64, 768), BF16)] * 4 + [((256, 768), BF16)],
        [((8, 4, 8, 768), F32)],
    )
    done_a = along_ring(mid_a, "x")
    done_b = lax.all_to_all(mid_b.reshape(4, 64, 768), "pb", 0, 0, tiled=True)

    def added(parts):
        total = parts[0].astype(F32)
        for part in parts[1:]:
            total = total + part.astype(F32)
        return total.astype(BF16)

    part = jnp.concatenate([added(done_a), added(done_b)], axis=1)
    rec = lax.all_to_all(part.reshape(8, 8, 1536), "z", 0, 0, tiled=True)
    rec = jnp.sum(rec.astype(F32), axis=0)
    reduced = jnp.concatenate(
        [rec[:, 0:512], rec[:, 768:1280], rec[:, 512:768], rec[:, 1280:1536]], axis=1
    )

    keep = jnp.where(first, reduced[0:4], reduced[4:8])
    got = swap(jnp.where(first, reduced[4:8], reduced[0:4]))
    low = jnp.where(first, keep, got)
    high = jnp.where(first, got, keep)

    def both(a, b):
        return jnp.concatenate([low[:, a:b], high[:, a:b]], axis=1)

    return (
        line,
        loss.reshape(()),
        grad_hidden.reshape(hidden.shape),
        both(512, 1024),
        both(0, 256),
        both(256, 512),
        both(1024, 1536).T,
    )


def solution(mesh):
    torus = Mesh(mesh.devices.reshape(mesh.shape["pb"], 8, 4, 2), AXES)
    placed = (
        P("pb", NEG, None, None),
        P("pb", NEG),
        P("pb", NEG),
        P(),
        P(),
        P(),
        P(AXES, None),
        P(AXES, None),
        P(AXES, None),
        P(None, AXES),
    )
    return jax.shard_map(
        shards,
        mesh=torus,
        in_specs=placed,
        out_specs=(
            P("pb", NEG),
            P(),
            P("pb", NEG, None, None),
            P(AXES, None),
            P(AXES, None),
            P(AXES, None),
            P(None, AXES),
        ),
        check_vma=False,
    )
```

time: 197 us -> 166 us (0.84)
  waiting for transfers between devices: 51.8 us -> 27.8 us
  starting transfers between devices: 62.4 us -> 72.3 us
  Pallas kernels: 40.9 us -> 33.8 us
  local copies, waits for them, and re-layouts: 22.6 us -> 16.1 us
  blocking collectives: 13.8 us -> 11.5 us
    ppermute x6 -> x9, waiting for transfers between devices: 17.8 us -> 0.11 us  [from_ring(): lax.ppermute(x, axis, [(i, (i + d) % 4) for i in range(4)])]
    unnamed x70 -> x28, local copies, waits for them, and re-layouts: 13.3 us -> 1.4 us
    ppermute x6 -> x9, starting transfers between devices: 5.43 us -> 14.3 us  [from_ring(): lax.ppermute(x, axis, [(i, (i + d) % 4) for i in range(4)])]
    pallas_call x10 -> x9, Pallas kernels: 40.9 us -> 33.8 us  [call(): pl.pallas_call(body, grid=(1,), out_shape=[jax.ShapeDtypeStruct(o, d) for...]
    ppermute x10 -> x11, starting transfers between devices: 14.2 us -> 20.7 us  [swap(): return lax.ppermute(x, 'c', [(0, 1), (1, 0)])]
    all_to_all x5 -> x4, starting transfers between devices: 26.2 us -> 21.5 us  [everyone(): lax.all_to_all(jnp.broadcast_to(x[None], (count, *x.shape)), axes, 0, 0,...]
    ppermute x10 -> x11, waiting for transfers between devices: 10.4 us -> 6.82 us  [swap(): return lax.ppermute(x, 'c', [(0, 1), (1, 0)])]
    all_to_all x1, waiting for transfers between devices: 5.97 us -> 3.58 us  [shards(): done_b = lax.all_to_all(mid_b.reshape(4, 64, 768), 'pb', 0, 0, tiled=True)]
  transfers between devices with their start and end apart: 29 -> 32, of which waited for: 22 -> 16; matrix products, arithmetic and copies ran while one was open for 2% -> 7% of each run, Pallas kernels for 13% -> 15%
where the time goes in v1:
time: 166 us; the launch traced here: 165 us
  starting transfers between devices  72.3 us (44%)
  Pallas kernels  33.8 us (20%)
  waiting for transfers between devices  27.8 us (17%)
  local copies, waits for them, and re-layouts  16.1 us (10%)
  blocking collectives  11.5 us (7%)
  other arithmetic  2.92 us (2%)
    pallas_call x9, Pallas kernels, call(): pl.pallas_call(body, grid=(1,), out_shape=[jax.ShapeDtypeStruct(o, d) for...  33.8 us
    all_to_all x4, starting transfers between devices, everyone(): lax.all_to_all(jnp.broadcast_to(x[None], (count, *x.shape)), axes, 0, 0,...  21.5 us
    ppermute x11, starting transfers between devices, swap(): return lax.ppermute(x, 'c', [(0, 1), (1, 0)])  20.7 us
    ppermute x9, starting transfers between devices, from_ring(): lax.ppermute(x, axis, [(i, (i + d) % 4) for i in range(4)])  14.3 us
    all_to_all x1, blocking collectives, shards(): rec = lax.all_to_all(part.reshape(8, 8, 1536), 'z', 0, 0, tiled=True)  11.5 us
    all_to_all x4, waiting for transfers between devices, everyone(): lax.all_to_all(jnp.broadcast_to(x[None], (count, *x.shape)), axes, 0, 0,...  9.45 us
    ppermute x6, waiting for transfers between devices, along_ring(): lax.ppermute(pieces[d], axis, [(i, (i + d) % 4) for i in range(4)])  7.85 us
    ppermute x6, starting transfers between devices, along_ring(): lax.ppermute(pieces[d], axis, [(i, (i + d) % 4) for i in range(4)])  7.06 us
  transfers between devices with their start and end apart: 32, of which 16 were waited for; matrix products, arithmetic and copies ran while one was open for 7% of the time, Pallas kernels for 15%

profile of v1, /device:TPU:1, one launch (start us, length us, event | category | flops | bytes accessed | tf_op | source)
XLA Modules:
  0.0 165.4 jit_solution(5268148511177758388)
XLA Ops:
  2.1 3.3 %collective-permute-start = (bf16[4,1536]{1,0:T(4,128)(2,1)S(1)}, bf16[4,1536]{1,0:T(4,128)(2,1)S(1)}, u32[]{:S(2)}, u32[]{:S(2)}) collective-permute-start(bf16[4,1536]{1,0:T(4,128)(2,1)S(1)} %broadcast_select_fusion.4), channel_id=1, source_target_pairs={{0,1},{1,0},{2,3},{3,2},{4,5},{5,4},{6,7},{7,6},{8,9},{9,8},{10,11... | collective-permute-start | bytes 36872 | tf_op jit(solution)/shard_map/ppermute | solution.py:397
  7.1 6.5 %all-to-all-start = ((bf16[8,8,1536]{2,1,0:T(8,128)(2,1)}), bf16[8,8,1536]{2,1,0:T(8,128)(2,1)S(1)}, u32[]{:S(2)}, u32[]{:S(2)}) async-start(bf16[8,8,1536]{2,1,0:T(8,128)(2,1)} %broadcast_in_dim.18), calls=%async_computation | async-start | bytes 393216 | tf_op jit(solution)/shard_map/all_to_all | solution.py:371
  14.9 2.9 %shard_map.171 = (bf16[512,1024]{1,0:T(8,128)(2,1)S(1)}, bf16[1024,512]{1,0:T(8,128)(2,1)}, bf16[8,1024]{1,0:T(8,128)(2,1)S(1)}, f32[8,1024]{1,0:T(8,128)S(1)}) custom-call(s32[4]{0:T(128)S(1)} %bitcast.47, bf16[512,1024]{1,0:T(8,128)(2,1)} %bitcast.32, f32[1,1024]{1,0:T(1,128)S(1)} %bitcast.45), custom_call_target="tpu_custom_call" | custom-call | flops 10000000 | bytes 3198976 | tf_op jit(solution)/shard_map/pallas_call | solution.py:49
  17.8 5.2 %all-to-all-done = bf16[8,8,1536]{2,1,0:T(8,128)(2,1)S(1)} async-done(((bf16[8,8,1536]{2,1,0:T(8,128)(2,1)}), bf16[8,8,1536]{2,1,0:T(8,128)(2,1)S(1)}, u32[]{:S(2)}, u32[]{:S(2)}) %all-to-all-start) | async-done | bytes 196640 | tf_op jit(solution)/shard_map/all_to_all | solution.py:371
  23.7 4.2 %all-to-all-start.1 = ((bf16[4,64,512]{2,1,0:T(8,128)(2,1)}), bf16[4,64,512]{2,1,0:T(8,128)(2,1)S(1)}, u32[]{:S(2)}, u32[]{:S(2)}) async-start(bf16[4,64,512]{2,1,0:T(8,128)(2,1)} %broadcast_in_dim.21), calls=%async_computation.1 | async-start | bytes 524288 | tf_op jit(solution)/shard_map/all_to_all | solution.py:371
  32.8 3.1 %collective-permute-start.3 = (bf16[512,1024]{1,0:T(8,128)(2,1)S(1)}, bf16[512,1024]{1,0:T(8,128)(2,1)}, u32[]{:S(2)}, u32[]{:S(2)}) collective-permute-start(bf16[512,1024]{1,0:T(8,128)(2,1)S(1)} %get-tuple-element.63.normed_ref), channel_id=1, source_target_pairs={{0,1},{1,0},{2,3},{3,2},{4,5},{5,4},{6,7},{7,6},{8,9},{9,8},{10,11... | collective-permute-start | bytes 3145736 | tf_op jit(solution)/shard_map/ppermute | solution.py:397
  37.8 4.6 %all-to-all-start.2 = ((bf16[4,256,512]{2,1,0:T(8,128)(2,1)}), bf16[4,256,512]{2,1,0:T(8,128)(2,1)}, u32[]{:S(2)}, u32[]{:S(2)}) async-start(bf16[4,256,512]{2,1,0:T(8,128)(2,1)} %broadcast_in_dim.22), calls=%async_computation.2 | async-start | bytes 2097152 | tf_op jit(solution)/shard_map/all_to_all | solution.py:371
  43.0 2.8 %collective-permute-start.9 = (bf16[256,512]{1,0:T(8,128)(2,1)S(1)}, bf16[256,512]{1,0:T(8,128)(2,1)S(1)}, u32[]{:S(2)}, u32[]{:S(2)}) collective-permute-start(bf16[256,512]{1,0:T(8,128)(2,1)S(1)} %bitcast.35), channel_id=1, source_target_pairs={{0,4},{2,6},{4,0},{6,2},{1,5},{3,7},{5,1},{7,3},{8,12},{10,14},{12... | collective-permute-start | bytes 786440 | tf_op jit(solution)/shard_map/ppermute | solution.py:378
  46.5 4.6 %collective-permute-start.1 = (f32[4]{0:T(128)S(1)}, f32[4]{0:T(128)S(1)}, u32[]{:S(2)}, u32[]{:S(2)}) collective-permute-start(f32[4]{0:T(128)S(1)} %bitcast.57), channel_id=1, source_target_pairs={{0,1},{1,0},{2,3},{3,2},{4,5},{5,4},{6,7},{7,6},{8,9},{9,8},{10,11... | collective-permute-start | bytes 56 | tf_op jit(solution)/shard_map/ppermute | solution.py:397
  65.3 6.8 %shard_map.173 = (f32[1024,256]{1,0:T(8,128)}, bf16[1024,256]{1,0:T(8,128)(2,1)S(1)}, bf16[1024,256]{1,0:T(8,128)(2,1)}, f32[8,512]{1,0:T(8,128)S(1)}, bf16[8,51...) custom-call(s32[2]{0:T(128)S(1)} %pad_add_fusion.at_ref, s32[8]{0:T(128)S(1)} %pad_add_fusion.1.len_ref, ...), custom_call_target="tpu_custom_call" | custom-call | flops 1100000000 | bytes 6504448 | tf_op jit(solution)/shard_map/pallas_call | solution.py:49
  77.2 6.3 %all-to-all-start.3 = ((f32[256,1,128]{2,1,0:T(1,128)}), f32[256,1,128]{2,1,0:T(1,128)S(1)}, u32[]{:S(2)}, u32[]{:S(2)}) async-start(f32[256,1,128]{2,1,0:T(1,128)} %broadcast_in_dim.49), calls=%async_computation.3 | async-start | bytes 262144 | tf_op jit(solution)/shard_map/all_to_all | solution.py:371
  83.6 7.5 %shard_map.176 = (f32[1024,512]{1,0:T(8,128)}, f32[8,512]{1,0:T(8,128)S(1)}, f32[8,1024]{1,0:T(8,128)S(1)}, f32[8,1024]{1,0:T(8,128)S(1)}, bf16[512,1024]{1,0:T(8,128)(2,1)}) custom-call(s32[2]{0:T(128)S(1)} %pad_add_fusion.at_ref, s32[8]{0:T(128)S(1)} %pad_add_fusion.1.len_ref, bf16[1024,256]{1,0:T(8,128)(2,1)} %copy-done.4, ...), custom_call_target="tpu_custom_call" | custom-call | flops 200000000 | bytes 8704000 | tf_op jit(solution)/shard_map/pallas_call | solution.py:49
  92.1 4.2 %all-to-all-done.3 = f32[256,1,128]{2,1,0:T(1,128)S(1)} async-done(((f32[256,1,128]{2,1,0:T(1,128)}), f32[256,1,128]{2,1,0:T(1,128)S(1)}, u32[]{:S(2)}, u32[]{:S(2)}) %all-to-all-start.3) | async-done | bytes 131104 | tf_op jit(solution)/shard_map/all_to_all | solution.py:371
  96.3 6.2 %shard_map.177 = (bf16[4,256,768]{2,1,0:T(8,128)(2,1)}, bf16[256,768]{1,0:T(8,128)(2,1)S(1)}, bf16[256,768]{1,0:T(8,128)(2,1)}, bf16[256,768]{1,0:T(8,128)(2,1)S...) custom-call(s32[2]{0:T(128)S(1)} %pad_add_fusion.at_ref, ...), custom_call_target="tpu_custom_call" | custom-call | flops 1100000000 | bytes 8671236 | tf_op jit(solution)/shard_map/pallas_call | solution.py:49
  102.6 4.4 %all-to-all-start.4 = ((bf16[4,256,768]{2,1,0:T(8,128)(2,1)}), bf16[4,256,768]{2,1,0:T(8,128)(2,1)}, u32[]{:S(2)}, u32[]{:S(2)}) async-start(bf16[4,256,768]{2,1,0:T(8,128)(2,1)} %get-tuple-element.86), calls=%async_computation.4 | async-start | bytes 3145728 | tf_op jit(solution)/shard_map/all_to_all | solution.py:518
  117.9 5.3 %shard_map.178 = bf16[512,1024]{1,0:T(8,128)(2,1)} custom-call(s32[8]{0:T(128)S(1)} %pad_add_fusion.1.len_ref, bf16[512,1024]{1,0:T(8,128)(2,1)S(1)} %bitcast.33, f32[1,1024]{1,0:T(1,128)S(1)} %bitcast.46, bf16[1024,512]{1,0:T(8,128)(2,1)} %get-tuple-element.91.skv_ref, f32[8,128]{1,0:T(8,128)S(1)} %get-tuple-element.92.g_ref, ...), custom_call_target="tpu_custom_call" | custom-call | flops 600000000 | bytes 5349376 | tf_op jit(solution)/shard_map/pallas_call | solution.py:49
  123.2 4.7 %collective-permute-done.18.refs_2_ = bf16[256,768]{1,0:T(8,128)(2,1)S(1)} collective-permute-done((bf16[256,768]{1,0:T(8,128)(2,1)S(1)}, bf16[256,768]{1,0:T(8,128)(2,1)S(1)}, u32[]{:S(2)}, u32[]{:S(2)}) %collective-permute-start.18) | collective-permute-done | bytes 393248 | tf_op jit(solution)/shard_map/ppermute | solution.py:384
  128.3 2.9 %shard_map.179 = (bf16[64,768]{1,0:T(8,128)(2,1)S(1)}, bf16[64,768]{1,0:T(8,128)(2,1)S(1)}, bf16[64,768]{1,0:T(8,128)(2,1)S(1)}, bf16[64,768]{1,0:T(8,128)(2,1)S(1)}, bf16[256,768]{1,0:T(8,128)(2,1)}) custom-call(s32[2]{0:T(128)S(1)} %pad_add_fusion.at_ref, bf16[4,256,768]{2,1,0:T(8,128)(2,1)} %all-to-all-done.4.got_a_ref, ...), custom_call_target="tpu_custom_call" | custom-call | bytes 3932160 | tf_op jit(solution)/shard_map/pallas_call | solution.py:49
  131.1 3.0 %collective-permute-start.24 = (bf16[64,768]{1,0:T(8,128)(2,1)S(1)}, bf16[64,768]{1,0:T(8,128)(2,1)S(1)}, u32[]{:S(2)}, u32[]{:S(2)}) collective-permute-start(bf16[64,768]{1,0:T(8,128)(2,1)S(1)} %get-tuple-element.105), channel_id=1, source_target_pairs={{0,6},{2,0},{4,2},{6,4},{1,7},{3,1},{5,3},{7,5},{8,14},{10,8},{12,... | collective-permute-start | bytes 294920 | tf_op jit(solution)/shard_map/ppermute | solution.py:384
  134.8 4.4 %all-to-all-start.5 = ((bf16[4,64,768]{2,1,0:T(8,128)(2,1)}), bf16[4,64,768]{2,1,0:T(8,128)(2,1)S(1)}, u32[]{:S(2)}, u32[]{:S(2)}) async-start(bf16[4,64,768]{2,1,0:T(8,128)(2,1)} %bitcast.20), calls=%async_computation.5 | async-start | bytes 786432 | tf_op jit(solution)/shard_map/all_to_all | solution.py:536
  139.3 2.7 %collective-permute-done.22 = bf16[64,768]{1,0:T(8,128)(2,1)S(1)} collective-permute-done((bf16[64,768]{1,0:T(8,128)(2,1)S(1)}, bf16[64,768]{1,0:T(8,128)(2,1)S(1)}, u32[]{:S(2)}, u32[]{:S(2)}) %collective-permute-start.22) | collective-permute-done | bytes 98336 | tf_op jit(solution)/shard_map/ppermute | solution.py:384
  142.0 3.6 %all-to-all-done.5 = bf16[4,64,768]{2,1,0:T(8,128)(2,1)S(1)} async-done(((bf16[4,64,768]{2,1,0:T(8,128)(2,1)}), bf16[4,64,768]{2,1,0:T(8,128)(2,1)S(1)}, u32[]{:S(2)}, u32[]{:S(2)}) %all-to-all-start.5) | async-done | bytes 393248 | tf_op jit(solution)/shard_map/all_to_all | solution.py:536
  145.7 11.5 %all_to_all.35 = bf16[8,8,1536]{2,1,0:T(8,128)(2,1)S(1)} all-to-all(bf16[8,8,1536]{2,1,0:T(8,128)(2,1)S(1)} %maximum_bitcast_fusion), channel_id=1, replica_groups=mesh['pb'=4,'z'=8,'x'=4,'c'=2] {'z'}, dimensions={0} | all-to-all | bytes 393216 | tf_op jit(solution)/shard_map/all_to_all | solution.py:545
  157.2 4.8 %collective-permute-start.25 = (f32[4,1536]{1,0:T(4,128)S(1)}, f32[4,1536]{1,0:T(4,128)S(1)}, u32[]{:S(2)}, u32[]{:S(2)}) collective-permute-start(f32[4,1536]{1,0:T(4,128)S(1)} %slice_select_fusion), channel_id=1, source_target_pairs={{0,1},{1,0},{2,3},{3,2},{4,5},{5,4},{6,7},{7,6},{8,9},{9,8},{10,11... | collective-permute-start | bytes 73736 | tf_op jit(solution)/shard_map/ppermute | solution.py:397
  (128 shorter events, 48.9 us)
Async XLA Ops:
  7.1 15.9 %all-to-all-start = ((bf16[8,8,1536]{2,1,0:T(8,128)(2,1)}), bf16[8,8,1536]{2,1,0:T(8,128)(2,1)S(1)}, u32[]{:S(2)}, u32[]{:S(2)}) async-start(bf16[8,8,1536]{2,1,0:T(8,128)(2,1)} %broadcast_in_dim.18), calls=%async_computation | async-start | bytes 393216 | tf_op jit(solution)/shard_map/all_to_all | solution.py:371
  23.7 12.9 %all-to-all-start.1 = ((bf16[4,64,512]{2,1,0:T(8,128)(2,1)}), bf16[4,64,512]{2,1,0:T(8,128)(2,1)S(1)}, u32[]{:S(2)}, u32[]{:S(2)}) async-start(bf16[4,64,512]{2,1,0:T(8,128)(2,1)} %broadcast_in_dim.21), calls=%async_computation.1 | async-start | bytes 524288 | tf_op jit(solution)/shard_map/all_to_all | solution.py:371
  27.9 8.0 %collective-permute-start.5 = (bf16[64,1024]{1,0:T(8,128)(2,1)S(1)}, bf16[64,1024]{1,0:T(8,128)(2,1)S(1)}, u32[]{:S(2)}, u32[]{:S(2)}) collective-permute-start(bf16[64,1024]{1,0:T(8,128)(2,1)S(1)} %slice.124.refs_0_), channel_id=1, source_target_pairs={{0,2},{2,4},{4,6},{6,0},{1,3},{3,5},{5,7},{7,1},{8,10},{10,12},{12... | collective-permute-start | bytes 393224 | tf_op jit(solution)/shard_map/ppermute | solution.py:378
  29.2 6.8 %collective-permute-start.6 = (bf16[64,1024]{1,0:T(8,128)(2,1)S(1)}, bf16[64,1024]{1,0:T(8,128)(2,1)S(1)}, u32[]{:S(2)}, u32[]{:S(2)}) collective-permute-start(bf16[64,1024]{1,0:T(8,128)(2,1)S(1)} %slice.124.refs_0_), channel_id=1, source_target_pairs={{0,4},{2,6},{4,0},{6,2},{1,5},{3,7},{5,1},{7,3},{8,12},{10,14},{12... | collective-permute-start | bytes 393224 | tf_op jit(solution)/shard_map/ppermute | solution.py:378
  32.8 32.5 %collective-permute-start.3 = (bf16[512,1024]{1,0:T(8,128)(2,1)S(1)}, bf16[512,1024]{1,0:T(8,128)(2,1)}, u32[]{:S(2)}, u32[]{:S(2)}) collective-permute-start(bf16[512,1024]{1,0:T(8,128)(2,1)S(1)} %get-tuple-element.63.normed_ref), channel_id=1, source_target_pairs={{0,1},{1,0},{2,3},{3,2},{4,5},{5,4},{6,7},{7,6},{8,9},{9,8},{10,11... | collective-permute-start | bytes 3145736 | tf_op jit(solution)/shard_map/ppermute | solution.py:397
  37.8 27.5 %all-to-all-start.2 = ((bf16[4,256,512]{2,1,0:T(8,128)(2,1)}), bf16[4,256,512]{2,1,0:T(8,128)(2,1)}, u32[]{:S(2)}, u32[]{:S(2)}) async-start(bf16[4,256,512]{2,1,0:T(8,128)(2,1)} %broadcast_in_dim.22), calls=%async_computation.2 | async-start | bytes 2097152 | tf_op jit(solution)/shard_map/all_to_all | solution.py:371
  42.4 13.4 %collective-permute-start.8 = (bf16[256,512]{1,0:T(8,128)(2,1)S(1)}, bf16[256,512]{1,0:T(8,128)(2,1)S(1)}, u32[]{:S(2)}, u32[]{:S(2)}) collective-permute-start(bf16[256,512]{1,0:T(8,128)(2,1)S(1)} %bitcast.34), channel_id=1, source_target_pairs={{0,2},{2,4},{4,6},{6,0},{1,3},{3,5},{5,7},{7,1},{8,10},{10,12},{12... | collective-permute-start | bytes 786440 | tf_op jit(solution)/shard_map/ppermute | solution.py:378
  43.0 14.6 %collective-permute-start.9 = (bf16[256,512]{1,0:T(8,128)(2,1)S(1)}, bf16[256,512]{1,0:T(8,128)(2,1)S(1)}, u32[]{:S(2)}, u32[]{:S(2)}) collective-permute-start(bf16[256,512]{1,0:T(8,128)(2,1)S(1)} %bitcast.35), channel_id=1, source_target_pairs={{0,4},{2,6},{4,0},{6,2},{1,5},{3,7},{5,1},{7,3},{8,12},{10,14},{12... | collective-permute-start | bytes 786440 | tf_op jit(solution)/shard_map/ppermute | solution.py:378
  45.8 14.2 %collective-permute-start.10 = (bf16[256,512]{1,0:T(8,128)(2,1)S(1)}, bf16[256,512]{1,0:T(8,128)(2,1)S(1)}, u32[]{:S(2)}, u32[]{:S(2)}) collective-permute-start(bf16[256,512]{1,0:T(8,128)(2,1)S(1)} %bitcast.36), channel_id=1, source_target_pairs={{0,6},{2,0},{4,2},{6,4},{1,7},{3,1},{5,3},{7,5},{8,14},{10,8},{12,... | collective-permute-start | bytes 786440 | tf_op jit(solution)/shard_map/ppermute | solution.py:378
  46.5 5.4 %collective-permute-start.1 = (f32[4]{0:T(128)S(1)}, f32[4]{0:T(128)S(1)}, u32[]{:S(2)}, u32[]{:S(2)}) collective-permute-start(f32[4]{0:T(128)S(1)} %bitcast.57), channel_id=1, source_target_pairs={{0,1},{1,0},{2,3},{3,2},{4,5},{5,4},{6,7},{7,6},{8,9},{9,8},{10,11... | collective-permute-start | bytes 56 | tf_op jit(solution)/shard_map/ppermute | solution.py:397
  55.4 36.7 %collective-permute-start.16 = (bf16[1024,512]{1,0:T(8,128)(2,1)}, bf16[1024,512]{1,0:T(8,128)(2,1)}, u32[]{:S(2)}, u32[]{:S(2)}) collective-permute-start(bf16[1024,512]{1,0:T(8,128)(2,1)} %get-tuple-element.84.turned_ref), channel_id=1, source_target_pairs={{0,1},{1,0},{2,3},{3,2},{4,5},{5,4},{6,7},{7,6},{8,9},{9,8},{10,11... | collective-permute-start | bytes 3145736 | tf_op jit(solution)/shard_map/ppermute | solution.py:397
  55.8 16.3 %collective-permute-start.11 = (bf16[256,512]{1,0:T(8,128)(2,1)S(1)}, bf16[256,512]{1,0:T(8,128)(2,1)S(1)}, u32[]{:S(2)}, u32[]{:S(2)}) collective-permute-start(bf16[256,512]{1,0:T(8,128)(2,1)S(1)} %get-tuple-element.107.refs_0_), channel_id=1, source_target_pairs={{0,64},{64,128},{128,192},{192,0},{1,65},{65,129},{129,193},{193,1... | collective-permute-start | bytes 786440 | tf_op jit(solution)/shard_map/ppermute | solution.py:378
  57.5 14.6 %collective-permute-start.12 = (bf16[256,512]{1,0:T(8,128)(2,1)S(1)}, bf16[256,512]{1,0:T(8,128)(2,1)S(1)}, u32[]{:S(2)}, u32[]{:S(2)}) collective-permute-start(bf16[256,512]{1,0:T(8,128)(2,1)S(1)} %get-tuple-element.107.refs_0_), channel_id=1, source_target_pairs={{0,128},{64,192},{128,0},{192,64},{1,129},{65,193},{129,1},{193,65... | collective-permute-start | bytes 786440 | tf_op jit(solution)/shard_map/ppermute | solution.py:378
  59.9 12.2 %collective-permute-start.13 = (bf16[256,512]{1,0:T(8,128)(2,1)S(1)}, bf16[256,512]{1,0:T(8,128)(2,1)S(1)}, u32[]{:S(2)}, u32[]{:S(2)}) collective-permute-start(bf16[256,512]{1,0:T(8,128)(2,1)S(1)} %get-tuple-element.107.refs_0_), channel_id=1, source_target_pairs={{0,192},{64,0},{128,64},{192,128},{1,193},{65,1},{129,65},{193,129... | collective-permute-start | bytes 786440 | tf_op jit(solution)/shard_map/ppermute | solution.py:378
  77.2 19.1 %all-to-all-start.3 = ((f32[256,1,128]{2,1,0:T(1,128)}), f32[256,1,128]{2,1,0:T(1,128)S(1)}, u32[]{:S(2)}, u32[]{:S(2)}) async-start(f32[256,1,128]{2,1,0:T(1,128)} %broadcast_in_dim.49), calls=%async_computation.3 | async-start | bytes 262144 | tf_op jit(solution)/shard_map/all_to_all | solution.py:371
  102.6 25.7 %all-to-all-start.4 = ((bf16[4,256,768]{2,1,0:T(8,128)(2,1)}), bf16[4,256,768]{2,1,0:T(8,128)(2,1)}, u32[]{:S(2)}, u32[]{:S(2)}) async-start(bf16[4,256,768]{2,1,0:T(8,128)(2,1)} %get-tuple-element.86), calls=%async_computation.4 | async-start | bytes 3145728 | tf_op jit(solution)/shard_map/all_to_all | solution.py:518
  106.9 11.0 %collective-permute-start.21 = (bf16[512,1024]{1,0:T(8,128)(2,1)}, bf16[512,1024]{1,0:T(8,128)(2,1)}, u32[]{:S(2)}, u32[]{:S(2)}) collective-permute-start(bf16[512,1024]{1,0:T(8,128)(2,1)} %get-tuple-element.95), channel_id=1, source_target_pairs={{0,1},{1,0},{2,3},{3,2},{4,5},{5,4},{6,7},{7,6},{8,9},{9,8},{10,11... | collective-permute-start | bytes 3145736 | tf_op jit(solution)/shard_map/ppermute | solution.py:397
  107.5 15.7 %collective-permute-start.17 = (bf16[256,768]{1,0:T(8,128)(2,1)}, bf16[256,768]{1,0:T(8,128)(2,1)S(1)}, u32[]{:S(2)}, u32[]{:S(2)}) collective-permute-start(bf16[256,768]{1,0:T(8,128)(2,1)} %get-tuple-element.88), channel_id=1, source_target_pairs={{0,2},{2,4},{4,6},{6,0},{1,3},{3,5},{5,7},{7,1},{8,10},{10,12},{12... | collective-permute-start | bytes 1179656 | tf_op jit(solution)/shard_map/ppermute | solution.py:384
  107.9 20.1 %collective-permute-start.18 = (bf16[256,768]{1,0:T(8,128)(2,1)S(1)}, bf16[256,768]{1,0:T(8,128)(2,1)S(1)}, u32[]{:S(2)}, u32[]{:S(2)}) collective-permute-start(bf16[256,768]{1,0:T(8,128)(2,1)S(1)} %get-tuple-element.89), channel_id=1, source_target_pairs={{0,4},{2,6},{4,0},{6,2},{1,5},{3,7},{5,1},{7,3},{8,12},{10,14},{12... | collective-permute-start | bytes 1179656 | tf_op jit(solution)/shard_map/ppermute | solution.py:384
  110.0 18.3 %collective-permute-start.19 = (bf16[256,768]{1,0:T(8,128)(2,1)S(1)}, bf16[256,768]{1,0:T(8,128)(2,1)}, u32[]{:S(2)}, u32[]{:S(2)}) collective-permute-start(bf16[256,768]{1,0:T(8,128)(2,1)S(1)} %get-tuple-element.90), channel_id=1, source_target_pairs={{0,6},{2,0},{4,2},{6,4},{1,7},{3,1},{5,3},{7,5},{8,14},{10,8},{12,... | collective-permute-start | bytes 1179656 | tf_op jit(solution)/shard_map/ppermute | solution.py:384
  131.1 8.0 %collective-permute-start.24 = (bf16[64,768]{1,0:T(8,128)(2,1)S(1)}, bf16[64,768]{1,0:T(8,128)(2,1)S(1)}, u32[]{:S(2)}, u32[]{:S(2)}) collective-permute-start(bf16[64,768]{1,0:T(8,128)(2,1)S(1)} %get-tuple-element.105), channel_id=1, source_target_pairs={{0,6},{2,0},{4,2},{6,4},{1,7},{3,1},{5,3},{7,5},{8,14},{10,8},{12,... | collective-permute-start | bytes 294920 | tf_op jit(solution)/shard_map/ppermute | solution.py:384
  134.3 7.6 %collective-permute-start.22 = (bf16[64,768]{1,0:T(8,128)(2,1)S(1)}, bf16[64,768]{1,0:T(8,128)(2,1)S(1)}, u32[]{:S(2)}, u32[]{:S(2)}) collective-permute-start(bf16[64,768]{1,0:T(8,128)(2,1)S(1)} %get-tuple-element.103), channel_id=1, source_target_pairs={{0,2},{2,4},{4,6},{6,0},{1,3},{3,5},{5,7},{7,1},{8,10},{10,12},{12... | collective-permute-start | bytes 294920 | tf_op jit(solution)/shard_map/ppermute | solution.py:384
  134.8 10.8 %all-to-all-start.5 = ((bf16[4,64,768]{2,1,0:T(8,128)(2,1)}), bf16[4,64,768]{2,1,0:T(8,128)(2,1)S(1)}, u32[]{:S(2)}, u32[]{:S(2)}) async-start(bf16[4,64,768]{2,1,0:T(8,128)(2,1)} %bitcast.20), calls=%async_computation.5 | async-start | bytes 786432 | tf_op jit(solution)/shard_map/all_to_all | solution.py:536
  157.2 5.7 %collective-permute-start.25 = (f32[4,1536]{1,0:T(4,128)S(1)}, f32[4,1536]{1,0:T(4,128)S(1)}, u32[]{:S(2)}, u32[]{:S(2)}) collective-permute-start(f32[4,1536]{1,0:T(4,128)S(1)} %slice_select_fusion), channel_id=1, source_target_pairs={{0,1},{1,0},{2,3},{3,2},{4,5},{5,4},{6,7},{7,6},{8,9},{9,8},{10,11... | collective-permute-start | bytes 73736 | tf_op jit(solution)/shard_map/ppermute | solution.py:397
  (22 other events, 203.2 us)

commit v2 on v1

--- a/solution.py
+++ b/solution.py
@@ -124,7 +124,7 @@
     a_refs, out_ref = refs[0:4], refs[4]
     x = at_ref[1]
     for d in range(4):
-        out_ref[:, pl.ds(lax.rem(x - d + 4, 4), 1)] = a_refs[d][...].reshape(8, 1, 8, 1024)
+        out_ref[:, pl.ds(lax.rem(x - d + 4, 4), 1)] = a_refs[d][...].reshape(8, 1, 8, 768)
 
 
 def attend_body(
@@ -141,13 +141,13 @@
         def _(i):
             src = pl.ds(pl.multiple_of(i * 256, 256), 256)
             dst = pl.ds(pl.multiple_of(side * ROWS + i * 256, 256), 256)
-            kv = dot(rows_ref[src, :], kv_ref[...])
+            kv = dot(rows_ref[src, :], kv_ref[:, 0:512])
             kproj_ref[dst, :] = kv[:, 0:256]
             vcast_ref[dst, :] = kv[:, 256:512].astype(BF16)
 
     q = jnp.zeros((8, 512), F32)
     for d in range(4):
-        q = q + dot(nlast_ref[:, block_at(x, -d, 256)], q_refs[d][...])
+        q = q + dot(nlast_ref[:, block_at(x, -d, 256)], q_refs[d][:, 0:512])
     qproj_ref[...] = q
     cos_q, sin_q = query_tables(len_ref, cos_ref, sin_ref)
     for h in range(4):
@@ -173,10 +173,15 @@
     ctx_ref[...] = ctx_scr[...].astype(BF16)
 
 
-def attended_body(at_ref, ctx_ref, *refs):
-    o_refs, out_ref = refs[0:4], refs[4]
+def attended_body(at_ref, ctx_ref, kvo_ref, *refs):
+    qo_refs, out_ref, o_ref, turn_scr = refs[0:4], refs[4], refs[5], refs[6]
     for d in range(4):
-        out_ref[:, block_at(at_ref[0], -d, 256)] = dot(ctx_ref[...], o_refs[d][...], LAST)
+        turn_scr[:, pl.ds(lax.rem(at_ref[1] - d + 4, 4), 1)] = qo_refs[d][:, 512:768].reshape(
+            32, 1, 8, 256
+        )
+    o_ref[:, 0:256] = kvo_ref[:, 512:768]
+    o_ref[:, 256:512] = turn_scr[...].reshape(1024, 256)
+    out_ref[...] = dot(ctx_ref[...], o_ref[...], LAST)
 
 
 def score_body(teach_ref, mine_ref, theirs_ref, xlast_ref, fg_ref, sv_ref, *refs):
@@ -217,18 +222,14 @@
     sin_ref,
     *refs,
 ):
-    o_refs, q_refs, kv_ref = refs[0:4], refs[4:8], refs[8]
-    gkv_ref, gq_ref, gr_ref, last_ref, send_ref, gc_scr, gq_scr, qr_scr, gr_scr = refs[9:]
+    o_ref, q_refs, kv_ref = refs[0], refs[1:5], refs[5]
+    gkv_ref, gq_ref, gr_ref, last_ref, send_ref, gc_scr, gq_scr, qr_scr = refs[6:]
     mask, even = block_mask()
     unit = unit_ref[...]
     gu = sv_ref[...] * fg_ref[...]
     gr = oscale_ref[:, 0:1] * (gu - unit * jnp.mean(gu * unit, axis=-1, keepdims=True))
     gr_ref[...] = gr
-    gr_scr[...] = gr.astype(BF16)
-    gc = jnp.zeros((8, 512), F32)
-    for d in range(4):
-        gc = gc + dot(gr_scr[:, block_at(at_ref[0], -d, 256)], o_refs[d][...])
-    gc_scr[...] = gc
+    gc_scr[...] = dot(gr.astype(BF16), o_ref[...])
     qr_scr[...] = qrot_ref[...].astype(F32)
     for p in range(BOTH):
         rows = slice(p * SEQ, (p + 1) * SEQ)
@@ -261,12 +262,12 @@
         )
     gqb = gq_ref[...].astype(BF16)
     for d in range(4):
-        last_ref[:, block_at(at_ref[1], -d, 256)] = dot(gqb, q_refs[d][...], LAST)
+        last_ref[:, block_at(at_ref[1], -d, 256)] = dot(gqb, q_refs[d][:, 0:512], LAST)
 
     @pl.loop(0, 2)
     def _(i):
         src = pl.ds(pl.multiple_of(ROWS + i * 256, 256), 256)
-        gn = dot(gkv_ref[src, :].astype(BF16), kv_ref[...], LAST)
+        gn = dot(gkv_ref[src, :].astype(BF16), kv_ref[:, 0:512], LAST)
         send_ref[pl.ds(pl.multiple_of(i * 256, 256), 256), :] = gn.astype(BF16)
 
 
@@ -358,13 +359,25 @@
         at = pos == len_ref[p] - 1
         last = last_ref[pl.ds(p, 1), :] + other_ref[pl.ds(PAIRS + p, 1), :]
         unit = got_ref[rows, :].astype(F32) + jnp.where(at, last, 0.0)
-        gn = dot(skv_ref[rows, :], kv_ref[...], LAST) + g_ref[pl.ds(p, 1), 0:1] * unit
+        gn = dot(skv_ref[rows, :], kv_ref[:, 0:512], LAST) + g_ref[pl.ds(p, 1), 0:1] * unit
         x = h_ref[rows, :].astype(F32)
         inv = lax.rsqrt(jnp.mean(x * x, axis=-1, keepdims=True) + EPS)
         s = gn * gain_ref[...]
         gi = inv * s - x * (inv * inv * inv * jnp.mean(s * x, axis=-1, keepdims=True))
         gi = gi + jnp.where(at, sr_ref[pl.ds(p, 1), :], 0.0)
         out_ref[rows, :] = gi.astype(BF16)
+
+
+def finish_body(rec_ref, gq_ref, gk_ref, gv_ref, go_ref):
+    for h in range(2):
+        total = rec_ref[0, h].astype(F32)
+        for z in range(1, 8):
+            total = total + rec_ref[z, h].astype(F32)
+        gk_ref[:, h * 256 : h * 256 + 256] = total[:, 0:256]
+        gv_ref[:, h * 256 : h * 256 + 256] = total[:, 256:512]
+        go_ref[:, h * 512 : h * 512 + 256] = total[:, 512:768]
+        gq_ref[:, h * 512 : h * 512 + 512] = total[:, 768:1280]
+        go_ref[:, h * 512 + 256 : h * 512 + 512] = total[:, 1280:1536]
 
 
 def everyone(x, axes, count):
@@ -409,8 +422,6 @@
     value_matrix,
     out_weight,
 ):
-    c = lax.axis_index("c")
-    first = c == 0
     at = jnp.stack([lax.axis_index("pb"), lax.axis_index("x")]).astype(jnp.int32)
     tokens = hidden.reshape(ROWS, D)
     lens = lengths[0]
@@ -425,20 +436,16 @@
             [
                 key_matrix[:, h * 256 : h * 256 + 256],
                 value_matrix[:, h * 256 : h * 256 + 256],
+                turned_out[:, h * 512 : h * 512 + 256],
                 query_weight[:, h * 512 : h * 512 + 512],
-                turned_out[:, h * 512 : h * 512 + 512],
+                turned_out[:, h * 512 + 256 : h * 512 + 512],
             ],
             axis=1,
         )
         for h in range(2)
     ]
-    mine = jnp.where(first, halves[0], halves[1])
-    theirs = swap(jnp.where(first, halves[1], halves[0]))
-    block = jnp.concatenate(
-        [jnp.where(first, mine, theirs), jnp.where(first, theirs, mine)], axis=0
-    )
-    wide = jnp.concatenate([block[:, 0:512], block[:, 1024:1536], block[:, 512:1024]], axis=1)
-    column = everyone(wide, "z", 8).reshape(64, 1536)
+    both_halves = jnp.broadcast_to(jnp.stack(halves)[None], (8, 2, 4, 1536)).reshape(16, 4, 1536)
+    column = lax.all_to_all(both_halves, ("z", "c"), 0, 0, tiled=True).reshape(64, 1536)
     normed, turned, nlast, xlast = call(
         prep_body,
         [lens],
@@ -446,28 +453,36 @@
         [((ROWS, D), BF16), ((D, ROWS), BF16), ((8, D), BF16), ((8, D), F32)],
         flops=10_000_000,
     )
-    column, normed, turned, nlast, xlast, lens_late, teach_late = lax.optimization_barrier(
-        (column, normed, turned, nlast, xlast, lens, teacher[0])
-    )
-    lens_both = jnp.concatenate([lens_late, swap(lens_late)])
-    teach = jnp.concatenate([teach_late, swap(teach_late)])
-    teach = jnp.broadcast_to(teach[:, None], (8, HW))
-    other, turned_other = swap(normed), swap(turned)
-    nlast = chunk_turn(jnp.concatenate([nlast[0:PAIRS], swap(nlast)[0:PAIRS]], axis=0))
-    xlast = jnp.concatenate([xlast[0:PAIRS], swap(xlast)[0:PAIRS]], axis=0)
-    slab_b = everyone(column[:, 1024:1536], "pb", 4).reshape(256, 512)
-    ring_a = from_ring(column[:, 0:1024], "x")
-    (slab_a,) = call(arrange_body, [at], ring_a, [((8, 4, 8, 1024), BF16)])
-    slab_a, slab_b = lax.optimization_barrier((slab_a, slab_b))
-    slab_a = slab_a.reshape(256, 1024)
-    qa = from_ring(slab_b, "x")
-    kva = everyone(slab_a[:, 0:512], "pb", 4).reshape(1024, 512)
-    oa = from_ring(slab_a[:, 512:1024], "pb")
+    nlast = chunk_turn(nlast)
+    wide = (PAIRS, HW)
+    pack = jnp.concatenate(
+        [
+            xlast[0:PAIRS],
+            nlast[0:PAIRS].astype(F32),
+            jnp.broadcast_to(lens.astype(F32)[:, None], wide),
+            jnp.broadcast_to(teacher[0][:, None], wide),
+        ],
+        axis=1,
+    )
+    column, normed, turned, pack = lax.optimization_barrier((column, normed, turned, pack))
+    other = swap(normed)
+    got = swap(pack)
+    slab_b = everyone(column[:, 768:1536], "pb", 4).reshape(256, 768)
+    ring_a = from_ring(column[:, 0:768], "x")
+    (slab_a,) = call(arrange_body, [at], ring_a, [((8, 4, 8, 768), BF16)])
+    slab_a, slab_b, other, got = lax.optimization_barrier((slab_a, slab_b, other, got))
+    packed = jnp.concatenate([pack, got], axis=0)
+    xlast = packed[:, 0:1024]
+    nlast = packed[:, 1024:2048].astype(BF16)
+    lens_both = packed[:, 2048].astype(jnp.int32)
+    teach = packed[:, 2048 + HW :]
+    kvo = everyone(slab_a.reshape(256, 768), "pb", 4).reshape(1024, 768)
+    qo = from_ring(slab_b, "x")
 
     kproj, krot, vcast, qproj, qrot, attn, ctx = call(
         attend_body,
         [at, lens_both],
-        [normed, other, nlast, cos, sin, kva, *qa],
+        [normed, other, nlast, cos, sin, kvo, *qo],
         [
             ((2 * ROWS, 256), F32),
             ((2 * ROWS, 256), BF16),
@@ -480,7 +495,16 @@
         [((8, 512), F32), ((8, 512), F32)],
         flops=1_100_000_000,
     )
-    (attended,) = call(attended_body, [at], [ctx, *oa], [((8, D), F32)], flops=10_000_000)
+    ctx, turned_late = lax.optimization_barrier((ctx, turned))
+    turned_other = swap(turned_late)
+    attended, oa = call(
+        attended_body,
+        [at],
+        [ctx, kvo, *qo],
+        [((8, D), F32), ((D, 512), BF16)],
+        [((32, 4, 8, 256), BF16)],
+        flops=10_000_000,
+    )
     unit, oscale, score, tot, line = call(
         score_body,
         [],
@@ -494,9 +518,9 @@
     gkv, gq, gr, last, send = call(
         unit_back_body,
         [at, lens_both],
-        [krot, vcast, kproj, qproj, qrot, attn, unit, oscale, fg, sv, cos, sin, *oa, *qa, kva],
+        [krot, vcast, kproj, qproj, qrot, attn, unit, oscale, fg, sv, cos, sin, oa, *qo, kvo],
         [((2 * ROWS, 512), F32), ((8, 512), F32), ((8, D), F32), ((8, D), F32), ((ROWS, D), BF16)],
-        [((8, 512), F32), ((8, 512), F32), ((8, 512), F32), ((8, D), BF16)],
+        [((8, 512), F32), ((8, 512), F32), ((8, 512), F32)],
         flops=200_000_000,
     )
     grturn = chunk_turn(gr)
@@ -520,7 +544,7 @@
     (grad_hidden,) = call(
         hidden_body,
         [lens_both],
-        [tokens, gain, skv, g, last, swap(last), sr, kva, got],
+        [tokens, gain, skv, g, last, swap(last), sr, kvo, got],
         [((ROWS, D), BF16)],
         flops=600_000_000,
     )
@@ -542,28 +566,22 @@
         return total.astype(BF16)
 
     part = jnp.concatenate([added(done_a), added(done_b)], axis=1)
-    rec = lax.all_to_all(part.reshape(8, 8, 1536), "z", 0, 0, tiled=True)
-    rec = jnp.sum(rec.astype(F32), axis=0)
-    reduced = jnp.concatenate(
-        [rec[:, 0:512], rec[:, 768:1280], rec[:, 512:768], rec[:, 1280:1536]], axis=1
-    )
-
-    keep = jnp.where(first, reduced[0:4], reduced[4:8])
-    got = swap(jnp.where(first, reduced[4:8], reduced[0:4]))
-    low = jnp.where(first, keep, got)
-    high = jnp.where(first, got, keep)
-
-    def both(a, b):
-        return jnp.concatenate([low[:, a:b], high[:, a:b]], axis=1)
+    rec = lax.all_to_all(part.reshape(16, 4, 1536), ("z", "c"), 0, 0, tiled=True)
+    grad_query, grad_key, grad_value, grad_out = call(
+        finish_body,
+        [],
+        [rec.reshape(8, 2, 4, 1536)],
+        [((4, D), F32), ((4, 512), F32), ((4, 512), F32), ((4, D), F32)],
+    )
 
     return (
         line,
         loss.reshape(()),
         grad_hidden.reshape(hidden.shape),
-        both(512, 1024),
-        both(0, 256),
-        both(256, 512),
-        both(1024, 1536).T,
+        grad_query,
+        grad_key,
+        grad_value,
+        grad_out.T,
     )
 
 

time: 166 us -> 169 us (1.018)
  starting transfers between devices: 72.3 us -> 56.4 us
  waiting for transfers between devices: 27.8 us -> 40.4 us
  blocking collectives: 11.5 us -> 17.1 us
  Pallas kernels: 33.8 us -> 37.3 us
  other arithmetic: 2.92 us -> 0.39 us
    ppermute x9 -> x6, waiting for transfers between devices: 0.11 us -> 17.8 us  [from_ring(): lax.ppermute(x, axis, [(i, (i + d) % 4) for i in range(4)])]
    ppermute x11 -> x6, starting transfers between devices: 20.7 us -> 5.1 us  [swap(): return lax.ppermute(x, 'c', [(0, 1), (1, 0)])]
    all_to_all x0 -> x1, starting transfers between devices: none -> 9.98 us  [shards(): lax.all_to_all(both_halves, ('z', 'c'), 0, 0, tiled=True).reshape(64, 1536)]
    ppermute x9 -> x6, starting transfers between devices: 14.3 us -> 8.67 us  [from_ring(): lax.ppermute(x, axis, [(i, (i + d) % 4) for i in range(4)])]
    all_to_all x1, blocking collectives: 11.5 us -> 17.1 us  [shards(): lax.all_to_all(part.reshape(16, 4, 1536), ('z', 'c'), 0, 0, tiled=True)]
    all_to_all x4 -> x3, waiting for transfers between devices: 9.45 us -> 3.88 us  [everyone(): lax.all_to_all(jnp.broadcast_to(x[None], (count, *x.shape)), axes, 0, 0,...]
    all_to_all x0 -> x1, waiting for transfers between devices: none -> 5.06 us  [shards(): lax.all_to_all(both_halves, ('z', 'c'), 0, 0, tiled=True).reshape(64, 1536)]
    ppermute x11 -> x6, waiting for transfers between devices: 6.82 us -> 2.06 us  [swap(): return lax.ppermute(x, 'c', [(0, 1), (1, 0)])]
  transfers between devices with their start and end apart: 32 -> 24, of which waited for: 16 -> 14; matrix products, arithmetic and copies ran while one was open for 7% -> 5% of each run, Pallas kernels for 15% -> 12%
where the time goes in v2:
time: 169 us; the launch traced here: 168 us
  starting transfers between devices  56.4 us (33%)
  waiting for transfers between devices  40.4 us (24%)
  Pallas kernels  37.3 us (22%)
  blocking collectives  17.1 us (10%)
  local copies, waits for them, and re-layouts  15.5 us (9%)
    pallas_call x10, Pallas kernels, call(): pl.pallas_call(body, grid=(1,), out_shape=[jax.ShapeDtypeStruct(o, d) for...  37.3 us
    ppermute x6, waiting for transfers between devices, from_ring(): lax.ppermute(x, axis, [(i, (i + d) % 4) for i in range(4)])  17.8 us
    all_to_all x1, blocking collectives, shards(): lax.all_to_all(part.reshape(16, 4, 1536), ('z', 'c'), 0, 0, tiled=True)  17.1 us
    all_to_all x3, starting transfers between devices, everyone(): lax.all_to_all(jnp.broadcast_to(x[None], (count, *x.shape)), axes, 0, 0,...  16.9 us
    all_to_all x1, starting transfers between devices, shards(): lax.all_to_all(both_halves, ('z', 'c'), 0, 0, tiled=True).reshape(64, 1536)  9.98 us
    ppermute x6, starting transfers between devices, from_ring(): lax.ppermute(x, axis, [(i, (i + d) % 4) for i in range(4)])  8.67 us
    ppermute x6, waiting for transfers between devices, along_ring(): lax.ppermute(pieces[d], axis, [(i, (i + d) % 4) for i in range(4)])  7.92 us
    ppermute x6, starting transfers between devices, along_ring(): lax.ppermute(pieces[d], axis, [(i, (i + d) % 4) for i in range(4)])  7.03 us
  transfers between devices with their start and end apart: 24, of which 14 were waited for; matrix products, arithmetic and copies ran while one was open for 5% of the time, Pallas kernels for 12%

profile of v2, /device:TPU:1, one launch (start us, length us, event | category | flops | bytes accessed | tf_op | source)
XLA Modules:
  0.0 168.0 jit_solution(11363644664755681750)
XLA Ops:
  5.0 10.0 %all-to-all-start = ((bf16[16,4,1536]{2,1,0:T(4,128)(2,1)}), bf16[16,4,1536]{2,1,0:T(4,128)(2,1)S(1)}, u32[]{:S(2)}, u32[]{:S(2)}) async-start(bf16[16,4,1536]{2,1,0:T(4,128)(2,1)} %bitcast.3), calls=%async_computation | async-start | bytes 393216 | tf_op jit(solution)/shard_map/all_to_all | solution.py:448
  16.3 2.9 %shard_map.171 = (bf16[512,1024]{1,0:T(8,128)(2,1)S(1)}, bf16[1024,512]{1,0:T(8,128)(2,1)}, bf16[8,1024]{1,0:T(8,128)(2,1)S(1)}, f32[8,1024]{1,0:T(8,128)S(1)}) custom-call(s32[4]{0:T(128)S(1)} %bitcast.50, bf16[512,1024]{1,0:T(8,128)(2,1)} %bitcast.39, f32[1,1024]{1,0:T(1,128)S(1)} %bitcast.44), custom_call_target="tpu_custom_call" | custom-call | flops 10000000 | bytes 3198976 | tf_op jit(solution)/shard_map/pallas_call | solution.py:49
  20.2 5.1 %all-to-all-done = bf16[16,4,1536]{2,1,0:T(4,128)(2,1)S(1)} async-done(((bf16[16,4,1536]{2,1,0:T(4,128)(2,1)}), bf16[16,4,1536]{2,1,0:T(4,128)(2,1)S(1)}, u32[]{:S(2)}, u32[]{:S(2)}) %all-to-all-start) | async-done | bytes 196640 | tf_op jit(solution)/shard_map/all_to_all | solution.py:448
  26.2 4.2 %all-to-all-start.1 = ((bf16[4,64,768]{2,1,0:T(8,128)(2,1)}), bf16[4,64,768]{2,1,0:T(8,128)(2,1)S(1)}, u32[]{:S(2)}, u32[]{:S(2)}) async-start(bf16[4,64,768]{2,1,0:T(8,128)(2,1)} %broadcast_in_dim.54), calls=%async_computation.1 | async-start | bytes 786432 | tf_op jit(solution)/shard_map/all_to_all | solution.py:384
  31.6 2.5 %collective-permute-start.1 = (bf16[64,768]{1,0:T(8,128)(2,1)S(1)}, bf16[64,768]{1,0:T(8,128)(2,1)S(1)}, u32[]{:S(2)}, u32[]{:S(2)}) collective-permute-start(bf16[64,768]{1,0:T(8,128)(2,1)S(1)} %get-tuple-element.122.refs_0_), channel_id=1, source_target_pairs={{0,4},{2,6},{4,0},{6,2},{1,5},{3,7},{5,1},{7,3},{8,12},{10,14},{12... | collective-permute-start | bytes 294920 | tf_op jit(solution)/shard_map/ppermute | solution.py:391
  40.6 4.5 %all-to-all-start.2 = ((bf16[4,256,768]{2,1,0:T(8,128)(2,1)}), bf16[4,256,768]{2,1,0:T(8,128)(2,1)}, u32[]{:S(2)}, u32[]{:S(2)}) async-start(bf16[4,256,768]{2,1,0:T(8,128)(2,1)} %broadcast_in_dim.56), calls=%async_computation.2 | async-start | bytes 3145728 | tf_op jit(solution)/shard_map/all_to_all | solution.py:384
  45.3 3.3 %collective-permute-start.6 = (bf16[256,768]{1,0:T(8,128)(2,1)S(1)}, bf16[256,768]{1,0:T(8,128)(2,1)S(1)}, u32[]{:S(2)}, u32[]{:S(2)}) collective-permute-start(bf16[256,768]{1,0:T(8,128)(2,1)S(1)} %bitcast.34), channel_id=1, source_target_pairs={{0,4},{2,6},{4,0},{6,2},{1,5},{3,7},{5,1},{7,3},{8,12},{10,14},{12... | collective-permute-start | bytes 1179656 | tf_op jit(solution)/shard_map/ppermute | solution.py:391
  49.1 6.2 %collective-permute-done.5.refs_1_.refs_2_ = bf16[256,768]{1,0:T(8,128)(2,1)S(1)} collective-permute-done((bf16[256,768]{1,0:T(8,128)(2,1)S(1)}, bf16[256,768]{1,0:T(8,128)(2,1)S(1)}, u32[]{:S(2)}, u32[]{:S(2)}) %collective-permute-start.5) | collective-permute-done | bytes 393248 | tf_op jit(solution)/shard_map/ppermute | solution.py:391
  55.3 9.2 %collective-permute-done.6.refs_2_.refs_3_ = bf16[256,768]{1,0:T(8,128)(2,1)S(1)} collective-permute-done((bf16[256,768]{1,0:T(8,128)(2,1)S(1)}, bf16[256,768]{1,0:T(8,128)(2,1)S(1)}, u32[]{:S(2)}, u32[]{:S(2)}) %collective-permute-start.6) | collective-permute-done | bytes 393248 | tf_op jit(solution)/shard_map/ppermute | solution.py:391
  65.4 7.3 %shard_map.173 = (f32[1024,256]{1,0:T(8,128)}, bf16[1024,256]{1,0:T(8,128)(2,1)}, bf16[1024,256]{1,0:T(8,128)(2,1)}, f32[8,512]{1,0:T(8,128)S(1)}, bf16[8,512]{1...) custom-call(s32[2]{0:T(128)S(1)} %pad_add_fusion.at_ref, s32[8]{0:T(128)S(1)} %convert_reduce_fusion.len_ref, ...), custom_call_target="tpu_custom_call" | custom-call | flops 1100000000 | bytes 7553024 | tf_op jit(solution)/shard_map/pallas_call | solution.py:49
  74.5 2.7 %shard_map.174 = (f32[8,1024]{1,0:T(8,128)S(1)}, bf16[1024,512]{1,0:T(8,128)(2,1)}) custom-call(s32[2]{0:T(128)S(1)} %pad_add_fusion.at_ref, bf16[8,512]{1,0:T(8,128)(2,1)S(1)} %get-tuple-element.77.ctx_ref, bf16[1024,768]{1,0:T(8,128)(2,1)} %bitcast.13.kv_ref.kvo_ref.refs_5_, bf16[256,768]{1,0:T(8,128)(2,1)S(1)} %bitcast.37, ...), custom_call_target="tpu_custom_call" | custom-call | flops 10000000 | bytes 4235264 | tf_op jit(solution)/shard_map/pallas_call | solution.py:49
  79.8 8.2 %all-to-all-start.3 = ((f32[256,1,128]{2,1,0:T(1,128)}), f32[256,1,128]{2,1,0:T(1,128)S(1)}, u32[]{:S(2)}, u32[]{:S(2)}) async-start(f32[256,1,128]{2,1,0:T(1,128)} %broadcast_in_dim.60), calls=%async_computation.3 | async-start | bytes 262144 | tf_op jit(solution)/shard_map/all_to_all | solution.py:384
  88.0 7.9 %shard_map.176 = (f32[1024,512]{1,0:T(8,128)}, f32[8,512]{1,0:T(8,128)S(1)}, f32[8,1024]{1,0:T(8,128)S(1)}, f32[8,1024]{1,0:T(8,128)S(1)}, bf16[512,1024]{1,0:T(8,128)(2,1)}) custom-call(s32[2]{0:T(128)S(1)} %pad_add_fusion.at_ref, s32[8]{0:T(128)S(1)} %convert_reduce_fusion.len_ref, bf16[1024,256]{1,0:T(8,128)(2,1)} %get-tuple-element.82.krot_ref, ...), custom_call_target="tpu_custom_call" | custom-call | flops 200000000 | bytes 9752576 | tf_op jit(solution)/shard_map/pallas_call | solution.py:49
  96.9 3.9 %all-to-all-done.3 = f32[256,1,128]{2,1,0:T(1,128)S(1)} async-done(((f32[256,1,128]{2,1,0:T(1,128)}), f32[256,1,128]{2,1,0:T(1,128)S(1)}, u32[]{:S(2)}, u32[]{:S(2)}) %all-to-all-start.3) | async-done | bytes 131104 | tf_op jit(solution)/shard_map/all_to_all | solution.py:384
  100.8 6.3 %shard_map.177 = (bf16[4,256,768]{2,1,0:T(8,128)(2,1)}, bf16[256,768]{1,0:T(8,128)(2,1)S(1)}, bf16[256,768]{1,0:T(8,128)(2,1)}, bf16[256,768]{1,0:T(8,128)(2,1)S...) custom-call(s32[2]{0:T(128)S(1)} %pad_add_fusion.at_ref, ...), custom_call_target="tpu_custom_call" | custom-call | flops 1100000000 | bytes 8671236 | tf_op jit(solution)/shard_map/pallas_call | solution.py:49
  107.1 4.4 %all-to-all-start.4 = ((bf16[4,256,768]{2,1,0:T(8,128)(2,1)}), bf16[4,256,768]{2,1,0:T(8,128)(2,1)}, u32[]{:S(2)}, u32[]{:S(2)}) async-start(bf16[4,256,768]{2,1,0:T(8,128)(2,1)} %get-tuple-element.96), calls=%async_computation.4 | async-start | bytes 3145728 | tf_op jit(solution)/shard_map/all_to_all | solution.py:542
  122.2 5.5 %shard_map.178 = bf16[512,1024]{1,0:T(8,128)(2,1)} custom-call(s32[8]{0:T(128)S(1)} %convert_reduce_fusion.len_ref, bf16[512,1024]{1,0:T(8,128)(2,1)S(1)} %bitcast.40, f32[1,1024]{1,0:T(1,128)S(1)} %bitcast.45, bf16[1024,512]{1,0:T(8,128)(2,1)} %get-tuple-element.101.skv_ref, f32[8,128]{1,0:T(8,128)S(1)} %get-tuple-element.102.g_ref, ...), custom_call_target="tpu_custom_call" | custom-call | flops 600000000 | bytes 5873664 | tf_op jit(solution)/shard_map/pallas_call | solution.py:49
  127.7 4.8 %collective-permute-done.11.refs_2_ = bf16[256,768]{1,0:T(8,128)(2,1)S(1)} collective-permute-done((bf16[256,768]{1,0:T(8,128)(2,1)S(1)}, bf16[256,768]{1,0:T(8,128)(2,1)S(1)}, u32[]{:S(2)}, u32[]{:S(2)}) %collective-permute-start.11) | collective-permute-done | bytes 393248 | tf_op jit(solution)/shard_map/ppermute | solution.py:397
  132.8 2.9 %shard_map.179 = (bf16[64,768]{1,0:T(8,128)(2,1)S(1)}, bf16[64,768]{1,0:T(8,128)(2,1)S(1)}, bf16[64,768]{1,0:T(8,128)(2,1)S(1)}, bf16[64,768]{1,0:T(8,128)(2,1)S(1)}, bf16[256,768]{1,0:T(8,128)(2,1)}) custom-call(s32[2]{0:T(128)S(1)} %pad_add_fusion.at_ref, bf16[4,256,768]{2,1,0:T(8,128)(2,1)} %all-to-all-done.4.got_a_ref, ...), custom_call_target="tpu_custom_call" | custom-call | bytes 3932160 | tf_op jit(solution)/shard_map/pallas_call | solution.py:49
  135.7 3.0 %collective-permute-start.17 = (bf16[64,768]{1,0:T(8,128)(2,1)S(1)}, bf16[64,768]{1,0:T(8,128)(2,1)S(1)}, u32[]{:S(2)}, u32[]{:S(2)}) collective-permute-start(bf16[64,768]{1,0:T(8,128)(2,1)S(1)} %get-tuple-element.115), channel_id=1, source_target_pairs={{0,6},{2,0},{4,2},{6,4},{1,7},{3,1},{5,3},{7,5},{8,14},{10,8},{12,... | collective-permute-start | bytes 294920 | tf_op jit(solution)/shard_map/ppermute | solution.py:397
  139.3 4.4 %all-to-all-start.5 = ((bf16[4,64,768]{2,1,0:T(8,128)(2,1)}), bf16[4,64,768]{2,1,0:T(8,128)(2,1)S(1)}, u32[]{:S(2)}, u32[]{:S(2)}) async-start(bf16[4,64,768]{2,1,0:T(8,128)(2,1)} %bitcast.22), calls=%async_computation.5 | async-start | bytes 786432 | tf_op jit(solution)/shard_map/all_to_all | solution.py:560
  143.8 2.7 %collective-permute-done.15 = bf16[64,768]{1,0:T(8,128)(2,1)S(1)} collective-permute-done((bf16[64,768]{1,0:T(8,128)(2,1)S(1)}, bf16[64,768]{1,0:T(8,128)(2,1)S(1)}, u32[]{:S(2)}, u32[]{:S(2)}) %collective-permute-start.15) | collective-permute-done | bytes 98336 | tf_op jit(solution)/shard_map/ppermute | solution.py:397
  146.5 3.6 %all-to-all-done.5 = bf16[4,64,768]{2,1,0:T(8,128)(2,1)S(1)} async-done(((bf16[4,64,768]{2,1,0:T(8,128)(2,1)}), bf16[4,64,768]{2,1,0:T(8,128)(2,1)S(1)}, u32[]{:S(2)}, u32[]{:S(2)}) %all-to-all-start.5) | async-done | bytes 393248 | tf_op jit(solution)/shard_map/all_to_all | solution.py:560
  150.3 17.1 %all_to_all.35 = bf16[16,4,1536]{2,1,0:T(4,128)(2,1)S(1)} all-to-all(bf16[16,4,1536]{2,1,0:T(4,128)(2,1)S(1)} %reshape.101), channel_id=1, replica_groups=mesh['pb'=4,'z'=8,'x'=4,'c'=2] {'z','c'}, dimensions={0} | all-to-all | bytes 393216 | tf_op jit(solution)/shard_map/all_to_all | solution.py:569
  (99 shorter events, 34.8 us)
Async XLA Ops:
  5.0 20.3 %all-to-all-start = ((bf16[16,4,1536]{2,1,0:T(4,128)(2,1)}), bf16[16,4,1536]{2,1,0:T(4,128)(2,1)S(1)}, u32[]{:S(2)}, u32[]{:S(2)}) async-start(bf16[16,4,1536]{2,1,0:T(4,128)(2,1)} %bitcast.3), calls=%async_computation | async-start | bytes 393216 | tf_op jit(solution)/shard_map/all_to_all | solution.py:448
  25.3 13.8 %collective-permute-start.3 = (bf16[512,1024]{1,0:T(8,128)(2,1)S(1)}, bf16[512,1024]{1,0:T(8,128)(2,1)S(1)}, u32[]{:S(2)}, u32[]{:S(2)}) collective-permute-start(bf16[512,1024]{1,0:T(8,128)(2,1)S(1)} %get-tuple-element.70.normed_ref), channel_id=1, source_target_pairs={{0,1},{1,0},{2,3},{3,2},{4,5},{5,4},{6,7},{7,6},{8,9},{9,8},{10,11... | collective-permute-start | bytes 3145736 | tf_op jit(solution)/shard_map/ppermute | solution.py:410
  26.2 12.9 %all-to-all-start.1 = ((bf16[4,64,768]{2,1,0:T(8,128)(2,1)}), bf16[4,64,768]{2,1,0:T(8,128)(2,1)S(1)}, u32[]{:S(2)}, u32[]{:S(2)}) async-start(bf16[4,64,768]{2,1,0:T(8,128)(2,1)} %broadcast_in_dim.54), calls=%async_computation.1 | async-start | bytes 786432 | tf_op jit(solution)/shard_map/all_to_all | solution.py:384
  30.4 6.5 %collective-permute-start = (bf16[64,768]{1,0:T(8,128)(2,1)S(1)}, bf16[64,768]{1,0:T(8,128)(2,1)S(1)}, u32[]{:S(2)}, u32[]{:S(2)}) collective-permute-start(bf16[64,768]{1,0:T(8,128)(2,1)S(1)} %get-tuple-element.122.refs_0_), channel_id=1, source_target_pairs={{0,2},{2,4},{4,6},{6,0},{1,3},{3,5},{5,7},{7,1},{8,10},{10,12},{12... | collective-permute-start | bytes 294920 | tf_op jit(solution)/shard_map/ppermute | solution.py:391
  31.6 6.6 %collective-permute-start.1 = (bf16[64,768]{1,0:T(8,128)(2,1)S(1)}, bf16[64,768]{1,0:T(8,128)(2,1)S(1)}, u32[]{:S(2)}, u32[]{:S(2)}) collective-permute-start(bf16[64,768]{1,0:T(8,128)(2,1)S(1)} %get-tuple-element.122.refs_0_), channel_id=1, source_target_pairs={{0,4},{2,6},{4,0},{6,2},{1,5},{3,7},{5,1},{7,3},{8,12},{10,14},{12... | collective-permute-start | bytes 294920 | tf_op jit(solution)/shard_map/ppermute | solution.py:391
  34.1 4.5 %collective-permute-start.2 = (bf16[64,768]{1,0:T(8,128)(2,1)S(1)}, bf16[64,768]{1,0:T(8,128)(2,1)S(1)}, u32[]{:S(2)}, u32[]{:S(2)}) collective-permute-start(bf16[64,768]{1,0:T(8,128)(2,1)S(1)} %get-tuple-element.122.refs_0_), channel_id=1, source_target_pairs={{0,6},{2,0},{4,2},{6,4},{1,7},{3,1},{5,3},{7,5},{8,14},{10,8},{12,... | collective-permute-start | bytes 294920 | tf_op jit(solution)/shard_map/ppermute | solution.py:391
  35.2 3.9 %collective-permute-start.4 = (f32[4,2304]{1,0:T(4,128)S(1)}, f32[4,2304]{1,0:T(4,128)S(1)}, u32[]{:S(2)}, u32[]{:S(2)}) collective-permute-start(f32[4,2304]{1,0:T(4,128)S(1)} %pad_maximum_fusion.1), channel_id=1, source_target_pairs={{0,1},{1,0},{2,3},{3,2},{4,5},{5,4},{6,7},{7,6},{8,9},{9,8},{10,11... | collective-permute-start | bytes 110600 | tf_op jit(solution)/shard_map/ppermute | solution.py:410
  40.6 24.8 %all-to-all-start.2 = ((bf16[4,256,768]{2,1,0:T(8,128)(2,1)}), bf16[4,256,768]{2,1,0:T(8,128)(2,1)}, u32[]{:S(2)}, u32[]{:S(2)}) async-start(bf16[4,256,768]{2,1,0:T(8,128)(2,1)} %broadcast_in_dim.56), calls=%async_computation.2 | async-start | bytes 3145728 | tf_op jit(solution)/shard_map/all_to_all | solution.py:384
  45.2 10.1 %collective-permute-start.5 = (bf16[256,768]{1,0:T(8,128)(2,1)S(1)}, bf16[256,768]{1,0:T(8,128)(2,1)S(1)}, u32[]{:S(2)}, u32[]{:S(2)}) collective-permute-start(bf16[256,768]{1,0:T(8,128)(2,1)S(1)} %bitcast.33), channel_id=1, source_target_pairs={{0,2},{2,4},{4,6},{6,0},{1,3},{3,5},{5,7},{7,1},{8,10},{10,12},{12... | collective-permute-start | bytes 1179656 | tf_op jit(solution)/shard_map/ppermute | solution.py:391
  45.3 19.2 %collective-permute-start.6 = (bf16[256,768]{1,0:T(8,128)(2,1)S(1)}, bf16[256,768]{1,0:T(8,128)(2,1)S(1)}, u32[]{:S(2)}, u32[]{:S(2)}) collective-permute-start(bf16[256,768]{1,0:T(8,128)(2,1)S(1)} %bitcast.34), channel_id=1, source_target_pairs={{0,4},{2,6},{4,0},{6,2},{1,5},{3,7},{5,1},{7,3},{8,12},{10,14},{12... | collective-permute-start | bytes 1179656 | tf_op jit(solution)/shard_map/ppermute | solution.py:391
  48.7 16.7 %collective-permute-start.7 = (bf16[256,768]{1,0:T(8,128)(2,1)S(1)}, bf16[256,768]{1,0:T(8,128)(2,1)S(1)}, u32[]{:S(2)}, u32[]{:S(2)}) collective-permute-start(bf16[256,768]{1,0:T(8,128)(2,1)S(1)} %bitcast.35), channel_id=1, source_target_pairs={{0,6},{2,0},{4,2},{6,4},{1,7},{3,1},{5,3},{7,5},{8,14},{10,8},{12,... | collective-permute-start | bytes 1179656 | tf_op jit(solution)/shard_map/ppermute | solution.py:391
  72.7 28.2 %collective-permute-start.9 = (bf16[1024,512]{1,0:T(8,128)(2,1)S(1)}, bf16[1024,512]{1,0:T(8,128)(2,1)}, u32[]{:S(2)}, u32[]{:S(2)}) collective-permute-start(bf16[1024,512]{1,0:T(8,128)(2,1)S(1)} %copy-done.10), channel_id=1, source_target_pairs={{0,1},{1,0},{2,3},{3,2},{4,5},{5,4},{6,7},{7,6},{8,9},{9,8},{10,11... | collective-permute-start | bytes 3145736 | tf_op jit(solution)/shard_map/ppermute | solution.py:410
  77.1 1.2 collective-permute-start.8
  79.8 21.0 %all-to-all-start.3 = ((f32[256,1,128]{2,1,0:T(1,128)}), f32[256,1,128]{2,1,0:T(1,128)S(1)}, u32[]{:S(2)}, u32[]{:S(2)}) async-start(f32[256,1,128]{2,1,0:T(1,128)} %broadcast_in_dim.60), calls=%async_computation.3 | async-start | bytes 262144 | tf_op jit(solution)/shard_map/all_to_all | solution.py:384
  107.1 25.7 %all-to-all-start.4 = ((bf16[4,256,768]{2,1,0:T(8,128)(2,1)}), bf16[4,256,768]{2,1,0:T(8,128)(2,1)}, u32[]{:S(2)}, u32[]{:S(2)}) async-start(bf16[4,256,768]{2,1,0:T(8,128)(2,1)} %get-tuple-element.96), calls=%async_computation.4 | async-start | bytes 3145728 | tf_op jit(solution)/shard_map/all_to_all | solution.py:542
  111.5 10.7 %collective-permute-start.14 = (bf16[512,1024]{1,0:T(8,128)(2,1)}, bf16[512,1024]{1,0:T(8,128)(2,1)}, u32[]{:S(2)}, u32[]{:S(2)}) collective-permute-start(bf16[512,1024]{1,0:T(8,128)(2,1)} %get-tuple-element.105), channel_id=1, source_target_pairs={{0,1},{1,0},{2,3},{3,2},{4,5},{5,4},{6,7},{7,6},{8,9},{9,8},{10,11... | collective-permute-start | bytes 3145736 | tf_op jit(solution)/shard_map/ppermute | solution.py:410
  112.1 15.6 %collective-permute-start.10 = (bf16[256,768]{1,0:T(8,128)(2,1)}, bf16[256,768]{1,0:T(8,128)(2,1)S(1)}, u32[]{:S(2)}, u32[]{:S(2)}) collective-permute-start(bf16[256,768]{1,0:T(8,128)(2,1)} %get-tuple-element.98), channel_id=1, source_target_pairs={{0,2},{2,4},{4,6},{6,0},{1,3},{3,5},{5,7},{7,1},{8,10},{10,12},{12... | collective-permute-start | bytes 1179656 | tf_op jit(solution)/shard_map/ppermute | solution.py:397
  112.5 20.1 %collective-permute-start.11 = (bf16[256,768]{1,0:T(8,128)(2,1)S(1)}, bf16[256,768]{1,0:T(8,128)(2,1)S(1)}, u32[]{:S(2)}, u32[]{:S(2)}) collective-permute-start(bf16[256,768]{1,0:T(8,128)(2,1)S(1)} %get-tuple-element.99), channel_id=1, source_target_pairs={{0,4},{2,6},{4,0},{6,2},{1,5},{3,7},{5,1},{7,3},{8,12},{10,14},{12... | collective-permute-start | bytes 1179656 | tf_op jit(solution)/shard_map/ppermute | solution.py:397
  114.5 18.3 %collective-permute-start.12 = (bf16[256,768]{1,0:T(8,128)(2,1)S(1)}, bf16[256,768]{1,0:T(8,128)(2,1)}, u32[]{:S(2)}, u32[]{:S(2)}) collective-permute-start(bf16[256,768]{1,0:T(8,128)(2,1)S(1)} %get-tuple-element.100), channel_id=1, source_target_pairs={{0,6},{2,0},{4,2},{6,4},{1,7},{3,1},{5,3},{7,5},{8,14},{10,8},{12,... | collective-permute-start | bytes 1179656 | tf_op jit(solution)/shard_map/ppermute | solution.py:397
  120.4 1.9 %collective-permute-start.13 = (f32[8,1024]{1,0:T(8,128)S(1)}, f32[8,1024]{1,0:T(8,128)S(1)}, u32[]{:S(2)}, u32[]{:S(2)}) collective-permute-start(f32[8,1024]{1,0:T(8,128)S(1)} %reshape.98.last_ref), channel_id=1, source_target_pairs={{0,1},{1,0},{2,3},{3,2},{4,5},{5,4},{6,7},{7,6},{8,9},{9,8},{10,11... | collective-permute-start | bytes 98312 | tf_op jit(solution)/shard_map/ppermute | solution.py:410
  135.7 8.0 %collective-permute-start.17 = (bf16[64,768]{1,0:T(8,128)(2,1)S(1)}, bf16[64,768]{1,0:T(8,128)(2,1)S(1)}, u32[]{:S(2)}, u32[]{:S(2)}) collective-permute-start(bf16[64,768]{1,0:T(8,128)(2,1)S(1)} %get-tuple-element.115), channel_id=1, source_target_pairs={{0,6},{2,0},{4,2},{6,4},{1,7},{3,1},{5,3},{7,5},{8,14},{10,8},{12,... | collective-permute-start | bytes 294920 | tf_op jit(solution)/shard_map/ppermute | solution.py:397
  138.7 5.1 %collective-permute-start.16 = (bf16[64,768]{1,0:T(8,128)(2,1)S(1)}, bf16[64,768]{1,0:T(8,128)(2,1)S(1)}, u32[]{:S(2)}, u32[]{:S(2)}) collective-permute-start(bf16[64,768]{1,0:T(8,128)(2,1)S(1)} %get-tuple-element.114), channel_id=1, source_target_pairs={{0,4},{2,6},{4,0},{6,2},{1,5},{3,7},{5,1},{7,3},{8,12},{10,14},{12... | collective-permute-start | bytes 294920 | tf_op jit(solution)/shard_map/ppermute | solution.py:397
  138.8 7.6 %collective-permute-start.15 = (bf16[64,768]{1,0:T(8,128)(2,1)S(1)}, bf16[64,768]{1,0:T(8,128)(2,1)S(1)}, u32[]{:S(2)}, u32[]{:S(2)}) collective-permute-start(bf16[64,768]{1,0:T(8,128)(2,1)S(1)} %get-tuple-element.113), channel_id=1, source_target_pairs={{0,2},{2,4},{4,6},{6,0},{1,3},{3,5},{5,7},{7,1},{8,10},{10,12},{12... | collective-permute-start | bytes 294920 | tf_op jit(solution)/shard_map/ppermute | solution.py:397
  139.3 10.8 %all-to-all-start.5 = ((bf16[4,64,768]{2,1,0:T(8,128)(2,1)}), bf16[4,64,768]{2,1,0:T(8,128)(2,1)S(1)}, u32[]{:S(2)}, u32[]{:S(2)}) async-start(bf16[4,64,768]{2,1,0:T(8,128)(2,1)} %bitcast.22), calls=%async_computation.5 | async-start | bytes 786432 | tf_op jit(solution)/shard_map/all_to_all | solution.py:560
  (13 other events, 134.0 us)

commit v3 on v2

--- a/solution.py
+++ b/solution.py
@@ -98,6 +98,18 @@
         jnp.concatenate([t[pl.ds(len_ref[p] - 1, 1), :] for p in range(BOTH)], axis=0)
         for t in (cos_ref, sin_ref)
     ]
+
+
+def pack_body(k_ref, v_ref, q_ref, o_ref, out_ref):
+    for h in range(2):
+        wide, tall = slice(h * 256, h * 256 + 256), h * 512
+        out_ref[0, h, :, 0:256] = k_ref[:, wide]
+        out_ref[0, h, :, 256:512] = v_ref[:, wide]
+        out_ref[0, h, :, 512:768] = o_ref[:, tall : tall + 256]
+        out_ref[0, h, :, 768:1280] = q_ref[:, tall : tall + 512]
+        out_ref[0, h, :, 1280:1536] = o_ref[:, tall + 256 : tall + 512]
+    for z in range(1, 8):
+        out_ref[z] = out_ref[0]
 
 
 def prep_body(len_ref, h_ref, gain_ref, normed_ref, turned_ref, nlast_ref, xlast_ref):
@@ -121,17 +133,22 @@
 
 
 def arrange_body(at_ref, *refs):
-    a_refs, out_ref = refs[0:4], refs[4]
+    a_refs, out_ref, slab_scr = refs[0:4], refs[4], refs[5]
     x = at_ref[1]
     for d in range(4):
-        out_ref[:, pl.ds(lax.rem(x - d + 4, 4), 1)] = a_refs[d][...].reshape(8, 1, 8, 768)
+        slab_scr[:, pl.ds(lax.rem(x - d + 4, 4), 1)] = a_refs[d][...].reshape(8, 1, 8, 768)
+    slab = slab_scr[...].reshape(256, 768)
+    for y in range(4):
+        out_ref[y] = slab
 
 
 def attend_body(
     at_ref, len_ref, normed_ref, other_ref, nlast_ref, cos_ref, sin_ref, kv_ref, *refs
 ):
+    out_ref, o_ref, turn_scr = refs[11], refs[12], refs[15]
     q_refs = refs[0:4]
-    kproj_ref, krot_ref, vcast_ref, qproj_ref, qrot_ref, attn_ref, ctx_ref, qr_scr, ctx_scr = refs[4:]
+    kproj_ref, krot_ref, vcast_ref, qproj_ref, qrot_ref, attn_ref, ctx_ref = refs[4:11]
+    qr_scr, ctx_scr = refs[13:15]
     x = at_ref[1]
     mask, even = block_mask()
     lane = lax.broadcasted_iota(jnp.int32, (8, SEQ), 1)
@@ -171,15 +188,9 @@
         c = dot(w.astype(BF16), vcast_ref[rows, :])
         ctx_scr[p : p + 1, :] = from_blocks(c, mask, even)
     ctx_ref[...] = ctx_scr[...].astype(BF16)
-
-
-def attended_body(at_ref, ctx_ref, kvo_ref, *refs):
-    qo_refs, out_ref, o_ref, turn_scr = refs[0:4], refs[4], refs[5], refs[6]
     for d in range(4):
-        turn_scr[:, pl.ds(lax.rem(at_ref[1] - d + 4, 4), 1)] = qo_refs[d][:, 512:768].reshape(
-            32, 1, 8, 256
-        )
-    o_ref[:, 0:256] = kvo_ref[:, 512:768]
+        turn_scr[:, pl.ds(lax.rem(x - d + 4, 4), 1)] = q_refs[d][:, 512:768].reshape(32, 1, 8, 256)
+    o_ref[:, 0:256] = kv_ref[:, 512:768]
     o_ref[:, 256:512] = turn_scr[...].reshape(1024, 256)
     out_ref[...] = dot(ctx_ref[...], o_ref[...], LAST)
 
@@ -201,8 +212,8 @@
     es = jnp.exp(s)
     et = jnp.exp(scaled)
     v = jnp.where(lane == 0, es, jnp.where(lane == 1, et, et * (scaled - s)))
-    v = jnp.where((row < PAIRS) & (lane < 3), v, 0.0)
-    tot_ref[...] = jnp.broadcast_to(jnp.sum(v, axis=0, keepdims=True), (8, HW))
+    v = jnp.where(lane < 3, v + pltpu.roll(v, PAIRS, 0), 0.0)
+    tot_ref[...] = jnp.broadcast_to(jnp.sum(v[0:PAIRS], axis=0, keepdims=True)[None], (32, 1, HW))
 
 
 def unit_back_body(
@@ -288,21 +299,17 @@
 ):
     out_a, outs_b, loss_ref, skv_ref, g_ref, sr_ref = refs[0], refs[1:5], *refs[5:9]
     srow_scr, sturn_scr, b_scr, sq_scr = refs[9:]
-    pb, x = at_ref[0], at_ref[1]
+    x = at_ref[1]
     lane = lax.broadcasted_iota(jnp.int32, (1, HW), 1)
 
     def pick(v, i):
         return jnp.sum(jnp.where(lane == i, v, 0.0), axis=-1, keepdims=True)
 
-    loss = jnp.zeros((1, 1), F32)
-    mine = jnp.zeros((1, HW), F32)
-    for q in range(4):
-        t = jnp.sum(tot_ref[q * 64 : (q + 1) * 64, :], axis=0, keepdims=True)
-        ts, tt, cr = pick(t, 0), pick(t, 1), pick(t, 2)
-        loss = loss + (cr / tt - jnp.log(tt) + jnp.log(ts))
-        mine = mine + jnp.where(pb == q, t, 0.0)
-    loss_ref[...] = loss
-    ts, tt = pick(mine, 0), pick(mine, 1)
+    t = tot_ref[0]
+    for i in range(1, 32):
+        t = t + tot_ref[i]
+    ts, tt, cr = pick(t, 0), pick(t, 1), pick(t, 2)
+    loss_ref[...] = jnp.broadcast_to(cr / tt - jnp.log(tt) + jnp.log(ts), (8, HW))
     row = lax.broadcasted_iota(jnp.int32, (8, HW), 0)
     g = GRAD_SCALE * (jnp.exp(score_ref[...]) / ts - jnp.exp(teach_ref[...] / 2.0) / tt)
     gcol = g[:, 0:1]
@@ -336,7 +343,7 @@
         outs_b[d][...] = b_scr[d]
 
 
-def middle_body(at_ref, got_a_ref, *refs):
+def middle_body(at_ref, loss_ref, got_a_ref, *refs):
     b_refs, out_a, out_b, a_scr = refs[0:4], refs[4:8], refs[8], refs[9]
     x = at_ref[1]
     total_a = got_a_ref[0].astype(F32)
@@ -344,7 +351,16 @@
     for d in range(1, 4):
         total_a = total_a + got_a_ref[d].astype(F32)
         total_b = total_b + b_refs[d][...].astype(F32)
-    out_b[...] = total_b.astype(BF16)
+    out_b[:, 0:64, :] = total_b.reshape(4, 64, 768).astype(BF16)
+    rest = jnp.broadcast_to(loss_ref[0:1, 0:1], (16, 768))
+    lane = lax.broadcasted_iota(jnp.int32, (16, 768), 1)
+    parts = jnp.zeros((16, 768), F32)
+    for i in range(3):
+        part = rest.astype(BF16).astype(F32)
+        parts = jnp.where(lane == i, part, parts)
+        rest = rest - part
+    for y in range(4):
+        out_b[y, 64:80, :] = parts.astype(BF16)
     a_scr[...] = total_a.reshape(8, 4, 8, 768)
     for d in range(4):
         out_a[d][...] = a_scr[:, pl.ds(lax.rem(x + d, 4), 1)].reshape(64, 768).astype(BF16)
@@ -430,21 +446,13 @@
     sv = score_vector[None]
     cos_np, sin_np = rope_consts()
     cos, sin = jnp.asarray(cos_np), jnp.asarray(sin_np)
-    turned_out = out_weight.T
-    halves = [
-        jnp.concatenate(
-            [
-                key_matrix[:, h * 256 : h * 256 + 256],
-                value_matrix[:, h * 256 : h * 256 + 256],
-                turned_out[:, h * 512 : h * 512 + 256],
-                query_weight[:, h * 512 : h * 512 + 512],
-                turned_out[:, h * 512 + 256 : h * 512 + 512],
-            ],
-            axis=1,
-        )
-        for h in range(2)
-    ]
-    both_halves = jnp.broadcast_to(jnp.stack(halves)[None], (8, 2, 4, 1536)).reshape(16, 4, 1536)
+    (both_halves,) = call(
+        pack_body,
+        [],
+        [key_matrix, value_matrix, query_weight, out_weight.T],
+        [((8, 2, 4, 1536), BF16)],
+    )
+    both_halves = both_halves.reshape(16, 4, 1536)
     column = lax.all_to_all(both_halves, ("z", "c"), 0, 0, tiled=True).reshape(64, 1536)
     normed, turned, nlast, xlast = call(
         prep_body,
@@ -469,17 +477,17 @@
     got = swap(pack)
     slab_b = everyone(column[:, 768:1536], "pb", 4).reshape(256, 768)
     ring_a = from_ring(column[:, 0:768], "x")
-    (slab_a,) = call(arrange_body, [at], ring_a, [((8, 4, 8, 768), BF16)])
+    (slab_a,) = call(arrange_body, [at], ring_a, [((4, 256, 768), BF16)], [((8, 4, 8, 768), BF16)])
     slab_a, slab_b, other, got = lax.optimization_barrier((slab_a, slab_b, other, got))
     packed = jnp.concatenate([pack, got], axis=0)
     xlast = packed[:, 0:1024]
     nlast = packed[:, 1024:2048].astype(BF16)
     lens_both = packed[:, 2048].astype(jnp.int32)
     teach = packed[:, 2048 + HW :]
-    kvo = everyone(slab_a.reshape(256, 768), "pb", 4).reshape(1024, 768)
+    kvo = lax.all_to_all(slab_a, "pb", 0, 0, tiled=True).reshape(1024, 768)
     qo = from_ring(slab_b, "x")
 
-    kproj, krot, vcast, qproj, qrot, attn, ctx = call(
+    kproj, krot, vcast, qproj, qrot, attn, ctx, attended, oa = call(
         attend_body,
         [at, lens_both],
         [normed, other, nlast, cos, sin, kvo, *qo],
@@ -491,29 +499,23 @@
             ((8, 512), BF16),
             ((64, SEQ), F32),
             ((8, 512), BF16),
+            ((8, D), F32),
+            ((D, 512), BF16),
         ],
-        [((8, 512), F32), ((8, 512), F32)],
+        [((8, 512), F32), ((8, 512), F32), ((32, 4, 8, 256), BF16)],
         flops=1_100_000_000,
     )
     ctx, turned_late = lax.optimization_barrier((ctx, turned))
     turned_other = swap(turned_late)
-    attended, oa = call(
-        attended_body,
-        [at],
-        [ctx, kvo, *qo],
-        [((8, D), F32), ((D, 512), BF16)],
-        [((32, 4, 8, 256), BF16)],
-        flops=10_000_000,
-    )
     unit, oscale, score, tot, line = call(
         score_body,
         [],
         [teach, attended, swap(attended), xlast, fg, sv],
-        [((8, D), F32), ((8, HW), F32), ((8, HW), F32), ((8, HW), F32), ((1, PAIRS), F32)],
+        [((8, D), F32), ((8, HW), F32), ((8, HW), F32), ((32, 1, HW), F32), ((1, PAIRS), F32)],
         flops=1_000_000,
     )
 
-    totals = everyone(tot[0:1], AXES, 256).reshape(256, HW)
+    totals = lax.all_to_all(tot, ("z", "x"), 0, 0, tiled=True)
 
     gkv, gq, gr, last, send = call(
         unit_back_body,
@@ -534,7 +536,7 @@
         [totals, score, teach, gkv, gq, gr, grturn, turned, turned_other, nlast, ctx],
         [pieces]
         + [((256, 768), BF16)] * 4
-        + [((1, 1), F32), ((ROWS * 2, 512), BF16), ((8, HW), F32), ((8, D), F32)],
+        + [((8, HW), F32), ((ROWS * 2, 512), BF16), ((8, HW), F32), ((8, D), F32)],
         [((8, D), BF16), ((8, D), BF16), pieces, ((8, 512), BF16)],
         flops=1_100_000_000,
     )
@@ -552,12 +554,15 @@
     *mid_a, mid_b = call(
         middle_body,
         [at],
-        [got_a, *got_b],
-        [((64, 768), BF16)] * 4 + [((256, 768), BF16)],
+        [loss, got_a, *got_b],
+        [((64, 768), BF16)] * 4 + [((4, 80, 768), BF16)],
         [((8, 4, 8, 768), F32)],
     )
     done_a = along_ring(mid_a, "x")
-    done_b = lax.all_to_all(mid_b.reshape(4, 64, 768), "pb", 0, 0, tiled=True)
+    done_b = lax.all_to_all(mid_b, "pb", 0, 0, tiled=True)
+    loss = jnp.sum(done_b[:, 64, 0:3].astype(F32), axis=1)
+    loss = (loss[0] + loss[1]) + (loss[2] + loss[3])
+    done_b = done_b[:, 0:64]
 
     def added(parts):
         total = parts[0].astype(F32)
@@ -576,7 +581,7 @@
 
     return (
         line,
-        loss.reshape(()),
+        loss,
         grad_hidden.reshape(hidden.shape),
         grad_query,
         grad_key,

time: 169 us -> 164 us (0.970)
  blocking collectives: 17.1 us -> 0 us
  starting transfers between devices: 56.4 us -> 62.2 us
  waiting for transfers between devices: 40.4 us -> 44.2 us
  between operations: 0.91 us -> 4.66 us
    all_to_all x1 -> x4, starting transfers between devices: 4.36 us -> 21.8 us  [the longest x1 7.62 us: shards(): lax.all_to_all(part.reshape(16, 4, 1536), ('z', 'c'), 0, 0, tiled=True)]
    all_to_all x1 -> x0, blocking collectives: 17.1 us -> none  [shards(): lax.all_to_all(part.reshape(16, 4, 1536), ('z', 'c'), 0, 0, tiled=True)]
    all_to_all x3 -> x1, starting transfers between devices: 16.9 us -> 4.18 us  [everyone(): lax.all_to_all(jnp.broadcast_to(x[None], (count, *x.shape)), axes, 0, 0,...]
    all_to_all x3 -> x1, waiting for transfers between devices: 3.88 us -> 0.01 us  [everyone(): lax.all_to_all(jnp.broadcast_to(x[None], (count, *x.shape)), axes, 0, 0,...]
    all_to_all x1 -> x4, waiting for transfers between devices: 3.62 us -> 7.02 us  [the longest x1 7.02 us: shards(): lax.all_to_all(part.reshape(16, 4, 1536), ('z', 'c'), 0, 0, tiled=True)]
    ppermute x6, waiting for transfers between devices: 7.92 us -> 11.3 us  [along_ring(): lax.ppermute(pieces[d], axis, [(i, (i + d) % 4) for i in range(4)])]
    broadcast_in_dim x4 -> x1, local copies, waits for them, and re-layouts: 2.88 us -> 0.77 us  [everyone(): jnp.broadcast_to(x[None], (count, *x.shape))]
    unnamed x30 -> x32, local copies, waits for them, and re-layouts: 4.35 us -> 5.13 us
  transfers between devices with their start and end apart: 24 -> 25, of which waited for: 14 -> 13; matrix products, arithmetic and copies ran while one was open for 5% -> 5% of each run, Pallas kernels for 12% -> 12%
where the time goes in v3:
time: 164 us; the launch traced here: 163 us
  starting transfers between devices  62.2 us (38%)
  waiting for transfers between devices  44.2 us (27%)
  Pallas kernels  37.6 us (23%)
  local copies, waits for them, and re-layouts  14.1 us (9%)
  between operations  4.66 us (3%)
    pallas_call x10, Pallas kernels, call(): pl.pallas_call(body, grid=(1,), out_shape=[jax.ShapeDtypeStruct(o, d) for...  37.6 us
    ppermute x6, waiting for transfers between devices, from_ring(): lax.ppermute(x, axis, [(i, (i + d) % 4) for i in range(4)])  17.9 us
    ppermute x6, waiting for transfers between devices, along_ring(): lax.ppermute(pieces[d], axis, [(i, (i + d) % 4) for i in range(4)])  11.3 us
    all_to_all x1, starting transfers between devices, shards(): lax.all_to_all(both_halves, ('z', 'c'), 0, 0, tiled=True).reshape(64, 1536)  9.98 us
    ppermute x6, starting transfers between devices, from_ring(): lax.ppermute(x, axis, [(i, (i + d) % 4) for i in range(4)])  8.65 us
    all_to_all x1, starting transfers between devices, shards(): lax.all_to_all(part.reshape(16, 4, 1536), ('z', 'c'), 0, 0, tiled=True)  7.62 us
    ppermute x6, starting transfers between devices, along_ring(): lax.ppermute(pieces[d], axis, [(i, (i + d) % 4) for i in range(4)])  7.58 us
    all_to_all x1, waiting for transfers between devices, shards(): lax.all_to_all(part.reshape(16, 4, 1536), ('z', 'c'), 0, 0, tiled=True)  7.02 us
  transfers between devices with their start and end apart: 25, of which 13 were waited for; matrix products, arithmetic and copies ran while one was open for 5% of the time, Pallas kernels for 12%

profile of v3, /device:TPU:1, one launch (start us, length us, event | category | flops | bytes accessed | tf_op | source)
XLA Modules:
  0.0 163.2 jit_solution(820370479184233289)
XLA Ops:
  4.1 10.0 %all-to-all-start = ((bf16[16,4,1536]{2,1,0:T(4,128)(2,1)}), bf16[16,4,1536]{2,1,0:T(4,128)(2,1)S(1)}, u32[]{:S(2)}, u32[]{:S(2)}) async-start(bf16[16,4,1536]{2,1,0:T(4,128)(2,1)} %bitcast.1), calls=%async_computation | async-start | bytes 393216 | tf_op jit(solution)/shard_map/all_to_all | solution.py:456
  15.5 2.9 %shard_map.172 = (bf16[512,1024]{1,0:T(8,128)(2,1)S(1)}, bf16[1024,512]{1,0:T(8,128)(2,1)}, bf16[8,1024]{1,0:T(8,128)(2,1)S(1)}, f32[8,1024]{1,0:T(8,128)S(1)}) custom-call(s32[4]{0:T(128)S(1)} %bitcast.41, bf16[512,1024]{1,0:T(8,128)(2,1)} %bitcast.26, f32[1,1024]{1,0:T(1,128)S(1)} %bitcast.34), custom_call_target="tpu_custom_call" | custom-call | flops 10000000 | bytes 3198976 | tf_op jit(solution)/shard_map/pallas_call | solution.py:49
  19.4 5.1 %all-to-all-done = bf16[16,4,1536]{2,1,0:T(4,128)(2,1)S(1)} async-done(((bf16[16,4,1536]{2,1,0:T(4,128)(2,1)}), bf16[16,4,1536]{2,1,0:T(4,128)(2,1)S(1)}, u32[]{:S(2)}, u32[]{:S(2)}) %all-to-all-start) | async-done | bytes 196640 | tf_op jit(solution)/shard_map/all_to_all | solution.py:456
  25.4 4.2 %all-to-all-start.1 = ((bf16[4,64,768]{2,1,0:T(8,128)(2,1)}), bf16[4,64,768]{2,1,0:T(8,128)(2,1)S(1)}, u32[]{:S(2)}, u32[]{:S(2)}) async-start(bf16[4,64,768]{2,1,0:T(8,128)(2,1)} %broadcast_in_dim.32), calls=%async_computation.1 | async-start | bytes 786432 | tf_op jit(solution)/shard_map/all_to_all | solution.py:400
  30.8 2.5 %collective-permute-start.1 = (bf16[64,768]{1,0:T(8,128)(2,1)S(1)}, bf16[64,768]{1,0:T(8,128)(2,1)S(1)}, u32[]{:S(2)}, u32[]{:S(2)}) collective-permute-start(bf16[64,768]{1,0:T(8,128)(2,1)S(1)} %get-tuple-element.122.refs_0_), channel_id=1, source_target_pairs={{0,4},{2,6},{4,0},{6,2},{1,5},{3,7},{5,1},{7,3},{8,12},{10,14},{12... | collective-permute-start | bytes 294920 | tf_op jit(solution)/shard_map/ppermute | solution.py:407
  40.6 4.5 %all-to-all-start.2 = ((bf16[4,256,768]{2,1,0:T(8,128)(2,1)}), bf16[4,256,768]{2,1,0:T(8,128)(2,1)}, u32[]{:S(2)}, u32[]{:S(2)}) async-start(bf16[4,256,768]{2,1,0:T(8,128)(2,1)} %shard_map.173), calls=%async_computation.2 | async-start | bytes 3145728 | tf_op jit(solution)/shard_map/all_to_all | solution.py:487
  45.2 3.3 %collective-permute-start.6 = (bf16[256,768]{1,0:T(8,128)(2,1)S(1)}, bf16[256,768]{1,0:T(8,128)(2,1)S(1)}, u32[]{:S(2)}, u32[]{:S(2)}) collective-permute-start(bf16[256,768]{1,0:T(8,128)(2,1)S(1)} %bitcast.29), channel_id=1, source_target_pairs={{0,4},{2,6},{4,0},{6,2},{1,5},{3,7},{5,1},{7,3},{8,12},{10,14},{12... | collective-permute-start | bytes 1179656 | tf_op jit(solution)/shard_map/ppermute | solution.py:407
  49.0 6.2 %collective-permute-done.5.refs_1_.refs_2_ = bf16[256,768]{1,0:T(8,128)(2,1)S(1)} collective-permute-done((bf16[256,768]{1,0:T(8,128)(2,1)S(1)}, bf16[256,768]{1,0:T(8,128)(2,1)S(1)}, u32[]{:S(2)}, u32[]{:S(2)}) %collective-permute-start.5) | collective-permute-done | bytes 393248 | tf_op jit(solution)/shard_map/ppermute | solution.py:407
  55.2 9.2 %collective-permute-done.6.refs_2_.refs_3_ = bf16[256,768]{1,0:T(8,128)(2,1)S(1)} collective-permute-done((bf16[256,768]{1,0:T(8,128)(2,1)S(1)}, bf16[256,768]{1,0:T(8,128)(2,1)S(1)}, u32[]{:S(2)}, u32[]{:S(2)}) %collective-permute-start.6) | collective-permute-done | bytes 393248 | tf_op jit(solution)/shard_map/ppermute | solution.py:407
  65.3 8.0 %shard_map.174 = (f32[1024,256]{1,0:T(8,128)}, bf16[1024,256]{1,0:T(8,128)(2,1)}, bf16[1024,256]{1,0:T(8,128)(2,1)}, f32[8,512]{1,0:T(8,128)S(1)}, bf16[8,512]{1...) custom-call(s32[2]{0:T(128)S(1)} %pad_add_fusion.at_ref, ...), custom_call_target="tpu_custom_call" | custom-call | flops 1100000000 | bytes 8634368 | tf_op jit(solution)/shard_map/pallas_call | solution.py:49
  78.1 5.2 %all-to-all-start.3 = ((f32[32,1,128]{2,1,0:T(1,128)}), f32[32,1,128]{2,1,0:T(1,128)S(1)}, u32[]{:S(2)}, u32[]{:S(2)}) async-start(f32[32,1,128]{2,1,0:T(1,128)} %get-tuple-element.77), calls=%async_computation.3 | async-start | bytes 32768 | tf_op jit(solution)/shard_map/all_to_all | solution.py:518
  83.3 7.9 %shard_map.176 = (f32[1024,512]{1,0:T(8,128)}, f32[8,512]{1,0:T(8,128)S(1)}, f32[8,1024]{1,0:T(8,128)S(1)}, f32[8,1024]{1,0:T(8,128)S(1)}, bf16[512,1024]{1,0:T(8,128)(2,1)}) custom-call(s32[2]{0:T(128)S(1)} %pad_add_fusion.at_ref, s32[8]{0:T(128)S(1)} %convert_reduce_fusion.len_ref, bf16[1024,256]{1,0:T(8,128)(2,1)} %get-tuple-element.79.krot_ref, ...), custom_call_target="tpu_custom_call" | custom-call | flops 200000000 | bytes 9752576 | tf_op jit(solution)/shard_map/pallas_call | solution.py:49
  92.3 6.4 %shard_map.177 = (bf16[4,256,768]{2,1,0:T(8,128)(2,1)}, bf16[256,768]{1,0:T(8,128)(2,1)S(1)}, bf16[256,768]{1,0:T(8,128)(2,1)}, bf16[256,768]{1,0:T(8,128)(2,1)S...) custom-call(s32[2]{0:T(128)S(1)} %pad_add_fusion.at_ref, ...), custom_call_target="tpu_custom_call" | custom-call | flops 1100000000 | bytes 8560640 | tf_op jit(solution)/shard_map/pallas_call | solution.py:49
  98.7 4.4 %all-to-all-start.4 = ((bf16[4,256,768]{2,1,0:T(8,128)(2,1)}), bf16[4,256,768]{2,1,0:T(8,128)(2,1)}, u32[]{:S(2)}, u32[]{:S(2)}) async-start(bf16[4,256,768]{2,1,0:T(8,128)(2,1)} %get-tuple-element.96), calls=%async_computation.4 | async-start | bytes 3145728 | tf_op jit(solution)/shard_map/all_to_all | solution.py:544
  105.1 2.4 %collective-permute-start.11 = (bf16[256,768]{1,0:T(8,128)(2,1)S(1)}, bf16[256,768]{1,0:T(8,128)(2,1)S(1)}, u32[]{:S(2)}, u32[]{:S(2)}) collective-permute-start(bf16[256,768]{1,0:T(8,128)(2,1)S(1)} %get-tuple-element.99), channel_id=1, source_target_pairs={{0,4},{2,6},{4,0},{6,2},{1,5},{3,7},{5,1},{7,3},{8,12},{10,14},{12... | collective-permute-start | bytes 1179656 | tf_op jit(solution)/shard_map/ppermute | solution.py:413
  115.4 5.5 %shard_map.178 = bf16[512,1024]{1,0:T(8,128)(2,1)} custom-call(s32[8]{0:T(128)S(1)} %convert_reduce_fusion.len_ref, bf16[512,1024]{1,0:T(8,128)(2,1)S(1)} %bitcast.27, f32[1,1024]{1,0:T(1,128)S(1)} %bitcast.35, bf16[1024,512]{1,0:T(8,128)(2,1)} %get-tuple-element.101.skv_ref, f32[8,128]{1,0:T(8,128)S(1)} %get-tuple-element.102.g_ref, ...), custom_call_target="tpu_custom_call" | custom-call | flops 600000000 | bytes 5873664 | tf_op jit(solution)/shard_map/pallas_call | solution.py:49
  120.9 4.4 %collective-permute-done.11.refs_2_ = bf16[256,768]{1,0:T(8,128)(2,1)S(1)} collective-permute-done((bf16[256,768]{1,0:T(8,128)(2,1)S(1)}, bf16[256,768]{1,0:T(8,128)(2,1)S(1)}, u32[]{:S(2)}, u32[]{:S(2)}) %collective-permute-start.11) | collective-permute-done | bytes 393248 | tf_op jit(solution)/shard_map/ppermute | solution.py:413
  125.3 2.9 %shard_map.179 = (bf16[64,768]{1,0:T(8,128)(2,1)S(1)}, bf16[64,768]{1,0:T(8,128)(2,1)S(1)}, bf16[64,768]{1,0:T(8,128)(2,1)S(1)}, bf16[64,768]{1,0:T(8,128)(2,1)S(1)}, bf16[4,80,768]{2,1,0:T(8,128)(2,1)}) custom-call(s32[2]{0:T(128)S(1)} %pad_add_fusion.at_ref, f32[8,128]{1,0:T(8,128)S(1)} %get-tuple-element.95.loss_ref, ...), custom_call_target="tpu_custom_call" | custom-call | bytes 4034560 | tf_op jit(solution)/shard_map/pallas_call | solution.py:49
  128.2 4.4 %all-to-all-start.5 = ((bf16[4,80,768]{2,1,0:T(8,128)(2,1)}), bf16[4,80,768]{2,1,0:T(8,128)(2,1)S(1)}, u32[]{:S(2)}, u32[]{:S(2)}) async-start(bf16[4,80,768]{2,1,0:T(8,128)(2,1)} %get-tuple-element.111), calls=%async_computation.5 | async-start | bytes 983040 | tf_op jit(solution)/shard_map/all_to_all | solution.py:562
  132.6 2.6 %collective-permute-start.17 = (bf16[64,768]{1,0:T(8,128)(2,1)S(1)}, bf16[64,768]{1,0:T(8,128)(2,1)S(1)}, u32[]{:S(2)}, u32[]{:S(2)}) collective-permute-start(bf16[64,768]{1,0:T(8,128)(2,1)S(1)} %get-tuple-element.116), channel_id=1, source_target_pairs={{0,6},{2,0},{4,2},{6,4},{1,7},{3,1},{5,3},{7,5},{8,14},{10,8},{12,... | collective-permute-start | bytes 294920 | tf_op jit(solution)/shard_map/ppermute | solution.py:413
  137.5 2.7 %collective-permute-done.16 = bf16[64,768]{1,0:T(8,128)(2,1)S(1)} collective-permute-done((bf16[64,768]{1,0:T(8,128)(2,1)S(1)}, bf16[64,768]{1,0:T(8,128)(2,1)S(1)}, u32[]{:S(2)}, u32[]{:S(2)}) %collective-permute-start.16) | collective-permute-done | bytes 98336 | tf_op jit(solution)/shard_map/ppermute | solution.py:413
  140.2 2.4 %collective-permute-done.15 = bf16[64,768]{1,0:T(8,128)(2,1)S(1)} collective-permute-done((bf16[64,768]{1,0:T(8,128)(2,1)S(1)}, bf16[64,768]{1,0:T(8,128)(2,1)S(1)}, u32[]{:S(2)}, u32[]{:S(2)}) %collective-permute-start.15) | collective-permute-done | bytes 98336 | tf_op jit(solution)/shard_map/ppermute | solution.py:413
  143.5 7.6 %all-to-all-start.6 = ((bf16[16,4,1536]{2,1,0:T(4,128)(2,1)}), bf16[16,4,1536]{2,1,0:T(4,128)(2,1)S(1)}, u32[]{:S(2)}, u32[]{:S(2)}) async-start(bf16[16,4,1536]{2,1,0:T(4,128)(2,1)} %reshape.88), calls=%async_computation.6 | async-start | bytes 393216 | tf_op jit(solution)/shard_map/all_to_all | solution.py:574
  154.4 7.0 %all-to-all-done.6 = bf16[16,4,1536]{2,1,0:T(4,128)(2,1)S(1)} async-done(((bf16[16,4,1536]{2,1,0:T(4,128)(2,1)}), bf16[16,4,1536]{2,1,0:T(4,128)(2,1)S(1)}, u32[]{:S(2)}, u32[]{:S(2)}) %all-to-all-start.6) | async-done | bytes 196640 | tf_op jit(solution)/shard_map/all_to_all | solution.py:574
  (98 shorter events, 36.9 us)
Async XLA Ops:
  4.1 20.3 %all-to-all-start = ((bf16[16,4,1536]{2,1,0:T(4,128)(2,1)}), bf16[16,4,1536]{2,1,0:T(4,128)(2,1)S(1)}, u32[]{:S(2)}, u32[]{:S(2)}) async-start(bf16[16,4,1536]{2,1,0:T(4,128)(2,1)} %bitcast.1), calls=%async_computation | async-start | bytes 393216 | tf_op jit(solution)/shard_map/all_to_all | solution.py:456
  24.5 15.0 %collective-permute-start.3 = (bf16[512,1024]{1,0:T(8,128)(2,1)S(1)}, bf16[512,1024]{1,0:T(8,128)(2,1)S(1)}, u32[]{:S(2)}, u32[]{:S(2)}) collective-permute-start(bf16[512,1024]{1,0:T(8,128)(2,1)S(1)} %get-tuple-element.70.normed_ref), channel_id=1, source_target_pairs={{0,1},{1,0},{2,3},{3,2},{4,5},{5,4},{6,7},{7,6},{8,9},{9,8},{10,11... | collective-permute-start | bytes 3145736 | tf_op jit(solution)/shard_map/ppermute | solution.py:426
  25.4 14.1 %all-to-all-start.1 = ((bf16[4,64,768]{2,1,0:T(8,128)(2,1)}), bf16[4,64,768]{2,1,0:T(8,128)(2,1)S(1)}, u32[]{:S(2)}, u32[]{:S(2)}) async-start(bf16[4,64,768]{2,1,0:T(8,128)(2,1)} %broadcast_in_dim.32), calls=%async_computation.1 | async-start | bytes 786432 | tf_op jit(solution)/shard_map/all_to_all | solution.py:400
  29.6 6.5 %collective-permute-start = (bf16[64,768]{1,0:T(8,128)(2,1)S(1)}, bf16[64,768]{1,0:T(8,128)(2,1)S(1)}, u32[]{:S(2)}, u32[]{:S(2)}) collective-permute-start(bf16[64,768]{1,0:T(8,128)(2,1)S(1)} %get-tuple-element.122.refs_0_), channel_id=1, source_target_pairs={{0,2},{2,4},{4,6},{6,0},{1,3},{3,5},{5,7},{7,1},{8,10},{10,12},{12... | collective-permute-start | bytes 294920 | tf_op jit(solution)/shard_map/ppermute | solution.py:407
  30.8 6.6 %collective-permute-start.1 = (bf16[64,768]{1,0:T(8,128)(2,1)S(1)}, bf16[64,768]{1,0:T(8,128)(2,1)S(1)}, u32[]{:S(2)}, u32[]{:S(2)}) collective-permute-start(bf16[64,768]{1,0:T(8,128)(2,1)S(1)} %get-tuple-element.122.refs_0_), channel_id=1, source_target_pairs={{0,4},{2,6},{4,0},{6,2},{1,5},{3,7},{5,1},{7,3},{8,12},{10,14},{12... | collective-permute-start | bytes 294920 | tf_op jit(solution)/shard_map/ppermute | solution.py:407
  33.2 4.5 %collective-permute-start.2 = (bf16[64,768]{1,0:T(8,128)(2,1)S(1)}, bf16[64,768]{1,0:T(8,128)(2,1)S(1)}, u32[]{:S(2)}, u32[]{:S(2)}) collective-permute-start(bf16[64,768]{1,0:T(8,128)(2,1)S(1)} %get-tuple-element.122.refs_0_), channel_id=1, source_target_pairs={{0,6},{2,0},{4,2},{6,4},{1,7},{3,1},{5,3},{7,5},{8,14},{10,8},{12,... | collective-permute-start | bytes 294920 | tf_op jit(solution)/shard_map/ppermute | solution.py:407
  34.4 5.1 %collective-permute-start.4 = (f32[4,2304]{1,0:T(4,128)S(1)}, f32[4,2304]{1,0:T(4,128)S(1)}, u32[]{:S(2)}, u32[]{:S(2)}) collective-permute-start(f32[4,2304]{1,0:T(4,128)S(1)} %pad_maximum_fusion.1), channel_id=1, source_target_pairs={{0,1},{1,0},{2,3},{3,2},{4,5},{5,4},{6,7},{7,6},{8,9},{9,8},{10,11... | collective-permute-start | bytes 110600 | tf_op jit(solution)/shard_map/ppermute | solution.py:426
  40.6 24.8 %all-to-all-start.2 = ((bf16[4,256,768]{2,1,0:T(8,128)(2,1)}), bf16[4,256,768]{2,1,0:T(8,128)(2,1)}, u32[]{:S(2)}, u32[]{:S(2)}) async-start(bf16[4,256,768]{2,1,0:T(8,128)(2,1)} %shard_map.173), calls=%async_computation.2 | async-start | bytes 3145728 | tf_op jit(solution)/shard_map/all_to_all | solution.py:487
  45.1 10.1 %collective-permute-start.5 = (bf16[256,768]{1,0:T(8,128)(2,1)S(1)}, bf16[256,768]{1,0:T(8,128)(2,1)S(1)}, u32[]{:S(2)}, u32[]{:S(2)}) collective-permute-start(bf16[256,768]{1,0:T(8,128)(2,1)S(1)} %bitcast.28), channel_id=1, source_target_pairs={{0,2},{2,4},{4,6},{6,0},{1,3},{3,5},{5,7},{7,1},{8,10},{10,12},{12... | collective-permute-start | bytes 1179656 | tf_op jit(solution)/shard_map/ppermute | solution.py:407
  45.2 19.2 %collective-permute-start.6 = (bf16[256,768]{1,0:T(8,128)(2,1)S(1)}, bf16[256,768]{1,0:T(8,128)(2,1)S(1)}, u32[]{:S(2)}, u32[]{:S(2)}) collective-permute-start(bf16[256,768]{1,0:T(8,128)(2,1)S(1)} %bitcast.29), channel_id=1, source_target_pairs={{0,4},{2,6},{4,0},{6,2},{1,5},{3,7},{5,1},{7,3},{8,12},{10,14},{12... | collective-permute-start | bytes 1179656 | tf_op jit(solution)/shard_map/ppermute | solution.py:407
  48.6 16.7 %collective-permute-start.7 = (bf16[256,768]{1,0:T(8,128)(2,1)S(1)}, bf16[256,768]{1,0:T(8,128)(2,1)S(1)}, u32[]{:S(2)}, u32[]{:S(2)}) collective-permute-start(bf16[256,768]{1,0:T(8,128)(2,1)S(1)} %bitcast.30), channel_id=1, source_target_pairs={{0,6},{2,0},{4,2},{6,4},{1,7},{3,1},{5,3},{7,5},{8,14},{10,8},{12,... | collective-permute-start | bytes 1179656 | tf_op jit(solution)/shard_map/ppermute | solution.py:407
  73.3 19.0 %collective-permute-start.9 = (bf16[1024,512]{1,0:T(8,128)(2,1)}, bf16[1024,512]{1,0:T(8,128)(2,1)}, u32[]{:S(2)}, u32[]{:S(2)}) collective-permute-start(bf16[1024,512]{1,0:T(8,128)(2,1)} %get-tuple-element.93.turned_ref), channel_id=1, source_target_pairs={{0,1},{1,0},{2,3},{3,2},{4,5},{5,4},{6,7},{7,6},{8,9},{9,8},{10,11... | collective-permute-start | bytes 3145736 | tf_op jit(solution)/shard_map/ppermute | solution.py:426
  75.1 2.2 %collective-permute-start.8 = (f32[8,1024]{1,0:T(8,128)S(1)}, f32[8,1024]{1,0:T(8,128)S(1)}, u32[]{:S(2)}, u32[]{:S(2)}) collective-permute-start(f32[8,1024]{1,0:T(8,128)S(1)} %get-tuple-element.75.mine_ref), channel_id=1, source_target_pairs={{0,1},{1,0},{2,3},{3,2},{4,5},{5,4},{6,7},{7,6},{8,9},{9,8},{10,11... | collective-permute-start | bytes 98312 | tf_op jit(solution)/shard_map/ppermute | solution.py:426
  78.1 14.2 %all-to-all-start.3 = ((f32[32,1,128]{2,1,0:T(1,128)}), f32[32,1,128]{2,1,0:T(1,128)S(1)}, u32[]{:S(2)}, u32[]{:S(2)}) async-start(f32[32,1,128]{2,1,0:T(1,128)} %get-tuple-element.77), calls=%async_computation.3 | async-start | bytes 32768 | tf_op jit(solution)/shard_map/all_to_all | solution.py:518
  98.7 26.6 %all-to-all-start.4 = ((bf16[4,256,768]{2,1,0:T(8,128)(2,1)}), bf16[4,256,768]{2,1,0:T(8,128)(2,1)}, u32[]{:S(2)}, u32[]{:S(2)}) async-start(bf16[4,256,768]{2,1,0:T(8,128)(2,1)} %get-tuple-element.96), calls=%async_computation.4 | async-start | bytes 3145728 | tf_op jit(solution)/shard_map/all_to_all | solution.py:544
  103.1 12.3 %collective-permute-start.14 = (bf16[512,1024]{1,0:T(8,128)(2,1)}, bf16[512,1024]{1,0:T(8,128)(2,1)}, u32[]{:S(2)}, u32[]{:S(2)}) collective-permute-start(bf16[512,1024]{1,0:T(8,128)(2,1)} %get-tuple-element.105), channel_id=1, source_target_pairs={{0,1},{1,0},{2,3},{3,2},{4,5},{5,4},{6,7},{7,6},{8,9},{9,8},{10,11... | collective-permute-start | bytes 3145736 | tf_op jit(solution)/shard_map/ppermute | solution.py:426
  104.2 16.7 %collective-permute-start.10 = (bf16[256,768]{1,0:T(8,128)(2,1)}, bf16[256,768]{1,0:T(8,128)(2,1)S(1)}, u32[]{:S(2)}, u32[]{:S(2)}) collective-permute-start(bf16[256,768]{1,0:T(8,128)(2,1)} %get-tuple-element.98), channel_id=1, source_target_pairs={{0,2},{2,4},{4,6},{6,0},{1,3},{3,5},{5,7},{7,1},{8,10},{10,12},{12... | collective-permute-start | bytes 1179656 | tf_op jit(solution)/shard_map/ppermute | solution.py:413
  105.1 20.2 %collective-permute-start.11 = (bf16[256,768]{1,0:T(8,128)(2,1)S(1)}, bf16[256,768]{1,0:T(8,128)(2,1)S(1)}, u32[]{:S(2)}, u32[]{:S(2)}) collective-permute-start(bf16[256,768]{1,0:T(8,128)(2,1)S(1)} %get-tuple-element.99), channel_id=1, source_target_pairs={{0,4},{2,6},{4,0},{6,2},{1,5},{3,7},{5,1},{7,3},{8,12},{10,14},{12... | collective-permute-start | bytes 1179656 | tf_op jit(solution)/shard_map/ppermute | solution.py:413
  107.4 17.8 %collective-permute-start.12 = (bf16[256,768]{1,0:T(8,128)(2,1)S(1)}, bf16[256,768]{1,0:T(8,128)(2,1)S(1)}, u32[]{:S(2)}, u32[]{:S(2)}) collective-permute-start(bf16[256,768]{1,0:T(8,128)(2,1)S(1)} %get-tuple-element.100), channel_id=1, source_target_pairs={{0,6},{2,0},{4,2},{6,4},{1,7},{3,1},{5,3},{7,5},{8,14},{10,8},{12,... | collective-permute-start | bytes 1179656 | tf_op jit(solution)/shard_map/ppermute | solution.py:413
  128.2 14.5 %all-to-all-start.5 = ((bf16[4,80,768]{2,1,0:T(8,128)(2,1)}), bf16[4,80,768]{2,1,0:T(8,128)(2,1)S(1)}, u32[]{:S(2)}, u32[]{:S(2)}) async-start(bf16[4,80,768]{2,1,0:T(8,128)(2,1)} %get-tuple-element.111), calls=%async_computation.5 | async-start | bytes 983040 | tf_op jit(solution)/shard_map/all_to_all | solution.py:562
  132.6 4.9 %collective-permute-start.17 = (bf16[64,768]{1,0:T(8,128)(2,1)S(1)}, bf16[64,768]{1,0:T(8,128)(2,1)S(1)}, u32[]{:S(2)}, u32[]{:S(2)}) collective-permute-start(bf16[64,768]{1,0:T(8,128)(2,1)S(1)} %get-tuple-element.116), channel_id=1, source_target_pairs={{0,6},{2,0},{4,2},{6,4},{1,7},{3,1},{5,3},{7,5},{8,14},{10,8},{12,... | collective-permute-start | bytes 294920 | tf_op jit(solution)/shard_map/ppermute | solution.py:413
  135.1 5.1 %collective-permute-start.16 = (bf16[64,768]{1,0:T(8,128)(2,1)S(1)}, bf16[64,768]{1,0:T(8,128)(2,1)S(1)}, u32[]{:S(2)}, u32[]{:S(2)}) collective-permute-start(bf16[64,768]{1,0:T(8,128)(2,1)S(1)} %get-tuple-element.115), channel_id=1, source_target_pairs={{0,4},{2,6},{4,0},{6,2},{1,5},{3,7},{5,1},{7,3},{8,12},{10,14},{12... | collective-permute-start | bytes 294920 | tf_op jit(solution)/shard_map/ppermute | solution.py:413
  135.7 6.9 %collective-permute-start.15 = (bf16[64,768]{1,0:T(8,128)(2,1)S(1)}, bf16[64,768]{1,0:T(8,128)(2,1)S(1)}, u32[]{:S(2)}, u32[]{:S(2)}) collective-permute-start(bf16[64,768]{1,0:T(8,128)(2,1)S(1)} %get-tuple-element.114), channel_id=1, source_target_pairs={{0,2},{2,4},{4,6},{6,0},{1,3},{3,5},{5,7},{7,1},{8,10},{10,12},{12... | collective-permute-start | bytes 294920 | tf_op jit(solution)/shard_map/ppermute | solution.py:413
  143.5 17.9 %all-to-all-start.6 = ((bf16[16,4,1536]{2,1,0:T(4,128)(2,1)}), bf16[16,4,1536]{2,1,0:T(4,128)(2,1)S(1)}, u32[]{:S(2)}, u32[]{:S(2)}) async-start(bf16[16,4,1536]{2,1,0:T(4,128)(2,1)} %reshape.88), calls=%async_computation.6 | async-start | bytes 393216 | tf_op jit(solution)/shard_map/all_to_all | solution.py:574
  (17 other events, 150.9 us)

commit v4 on v3

--- a/solution.py
+++ b/solution.py
@@ -41,17 +41,22 @@
     return pl.BlockSpec(shape, lambda i: (0,) * len(shape), pipeline_mode=pl.Buffered(1))
 
 
-def call(body, scalars, arrays, outs, scratch=(), flops=0, grant=52, light=False):
+def block(cuts, key, shape):
+    if key in cuts:
+        return pl.BlockSpec(cuts[key], lambda i: (i,) + (0,) * (len(shape) - 1))
+    return whole(shape)
+
+
+def call(body, scalars, arrays, outs, scratch=(), flops=0, grant=52, cuts=()):
     moved = sum(a.size * a.dtype.itemsize for a in arrays)
     moved += sum(int(np.prod(o)) * np.dtype(d).itemsize for o, d in outs)
-    if light:
-        moved = flops = 1024
     return pl.pallas_call(
         body,
-        grid=(1,),
+        grid=(4 if cuts else 1,),
         out_shape=[jax.ShapeDtypeStruct(o, d) for o, d in outs],
-        in_specs=[SM] * len(scalars) + [whole(a.shape) for a in arrays],
-        out_specs=[whole(o) for o, _ in outs],
+        in_specs=[SM] * len(scalars)
+        + [block(cuts, k, a.shape) for k, a in enumerate(arrays)],
+        out_specs=[block(cuts, -1 - k, o) for k, (o, _) in enumerate(outs)],
         scratch_shapes=[pltpu.VMEM(o, d) for o, d in scratch],
         compiler_params=pltpu.CompilerParams(vmem_limit_bytes=grant << 20),
         cost_estimate=pl.CostEstimate(flops=flops, bytes_accessed=moved, transcendentals=0),
@@ -145,13 +150,13 @@
 def attend_body(
     at_ref, len_ref, normed_ref, other_ref, nlast_ref, cos_ref, sin_ref, kv_ref, *refs
 ):
-    out_ref, o_ref, turn_scr = refs[11], refs[12], refs[15]
+    out_ref, o_ref, turn_scr, lg_scr = refs[11], refs[12], refs[15], refs[16]
     q_refs = refs[0:4]
     kproj_ref, krot_ref, vcast_ref, qproj_ref, qrot_ref, attn_ref, ctx_ref = refs[4:11]
     qr_scr, ctx_scr = refs[13:15]
     x = at_ref[1]
     mask, even = block_mask()
-    lane = lax.broadcasted_iota(jnp.int32, (8, SEQ), 1)
+    lane = lax.broadcasted_iota(jnp.int32, (8 * BOTH, SEQ), 1)
     for side, rows_ref in enumerate((normed_ref, other_ref)):
 
         @pl.loop(0, 2)
@@ -180,12 +185,19 @@
             u = k * lax.rsqrt(jnp.mean(k * k, axis=-1, keepdims=True) + EPS)
             r = u * cos_ref[...] + half_turn(u) * sin_ref[...]
             krot_ref[rows, g * HW : (g + 1) * HW] = r.astype(BF16)
+    for p in range(BOTH):
+        rows = slice(p * SEQ, (p + 1) * SEQ)
         qb = to_blocks(qr_scr[p : p + 1, :], mask, even).astype(BF16)
-        logits = dot(qb, krot_ref[rows, :], LAST) * SCALE
-        ex = jnp.where(lane <= len_ref[p] - 1, jnp.exp(logits), 0.0)
-        w = ex / jnp.sum(ex, axis=-1, keepdims=True)
-        attn_ref[p * 8 : (p + 1) * 8, :] = w
-        c = dot(w.astype(BF16), vcast_ref[rows, :])
+        lg_scr[p * 8 : (p + 1) * 8, :] = dot(qb, krot_ref[rows, :], LAST)
+    last = jnp.concatenate(
+        [jnp.full((8, SEQ), len_ref[p] - 1, jnp.int32) for p in range(BOTH)], axis=0
+    )
+    ex = jnp.where(lane <= last, jnp.exp(lg_scr[...] * SCALE), 0.0)
+    w = ex / jnp.sum(ex, axis=-1, keepdims=True)
+    attn_ref[...] = w
+    probs = w.astype(BF16)
+    for p in range(BOTH):
+        c = dot(probs[p * 8 : (p + 1) * 8, :], vcast_ref[p * SEQ : (p + 1) * SEQ, :])
         ctx_scr[p : p + 1, :] = from_blocks(c, mask, even)
     ctx_ref[...] = ctx_scr[...].astype(BF16)
     for d in range(4):
@@ -234,7 +246,7 @@
     *refs,
 ):
     o_ref, q_refs, kv_ref = refs[0], refs[1:5], refs[5]
-    gkv_ref, gq_ref, gr_ref, last_ref, send_ref, gc_scr, gq_scr, qr_scr = refs[6:]
+    gkv_ref, gq_ref, gr_ref, last_ref, send_ref, gc_scr, gq_scr, qr_scr, gp_scr = refs[6:]
     mask, even = block_mask()
     unit = unit_ref[...]
     gu = sv_ref[...] * fg_ref[...]
@@ -242,15 +254,23 @@
     gr_ref[...] = gr
     gc_scr[...] = dot(gr.astype(BF16), o_ref[...])
     qr_scr[...] = qrot_ref[...].astype(F32)
+    blocks = []
     for p in range(BOTH):
         rows = slice(p * SEQ, (p + 1) * SEQ)
         gb = to_blocks(gc_scr[p : p + 1, :], mask, even).astype(BF16)
+        blocks.append(gb)
+        gp_scr[p * 8 : (p + 1) * 8, :] = dot(gb, vcast_ref[rows, :], LAST)
+    w = attn_ref[...]
+    gp = gp_scr[...]
+    spread = jnp.sum(w * gp, axis=-1, keepdims=True)
+    dls = (w * (gp - spread)).astype(BF16)
+    probs = w.astype(BF16)
+    for p in range(BOTH):
+        rows = slice(p * SEQ, (p + 1) * SEQ)
+        eight = slice(p * 8, (p + 1) * 8)
         qb = to_blocks(qr_scr[p : p + 1, :], mask, even).astype(BF16)
-        w = attn_ref[p * 8 : (p + 1) * 8, :]
-        gp = dot(gb, vcast_ref[rows, :], LAST)
-        gkv_ref[rows, 256:512] = dot(w.astype(BF16), gb, FIRST)
-        spread = jnp.sum(w * gp, axis=-1, keepdims=True)
-        dl = (w * (gp - spread)).astype(BF16)
+        gkv_ref[rows, 256:512] = dot(probs[eight, :], blocks[p], FIRST)
+        dl = dls[eight, :]
         gq_scr[p : p + 1, :] = from_blocks(dot(dl, krot_ref[rows, :]) * SCALE, mask, even)
         gk = dot(dl, qb, FIRST) * SCALE
         for g in range(2):
@@ -298,49 +318,52 @@
     *refs,
 ):
     out_a, outs_b, loss_ref, skv_ref, g_ref, sr_ref = refs[0], refs[1:5], *refs[5:9]
-    srow_scr, sturn_scr, b_scr, sq_scr = refs[9:]
+    srow_scr, sturn_scr, sq_scr = refs[9:]
     x = at_ref[1]
-    lane = lax.broadcasted_iota(jnp.int32, (1, HW), 1)
-
-    def pick(v, i):
-        return jnp.sum(jnp.where(lane == i, v, 0.0), axis=-1, keepdims=True)
-
-    t = tot_ref[0]
-    for i in range(1, 32):
-        t = t + tot_ref[i]
-    ts, tt, cr = pick(t, 0), pick(t, 1), pick(t, 2)
-    loss_ref[...] = jnp.broadcast_to(cr / tt - jnp.log(tt) + jnp.log(ts), (8, HW))
-    row = lax.broadcasted_iota(jnp.int32, (8, HW), 0)
-    g = GRAD_SCALE * (jnp.exp(score_ref[...]) / ts - jnp.exp(teach_ref[...] / 2.0) / tt)
-    gcol = g[:, 0:1]
-    sr = gr_ref[...] * gcol
-    sr_ref[...] = sr
-    g_ref[...] = g
-    sq_scr[...] = (gq_ref[...] * gcol).astype(BF16)
-    srow_scr[...] = sr.astype(BF16)
-    sturn_scr[...] = (grturn_ref[...] * gcol).astype(BF16)
-    for p in range(BOTH):
-        rows = slice(p * SEQ, (p + 1) * SEQ)
-        skv_ref[rows, :] = (gkv_ref[rows, :] * gcol[p : p + 1, :]).astype(BF16)
-
-    @pl.loop(0, 4)
-    def _(i):
-        rows = pl.ds(pl.multiple_of(i * 256, 256), 256)
-        kv = dot(turned_ref[rows, :], skv_ref[0:ROWS, :]) + dot(
-            turned_other_ref[rows, :], skv_ref[ROWS : 2 * ROWS, :]
-        )
-        o_low = dot(srow_scr[:, rows], ctx_ref[:, 0:256], FIRST)
-        rows_x = block_at(x, i, 256)
-        q = dot(nlast_ref[:, rows_x], sq_scr[...], FIRST)
-        o_high = dot(sturn_scr[:, rows_x], ctx_ref[:, 256:512], FIRST)
-        here = pl.ds(i, 1)
-        out_a[here, :, 0:512] = kv.astype(BF16)[None]
-        out_a[here, :, 512:768] = o_low.astype(BF16)[None]
-        b_scr[here, :, 0:512] = q.astype(BF16)[None]
-        b_scr[here, :, 512:768] = o_high.astype(BF16)[None]
-
+    i = pl.program_id(0)
+
+    @pl.when(i == 0)
+    def _():
+        lane = lax.broadcasted_iota(jnp.int32, (1, HW), 1)
+
+        def pick(v, i):
+            return jnp.sum(jnp.where(lane == i, v, 0.0), axis=-1, keepdims=True)
+
+        t = tot_ref[0]
+        for i in range(1, 32):
+            t = t + tot_ref[i]
+        ts, tt, cr = pick(t, 0), pick(t, 1), pick(t, 2)
+        loss_ref[...] = jnp.broadcast_to(cr / tt - jnp.log(tt) + jnp.log(ts), (8, HW))
+        row = lax.broadcasted_iota(jnp.int32, (8, HW), 0)
+        g = GRAD_SCALE * (jnp.exp(score_ref[...]) / ts - jnp.exp(teach_ref[...] / 2.0) / tt)
+        gcol = g[:, 0:1]
+        sr = gr_ref[...] * gcol
+        sr_ref[...] = sr
+        g_ref[...] = g
+        sq_scr[...] = (gq_ref[...] * gcol).astype(BF16)
+        srow_scr[...] = sr.astype(BF16)
+        sturn_scr[...] = (grturn_ref[...] * gcol).astype(BF16)
+        for p in range(BOTH):
+            rows = slice(p * SEQ, (p + 1) * SEQ)
+            skv_ref[rows, :] = (gkv_ref[rows, :] * gcol[p : p + 1, :]).astype(BF16)
+
+    rows = pl.ds(pl.multiple_of(i * 256, 256), 256)
+    kv = dot(turned_ref[...], skv_ref[0:ROWS, :]) + dot(
+        turned_other_ref[...], skv_ref[ROWS : 2 * ROWS, :]
+    )
+    o_low = dot(srow_scr[:, rows], ctx_ref[:, 0:256], FIRST)
+    rows_x = block_at(x, i, 256)
+    q = dot(nlast_ref[:, rows_x], sq_scr[...], FIRST)
+    o_high = dot(sturn_scr[:, rows_x], ctx_ref[:, 256:512], FIRST)
+    out_a[0, :, 0:512] = kv.astype(BF16)
+    out_a[0, :, 512:768] = o_low.astype(BF16)
+    q, o_high = q.astype(BF16), o_high.astype(BF16)
     for d in range(4):
-        outs_b[d][...] = b_scr[d]
+
+        @pl.when(i == d)
+        def _():
+            outs_b[d][:, 0:512] = q
+            outs_b[d][:, 512:768] = o_high
 
 
 def middle_body(at_ref, loss_ref, got_a_ref, *refs):
@@ -451,6 +474,7 @@
         [],
         [key_matrix, value_matrix, query_weight, out_weight.T],
         [((8, 2, 4, 1536), BF16)],
+        grant=62,
     )
     both_halves = both_halves.reshape(16, 4, 1536)
     column = lax.all_to_all(both_halves, ("z", "c"), 0, 0, tiled=True).reshape(64, 1536)
@@ -478,7 +502,7 @@
     slab_b = everyone(column[:, 768:1536], "pb", 4).reshape(256, 768)
     ring_a = from_ring(column[:, 0:768], "x")
     (slab_a,) = call(arrange_body, [at], ring_a, [((4, 256, 768), BF16)], [((8, 4, 8, 768), BF16)])
-    slab_a, slab_b, other, got = lax.optimization_barrier((slab_a, slab_b, other, got))
+    slab_a, slab_b, got = lax.optimization_barrier((slab_a, slab_b, got))
     packed = jnp.concatenate([pack, got], axis=0)
     xlast = packed[:, 0:1024]
     nlast = packed[:, 1024:2048].astype(BF16)
@@ -502,7 +526,7 @@
             ((8, D), F32),
             ((D, 512), BF16),
         ],
-        [((8, 512), F32), ((8, 512), F32), ((32, 4, 8, 256), BF16)],
+        [((8, 512), F32), ((8, 512), F32), ((32, 4, 8, 256), BF16), ((8 * BOTH, SEQ), F32)],
         flops=1_100_000_000,
     )
     ctx, turned_late = lax.optimization_barrier((ctx, turned))
@@ -522,7 +546,7 @@
         [at, lens_both],
         [krot, vcast, kproj, qproj, qrot, attn, unit, oscale, fg, sv, cos, sin, oa, *qo, kvo],
         [((2 * ROWS, 512), F32), ((8, 512), F32), ((8, D), F32), ((8, D), F32), ((ROWS, D), BF16)],
-        [((8, 512), F32), ((8, 512), F32), ((8, 512), F32)],
+        [((8, 512), F32), ((8, 512), F32), ((8, 512), F32), ((8 * BOTH, SEQ), F32)],
         flops=200_000_000,
     )
     grturn = chunk_turn(gr)
@@ -537,8 +561,9 @@
         [pieces]
         + [((256, 768), BF16)] * 4
         + [((8, HW), F32), ((ROWS * 2, 512), BF16), ((8, HW), F32), ((8, D), F32)],
-        [((8, D), BF16), ((8, D), BF16), pieces, ((8, 512), BF16)],
+        [((8, D), BF16), ((8, D), BF16), ((8, 512), BF16)],
         flops=1_100_000_000,
+        cuts={7: (256, 512), 8: (256, 512), -1: (1, 256, 768)},
     )
     chip_b, (loss, skv, g, sr) = rest[0:4], rest[4:]
     got_a = lax.all_to_all(chip_a, "pb", 0, 0, tiled=True)

time: 164 us -> 161 us (0.982)
  local copies, waits for them, and re-layouts: 14.1 us -> 10.3 us
  waiting for transfers between devices: 44.2 us -> 46.5 us
    unnamed x32 -> x22, local copies, waits for them, and re-layouts: 5.13 us -> 1.38 us
  transfers between devices with their start and end apart: 25 -> 25, of which waited for: 13 -> 13; matrix products, arithmetic and copies ran while one was open for 5% -> 5% of each run, Pallas kernels for 12% -> 11%
where the time goes in v4:
time: 161 us; the launch traced here: 160 us
  starting transfers between devices  61.5 us (38%)
  waiting for transfers between devices  46.5 us (29%)
  Pallas kernels  36.9 us (23%)
  local copies, waits for them, and re-layouts  10.3 us (6%)
  between operations  4.63 us (3%)
    pallas_call x10, Pallas kernels, call(): pl.pallas_call(body, grid=(4 if cuts else 1,), out_shape=[jax.ShapeDtypeS...  36.9 us
    ppermute x6, waiting for transfers between devices, from_ring(): lax.ppermute(x, axis, [(i, (i + d) % 4) for i in range(4)])  19.2 us
    ppermute x6, waiting for transfers between devices, along_ring(): lax.ppermute(pieces[d], axis, [(i, (i + d) % 4) for i in range(4)])  12.1 us
    all_to_all x1, starting transfers between devices, shards(): lax.all_to_all(both_halves, ('z', 'c'), 0, 0, tiled=True).reshape(64, 1536)  9.98 us
    ppermute x6, starting transfers between devices, from_ring(): lax.ppermute(x, axis, [(i, (i + d) % 4) for i in range(4)])  9.28 us
    ppermute x6, starting transfers between devices, along_ring(): lax.ppermute(pieces[d], axis, [(i, (i + d) % 4) for i in range(4)])  7.24 us
    all_to_all x1, waiting for transfers between devices, shards(): lax.all_to_all(part.reshape(16, 4, 1536), ('z', 'c'), 0, 0, tiled=True)  7.02 us
    all_to_all x1, starting transfers between devices, shards(): lax.all_to_all(part.reshape(16, 4, 1536), ('z', 'c'), 0, 0, tiled=True)  6.39 us
  transfers between devices with their start and end apart: 25, of which 13 were waited for; matrix products, arithmetic and copies ran while one was open for 5% of the time, Pallas kernels for 11%

profile of v4, /device:TPU:1, one launch (start us, length us, event | category | flops | bytes accessed | tf_op | source)
XLA Modules:
  0.0 160.3 jit_solution(10533180164827244551)
XLA Ops:
  2.1 10.0 %all-to-all-start = ((bf16[16,4,1536]{2,1,0:T(4,128)(2,1)}), bf16[16,4,1536]{2,1,0:T(4,128)(2,1)S(1)}, u32[]{:S(2)}, u32[]{:S(2)}) async-start(bf16[16,4,1536]{2,1,0:T(4,128)(2,1)} %bitcast.44), calls=%async_computation | async-start | bytes 393216 | tf_op jit(solution)/shard_map/all_to_all | solution.py:480
  13.4 2.9 %shard_map.172 = (bf16[512,1024]{1,0:T(8,128)(2,1)S(1)}, bf16[1024,512]{1,0:T(8,128)(2,1)}, bf16[8,1024]{1,0:T(8,128)(2,1)S(1)}, f32[8,1024]{1,0:T(8,128)S(1)}) custom-call(s32[4]{0:T(128)S(1)} %bitcast.40, bf16[512,1024]{1,0:T(8,128)(2,1)} %bitcast.26, f32[1,1024]{1,0:T(1,128)S(1)} %bitcast.34), custom_call_target="tpu_custom_call" | custom-call | flops 10000000 | bytes 3198976 | tf_op jit(solution)/shard_map/pallas_call | solution.py:53
  17.3 5.1 %all-to-all-done = bf16[16,4,1536]{2,1,0:T(4,128)(2,1)S(1)} async-done(((bf16[16,4,1536]{2,1,0:T(4,128)(2,1)}), bf16[16,4,1536]{2,1,0:T(4,128)(2,1)S(1)}, u32[]{:S(2)}, u32[]{:S(2)}) %all-to-all-start) | async-done | bytes 196640 | tf_op jit(solution)/shard_map/all_to_all | solution.py:480
  23.3 4.2 %all-to-all-start.1 = ((bf16[4,64,768]{2,1,0:T(8,128)(2,1)}), bf16[4,64,768]{2,1,0:T(8,128)(2,1)S(1)}, u32[]{:S(2)}, u32[]{:S(2)}) async-start(bf16[4,64,768]{2,1,0:T(8,128)(2,1)} %broadcast_in_dim.32), calls=%async_computation.1 | async-start | bytes 786432 | tf_op jit(solution)/shard_map/all_to_all | solution.py:423
  28.7 2.5 %collective-permute-start.1 = (bf16[64,768]{1,0:T(8,128)(2,1)S(1)}, bf16[64,768]{1,0:T(8,128)(2,1)S(1)}, u32[]{:S(2)}, u32[]{:S(2)}) collective-permute-start(bf16[64,768]{1,0:T(8,128)(2,1)S(1)} %get-tuple-element.120.refs_0_), channel_id=1, source_target_pairs={{0,4},{2,6},{4,0},{6,2},{1,5},{3,7},{5,1},{7,3},{8,12},{10,14},{12... | collective-permute-start | bytes 294920 | tf_op jit(solution)/shard_map/ppermute | solution.py:430
  33.2 3.0 %collective-permute-done.1.refs_2_ = bf16[64,768]{1,0:T(8,128)(2,1)S(1)} collective-permute-done((bf16[64,768]{1,0:T(8,128)(2,1)S(1)}, bf16[64,768]{1,0:T(8,128)(2,1)S(1)}, u32[]{:S(2)}, u32[]{:S(2)}) %collective-permute-start.1) | collective-permute-done | bytes 98336 | tf_op jit(solution)/shard_map/ppermute | solution.py:430
  38.0 4.5 %all-to-all-start.2 = ((bf16[4,256,768]{2,1,0:T(8,128)(2,1)}), bf16[4,256,768]{2,1,0:T(8,128)(2,1)}, u32[]{:S(2)}, u32[]{:S(2)}) async-start(bf16[4,256,768]{2,1,0:T(8,128)(2,1)} %shard_map.173), calls=%async_computation.2 | async-start | bytes 3145728 | tf_op jit(solution)/shard_map/all_to_all | solution.py:511
  48.1 7.4 %collective-permute-done.5.refs_1_.refs_2_ = bf16[256,768]{1,0:T(8,128)(2,1)S(1)} collective-permute-done((bf16[256,768]{1,0:T(8,128)(2,1)S(1)}, bf16[256,768]{1,0:T(8,128)(2,1)S(1)}, u32[]{:S(2)}, u32[]{:S(2)}) %collective-permute-start.5) | collective-permute-done | bytes 393248 | tf_op jit(solution)/shard_map/ppermute | solution.py:430
  55.5 8.8 %collective-permute-done.6.refs_2_.refs_3_ = bf16[256,768]{1,0:T(8,128)(2,1)S(1)} collective-permute-done((bf16[256,768]{1,0:T(8,128)(2,1)S(1)}, bf16[256,768]{1,0:T(8,128)(2,1)S(1)}, u32[]{:S(2)}, u32[]{:S(2)}) %collective-permute-start.6) | collective-permute-done | bytes 393248 | tf_op jit(solution)/shard_map/ppermute | solution.py:430
  64.4 7.1 %shard_map.174 = (f32[1024,256]{1,0:T(8,128)}, bf16[1024,256]{1,0:T(8,128)(2,1)}, bf16[1024,256]{1,0:T(8,128)(2,1)}, f32[8,512]{1,0:T(8,128)S(1)}, bf16[8,512]{1...) custom-call(s32[2]{0:T(128)S(1)} %pad_add_fusion.at_ref, ...), custom_call_target="tpu_custom_call" | custom-call | flops 1100000000 | bytes 8634368 | tf_op jit(solution)/shard_map/pallas_call | solution.py:53
  75.4 5.1 %all-to-all-start.3 = ((f32[32,1,128]{2,1,0:T(1,128)}), f32[32,1,128]{2,1,0:T(1,128)S(1)}, u32[]{:S(2)}, u32[]{:S(2)}) async-start(f32[32,1,128]{2,1,0:T(1,128)} %get-tuple-element.75), calls=%async_computation.3 | async-start | bytes 32768 | tf_op jit(solution)/shard_map/all_to_all | solution.py:542
  80.6 7.1 %shard_map.176 = (f32[1024,512]{1,0:T(8,128)}, f32[8,512]{1,0:T(8,128)S(1)}, f32[8,1024]{1,0:T(8,128)S(1)}, f32[8,1024]{1,0:T(8,128)S(1)}, bf16[512,1024]{1,0:T(8,128)(2,1)}) custom-call(s32[2]{0:T(128)S(1)} %pad_add_fusion.at_ref, s32[8]{0:T(128)S(1)} %convert_reduce_fusion.len_ref, bf16[1024,256]{1,0:T(8,128)(2,1)} %get-tuple-element.77.krot_ref, ...), custom_call_target="tpu_custom_call" | custom-call | flops 200000000 | bytes 9752576 | tf_op jit(solution)/shard_map/pallas_call | solution.py:53
  88.9 6.6 %shard_map.177 = (bf16[4,256,768]{2,1,0:T(8,128)(2,1)}, bf16[256,768]{1,0:T(8,128)(2,1)S(1)}, bf16[256,768]{1,0:T(8,128)(2,1)}, bf16[256,768]{1,0:T(8,128)(2,1)}...) custom-call(s32[2]{0:T(128)S(1)} %pad_add_fusion.at_ref, ...), custom_call_target="tpu_custom_call" | custom-call | flops 1100000000 | bytes 8560640 | tf_op jit(solution)/shard_map/pallas_call | solution.py:53
  95.5 4.5 %all-to-all-start.4 = ((bf16[4,256,768]{2,1,0:T(8,128)(2,1)}), bf16[4,256,768]{2,1,0:T(8,128)(2,1)}, u32[]{:S(2)}, u32[]{:S(2)}) async-start(bf16[4,256,768]{2,1,0:T(8,128)(2,1)} %get-tuple-element.94), calls=%async_computation.4 | async-start | bytes 3145728 | tf_op jit(solution)/shard_map/all_to_all | solution.py:569
  106.7 2.2 %copy.28 = f32[8,32,4,8]{3,2,1,0:T(4,128)} copy(f32[8,32,4,8]{3,1,2,0:T(8,128)} %bitcast.41) | data formatting | bytes 65536 | tf_op jit(solution)/shard_map/transpose | solution.py:445
  112.3 5.5 %shard_map.178 = bf16[512,1024]{1,0:T(8,128)(2,1)} custom-call(s32[8]{0:T(128)S(1)} %convert_reduce_fusion.len_ref, bf16[512,1024]{1,0:T(8,128)(2,1)S(1)} %bitcast.27, f32[1,1024]{1,0:T(1,128)S(1)} %bitcast.35, bf16[1024,512]{1,0:T(8,128)(2,1)} %get-tuple-element.99.skv_ref, f32[8,128]{1,0:T(8,128)S(1)} %get-tuple-element.100.g_ref, ...), custom_call_target="tpu_custom_call" | custom-call | flops 600000000 | bytes 5873664 | tf_op jit(solution)/shard_map/pallas_call | solution.py:53
  117.8 4.5 %collective-permute-done.11.refs_2_ = bf16[256,768]{1,0:T(8,128)(2,1)S(1)} collective-permute-done((bf16[256,768]{1,0:T(8,128)(2,1)}, bf16[256,768]{1,0:T(8,128)(2,1)S(1)}, u32[]{:S(2)}, u32[]{:S(2)}) %collective-permute-start.11) | collective-permute-done | bytes 393248 | tf_op jit(solution)/shard_map/ppermute | solution.py:436
  122.8 2.9 %shard_map.179 = (bf16[64,768]{1,0:T(8,128)(2,1)S(1)}, bf16[64,768]{1,0:T(8,128)(2,1)S(1)}, bf16[64,768]{1,0:T(8,128)(2,1)S(1)}, bf16[64,768]{1,0:T(8,128)(2,1)S(1)}, bf16[4,80,768]{2,1,0:T(8,128)(2,1)}) custom-call(s32[2]{0:T(128)S(1)} %pad_add_fusion.at_ref, f32[8,128]{1,0:T(8,128)S(1)} %get-tuple-element.93.loss_ref, ...), custom_call_target="tpu_custom_call" | custom-call | bytes 4034560 | tf_op jit(solution)/shard_map/pallas_call | solution.py:53
  125.7 4.5 %all-to-all-start.5 = ((bf16[4,80,768]{2,1,0:T(8,128)(2,1)}), bf16[4,80,768]{2,1,0:T(8,128)(2,1)S(1)}, u32[]{:S(2)}, u32[]{:S(2)}) async-start(bf16[4,80,768]{2,1,0:T(8,128)(2,1)} %get-tuple-element.109), calls=%async_computation.5 | async-start | bytes 983040 | tf_op jit(solution)/shard_map/all_to_all | solution.py:587
  130.2 3.0 %collective-permute-start.17 = (bf16[64,768]{1,0:T(8,128)(2,1)S(1)}, bf16[64,768]{1,0:T(8,128)(2,1)S(1)}, u32[]{:S(2)}, u32[]{:S(2)}) collective-permute-start(bf16[64,768]{1,0:T(8,128)(2,1)S(1)} %get-tuple-element.114), channel_id=1, source_target_pairs={{0,6},{2,0},{4,2},{6,4},{1,7},{3,1},{5,3},{7,5},{8,14},{10,8},{12,... | collective-permute-start | bytes 294920 | tf_op jit(solution)/shard_map/ppermute | solution.py:436
  135.6 2.8 %collective-permute-done.16 = bf16[64,768]{1,0:T(8,128)(2,1)S(1)} collective-permute-done((bf16[64,768]{1,0:T(8,128)(2,1)S(1)}, bf16[64,768]{1,0:T(8,128)(2,1)S(1)}, u32[]{:S(2)}, u32[]{:S(2)}) %collective-permute-start.16) | collective-permute-done | bytes 98336 | tf_op jit(solution)/shard_map/ppermute | solution.py:436
  138.3 2.6 %collective-permute-done.15 = bf16[64,768]{1,0:T(8,128)(2,1)S(1)} collective-permute-done((bf16[64,768]{1,0:T(8,128)(2,1)S(1)}, bf16[64,768]{1,0:T(8,128)(2,1)S(1)}, u32[]{:S(2)}, u32[]{:S(2)}) %collective-permute-start.15) | collective-permute-done | bytes 98336 | tf_op jit(solution)/shard_map/ppermute | solution.py:436
  141.8 6.4 %all-to-all-start.6 = ((bf16[16,4,1536]{2,1,0:T(4,128)(2,1)}), bf16[16,4,1536]{2,1,0:T(4,128)(2,1)S(1)}, u32[]{:S(2)}, u32[]{:S(2)}) async-start(bf16[16,4,1536]{2,1,0:T(4,128)(2,1)} %reshape.88), calls=%async_computation.6 | async-start | bytes 393216 | tf_op jit(solution)/shard_map/all_to_all | solution.py:599
  151.5 7.0 %all-to-all-done.6 = bf16[16,4,1536]{2,1,0:T(4,128)(2,1)S(1)} async-done(((bf16[16,4,1536]{2,1,0:T(4,128)(2,1)}), bf16[16,4,1536]{2,1,0:T(4,128)(2,1)S(1)}, u32[]{:S(2)}, u32[]{:S(2)}) %all-to-all-start.6) | async-done | bytes 196640 | tf_op jit(solution)/shard_map/all_to_all | solution.py:599
  (88 shorter events, 35.6 us)
Async XLA Ops:
  2.1 20.3 %all-to-all-start = ((bf16[16,4,1536]{2,1,0:T(4,128)(2,1)}), bf16[16,4,1536]{2,1,0:T(4,128)(2,1)S(1)}, u32[]{:S(2)}, u32[]{:S(2)}) async-start(bf16[16,4,1536]{2,1,0:T(4,128)(2,1)} %bitcast.44), calls=%async_computation | async-start | bytes 393216 | tf_op jit(solution)/shard_map/all_to_all | solution.py:480
  23.3 14.7 %all-to-all-start.1 = ((bf16[4,64,768]{2,1,0:T(8,128)(2,1)}), bf16[4,64,768]{2,1,0:T(8,128)(2,1)S(1)}, u32[]{:S(2)}, u32[]{:S(2)}) async-start(bf16[4,64,768]{2,1,0:T(8,128)(2,1)} %broadcast_in_dim.32), calls=%async_computation.1 | async-start | bytes 786432 | tf_op jit(solution)/shard_map/all_to_all | solution.py:423
  27.4 5.7 %collective-permute-start = (bf16[64,768]{1,0:T(8,128)(2,1)S(1)}, bf16[64,768]{1,0:T(8,128)(2,1)S(1)}, u32[]{:S(2)}, u32[]{:S(2)}) collective-permute-start(bf16[64,768]{1,0:T(8,128)(2,1)S(1)} %get-tuple-element.120.refs_0_), channel_id=1, source_target_pairs={{0,2},{2,4},{4,6},{6,0},{1,3},{3,5},{5,7},{7,1},{8,10},{10,12},{12... | collective-permute-start | bytes 294920 | tf_op jit(solution)/shard_map/ppermute | solution.py:430
  28.7 7.5 %collective-permute-start.1 = (bf16[64,768]{1,0:T(8,128)(2,1)S(1)}, bf16[64,768]{1,0:T(8,128)(2,1)S(1)}, u32[]{:S(2)}, u32[]{:S(2)}) collective-permute-start(bf16[64,768]{1,0:T(8,128)(2,1)S(1)} %get-tuple-element.120.refs_0_), channel_id=1, source_target_pairs={{0,4},{2,6},{4,0},{6,2},{1,5},{3,7},{5,1},{7,3},{8,12},{10,14},{12... | collective-permute-start | bytes 294920 | tf_op jit(solution)/shard_map/ppermute | solution.py:430
  31.1 5.1 %collective-permute-start.2 = (bf16[64,768]{1,0:T(8,128)(2,1)S(1)}, bf16[64,768]{1,0:T(8,128)(2,1)S(1)}, u32[]{:S(2)}, u32[]{:S(2)}) collective-permute-start(bf16[64,768]{1,0:T(8,128)(2,1)S(1)} %get-tuple-element.120.refs_0_), channel_id=1, source_target_pairs={{0,6},{2,0},{4,2},{6,4},{1,7},{3,1},{5,3},{7,5},{8,14},{10,8},{12,... | collective-permute-start | bytes 294920 | tf_op jit(solution)/shard_map/ppermute | solution.py:430
  32.3 5.7 %collective-permute-start.3 = (f32[4,2304]{1,0:T(4,128)S(1)}, f32[4,2304]{1,0:T(4,128)S(1)}, u32[]{:S(2)}, u32[]{:S(2)}) collective-permute-start(f32[4,2304]{1,0:T(4,128)S(1)} %pad_maximum_fusion.1), channel_id=1, source_target_pairs={{0,1},{1,0},{2,3},{3,2},{4,5},{5,4},{6,7},{7,6},{8,9},{9,8},{10,11... | collective-permute-start | bytes 110600 | tf_op jit(solution)/shard_map/ppermute | solution.py:449
  38.0 26.3 %all-to-all-start.2 = ((bf16[4,256,768]{2,1,0:T(8,128)(2,1)}), bf16[4,256,768]{2,1,0:T(8,128)(2,1)}, u32[]{:S(2)}, u32[]{:S(2)}) async-start(bf16[4,256,768]{2,1,0:T(8,128)(2,1)} %shard_map.173), calls=%async_computation.2 | async-start | bytes 3145728 | tf_op jit(solution)/shard_map/all_to_all | solution.py:511
  42.5 21.8 %collective-permute-start.4 = (bf16[512,1024]{1,0:T(8,128)(2,1)S(1)}, bf16[512,1024]{1,0:T(8,128)(2,1)}, u32[]{:S(2)}, u32[]{:S(2)}) collective-permute-start(bf16[512,1024]{1,0:T(8,128)(2,1)S(1)} %get-tuple-element.70.normed_ref), channel_id=1, source_target_pairs={{0,1},{1,0},{2,3},{3,2},{4,5},{5,4},{6,7},{7,6},{8,9},{9,8},{10,11... | collective-permute-start | bytes 3145736 | tf_op jit(solution)/shard_map/ppermute | solution.py:449
  43.5 12.0 %collective-permute-start.5 = (bf16[256,768]{1,0:T(8,128)(2,1)S(1)}, bf16[256,768]{1,0:T(8,128)(2,1)S(1)}, u32[]{:S(2)}, u32[]{:S(2)}) collective-permute-start(bf16[256,768]{1,0:T(8,128)(2,1)S(1)} %bitcast.28), channel_id=1, source_target_pairs={{0,2},{2,4},{4,6},{6,0},{1,3},{3,5},{5,7},{7,1},{8,10},{10,12},{12... | collective-permute-start | bytes 1179656 | tf_op jit(solution)/shard_map/ppermute | solution.py:430
  44.6 19.7 %collective-permute-start.6 = (bf16[256,768]{1,0:T(8,128)(2,1)S(1)}, bf16[256,768]{1,0:T(8,128)(2,1)S(1)}, u32[]{:S(2)}, u32[]{:S(2)}) collective-permute-start(bf16[256,768]{1,0:T(8,128)(2,1)S(1)} %bitcast.29), channel_id=1, source_target_pairs={{0,4},{2,6},{4,0},{6,2},{1,5},{3,7},{5,1},{7,3},{8,12},{10,14},{12... | collective-permute-start | bytes 1179656 | tf_op jit(solution)/shard_map/ppermute | solution.py:430
  46.7 17.6 %collective-permute-start.7 = (bf16[256,768]{1,0:T(8,128)(2,1)S(1)}, bf16[256,768]{1,0:T(8,128)(2,1)S(1)}, u32[]{:S(2)}, u32[]{:S(2)}) collective-permute-start(bf16[256,768]{1,0:T(8,128)(2,1)S(1)} %bitcast.30), channel_id=1, source_target_pairs={{0,6},{2,0},{4,2},{6,4},{1,7},{3,1},{5,3},{7,5},{8,14},{10,8},{12,... | collective-permute-start | bytes 1179656 | tf_op jit(solution)/shard_map/ppermute | solution.py:430
  71.4 17.5 %collective-permute-start.9 = (bf16[1024,512]{1,0:T(8,128)(2,1)}, bf16[1024,512]{1,0:T(8,128)(2,1)}, u32[]{:S(2)}, u32[]{:S(2)}) collective-permute-start(bf16[1024,512]{1,0:T(8,128)(2,1)} %get-tuple-element.91.turned_ref), channel_id=1, source_target_pairs={{0,1},{1,0},{2,3},{3,2},{4,5},{5,4},{6,7},{7,6},{8,9},{9,8},{10,11... | collective-permute-start | bytes 3145736 | tf_op jit(solution)/shard_map/ppermute | solution.py:449
  72.4 2.2 %collective-permute-start.8 = (f32[8,1024]{1,0:T(8,128)S(1)}, f32[8,1024]{1,0:T(8,128)S(1)}, u32[]{:S(2)}, u32[]{:S(2)}) collective-permute-start(f32[8,1024]{1,0:T(8,128)S(1)} %get-tuple-element.73.mine_ref), channel_id=1, source_target_pairs={{0,1},{1,0},{2,3},{3,2},{4,5},{5,4},{6,7},{7,6},{8,9},{9,8},{10,11... | collective-permute-start | bytes 98312 | tf_op jit(solution)/shard_map/ppermute | solution.py:449
  75.4 13.5 %all-to-all-start.3 = ((f32[32,1,128]{2,1,0:T(1,128)}), f32[32,1,128]{2,1,0:T(1,128)S(1)}, u32[]{:S(2)}, u32[]{:S(2)}) async-start(f32[32,1,128]{2,1,0:T(1,128)} %get-tuple-element.75), calls=%async_computation.3 | async-start | bytes 32768 | tf_op jit(solution)/shard_map/all_to_all | solution.py:542
  95.5 27.3 %all-to-all-start.4 = ((bf16[4,256,768]{2,1,0:T(8,128)(2,1)}), bf16[4,256,768]{2,1,0:T(8,128)(2,1)}, u32[]{:S(2)}, u32[]{:S(2)}) async-start(bf16[4,256,768]{2,1,0:T(8,128)(2,1)} %get-tuple-element.94), calls=%async_computation.4 | async-start | bytes 3145728 | tf_op jit(solution)/shard_map/all_to_all | solution.py:569
  100.0 12.3 %collective-permute-start.14 = (bf16[512,1024]{1,0:T(8,128)(2,1)}, bf16[512,1024]{1,0:T(8,128)(2,1)}, u32[]{:S(2)}, u32[]{:S(2)}) collective-permute-start(bf16[512,1024]{1,0:T(8,128)(2,1)} %get-tuple-element.103), channel_id=1, source_target_pairs={{0,1},{1,0},{2,3},{3,2},{4,5},{5,4},{6,7},{7,6},{8,9},{9,8},{10,11... | collective-permute-start | bytes 3145736 | tf_op jit(solution)/shard_map/ppermute | solution.py:449
  102.0 15.9 %collective-permute-start.10 = (bf16[256,768]{1,0:T(8,128)(2,1)}, bf16[256,768]{1,0:T(8,128)(2,1)S(1)}, u32[]{:S(2)}, u32[]{:S(2)}) collective-permute-start(bf16[256,768]{1,0:T(8,128)(2,1)} %get-tuple-element.96), channel_id=1, source_target_pairs={{0,2},{2,4},{4,6},{6,0},{1,3},{3,5},{5,7},{7,1},{8,10},{10,12},{12... | collective-permute-start | bytes 1179656 | tf_op jit(solution)/shard_map/ppermute | solution.py:436
  102.3 20.0 %collective-permute-start.11 = (bf16[256,768]{1,0:T(8,128)(2,1)}, bf16[256,768]{1,0:T(8,128)(2,1)S(1)}, u32[]{:S(2)}, u32[]{:S(2)}) collective-permute-start(bf16[256,768]{1,0:T(8,128)(2,1)} %get-tuple-element.97), channel_id=1, source_target_pairs={{0,4},{2,6},{4,0},{6,2},{1,5},{3,7},{5,1},{7,3},{8,12},{10,14},{12... | collective-permute-start | bytes 1179656 | tf_op jit(solution)/shard_map/ppermute | solution.py:436
  104.4 18.4 %collective-permute-start.12 = (bf16[256,768]{1,0:T(8,128)(2,1)S(1)}, bf16[256,768]{1,0:T(8,128)(2,1)S(1)}, u32[]{:S(2)}, u32[]{:S(2)}) collective-permute-start(bf16[256,768]{1,0:T(8,128)(2,1)S(1)} %get-tuple-element.98), channel_id=1, source_target_pairs={{0,6},{2,0},{4,2},{6,4},{1,7},{3,1},{5,3},{7,5},{8,14},{10,8},{12,... | collective-permute-start | bytes 1179656 | tf_op jit(solution)/shard_map/ppermute | solution.py:436
  125.7 15.3 %all-to-all-start.5 = ((bf16[4,80,768]{2,1,0:T(8,128)(2,1)}), bf16[4,80,768]{2,1,0:T(8,128)(2,1)S(1)}, u32[]{:S(2)}, u32[]{:S(2)}) async-start(bf16[4,80,768]{2,1,0:T(8,128)(2,1)} %get-tuple-element.109), calls=%async_computation.5 | async-start | bytes 983040 | tf_op jit(solution)/shard_map/all_to_all | solution.py:587
  130.2 5.4 %collective-permute-start.17 = (bf16[64,768]{1,0:T(8,128)(2,1)S(1)}, bf16[64,768]{1,0:T(8,128)(2,1)S(1)}, u32[]{:S(2)}, u32[]{:S(2)}) collective-permute-start(bf16[64,768]{1,0:T(8,128)(2,1)S(1)} %get-tuple-element.114), channel_id=1, source_target_pairs={{0,6},{2,0},{4,2},{6,4},{1,7},{3,1},{5,3},{7,5},{8,14},{10,8},{12,... | collective-permute-start | bytes 294920 | tf_op jit(solution)/shard_map/ppermute | solution.py:436
  133.2 5.1 %collective-permute-start.16 = (bf16[64,768]{1,0:T(8,128)(2,1)S(1)}, bf16[64,768]{1,0:T(8,128)(2,1)S(1)}, u32[]{:S(2)}, u32[]{:S(2)}) collective-permute-start(bf16[64,768]{1,0:T(8,128)(2,1)S(1)} %get-tuple-element.113), channel_id=1, source_target_pairs={{0,4},{2,6},{4,0},{6,2},{1,5},{3,7},{5,1},{7,3},{8,12},{10,14},{12... | collective-permute-start | bytes 294920 | tf_op jit(solution)/shard_map/ppermute | solution.py:436
  133.6 7.4 %collective-permute-start.15 = (bf16[64,768]{1,0:T(8,128)(2,1)S(1)}, bf16[64,768]{1,0:T(8,128)(2,1)S(1)}, u32[]{:S(2)}, u32[]{:S(2)}) collective-permute-start(bf16[64,768]{1,0:T(8,128)(2,1)S(1)} %get-tuple-element.112), channel_id=1, source_target_pairs={{0,2},{2,4},{4,6},{6,0},{1,3},{3,5},{5,7},{7,1},{8,10},{10,12},{12... | collective-permute-start | bytes 294920 | tf_op jit(solution)/shard_map/ppermute | solution.py:436
  141.8 16.7 %all-to-all-start.6 = ((bf16[16,4,1536]{2,1,0:T(4,128)(2,1)}), bf16[16,4,1536]{2,1,0:T(4,128)(2,1)S(1)}, u32[]{:S(2)}, u32[]{:S(2)}) async-start(bf16[16,4,1536]{2,1,0:T(4,128)(2,1)} %reshape.88), calls=%async_computation.6 | async-start | bytes 393216 | tf_op jit(solution)/shard_map/all_to_all | solution.py:599
  (12 other events, 159.9 us)

commit v5 on v4

--- a/solution.py
+++ b/solution.py
@@ -18,6 +18,9 @@
 D = 1024
 ROWS = PAIRS * SEQ
 BOTH = 2 * PAIRS
+LOW = 384
+WA = 512 + LOW
+WB = 1024 - LOW
 F32 = jnp.float32
 BF16 = jnp.bfloat16
 SM = pl.BlockSpec(memory_space=pltpu.SMEM)
@@ -41,22 +44,15 @@
     return pl.BlockSpec(shape, lambda i: (0,) * len(shape), pipeline_mode=pl.Buffered(1))
 
 
-def block(cuts, key, shape):
-    if key in cuts:
-        return pl.BlockSpec(cuts[key], lambda i: (i,) + (0,) * (len(shape) - 1))
-    return whole(shape)
-
-
-def call(body, scalars, arrays, outs, scratch=(), flops=0, grant=52, cuts=()):
+def call(body, scalars, arrays, outs, scratch=(), flops=0, grant=52):
     moved = sum(a.size * a.dtype.itemsize for a in arrays)
     moved += sum(int(np.prod(o)) * np.dtype(d).itemsize for o, d in outs)
     return pl.pallas_call(
         body,
-        grid=(4 if cuts else 1,),
+        grid=(1,),
         out_shape=[jax.ShapeDtypeStruct(o, d) for o, d in outs],
-        in_specs=[SM] * len(scalars)
-        + [block(cuts, k, a.shape) for k, a in enumerate(arrays)],
-        out_specs=[block(cuts, -1 - k, o) for k, (o, _) in enumerate(outs)],
+        in_specs=[SM] * len(scalars) + [whole(a.shape) for a in arrays],
+        out_specs=[whole(o) for o, _ in outs],
         scratch_shapes=[pltpu.VMEM(o, d) for o, d in scratch],
         compiler_params=pltpu.CompilerParams(vmem_limit_bytes=grant << 20),
         cost_estimate=pl.CostEstimate(flops=flops, bytes_accessed=moved, transcendentals=0),
@@ -110,9 +106,9 @@
         wide, tall = slice(h * 256, h * 256 + 256), h * 512
         out_ref[0, h, :, 0:256] = k_ref[:, wide]
         out_ref[0, h, :, 256:512] = v_ref[:, wide]
-        out_ref[0, h, :, 512:768] = o_ref[:, tall : tall + 256]
-        out_ref[0, h, :, 768:1280] = q_ref[:, tall : tall + 512]
-        out_ref[0, h, :, 1280:1536] = o_ref[:, tall + 256 : tall + 512]
+        out_ref[0, h, :, 512:WA] = o_ref[:, tall : tall + LOW]
+        out_ref[0, h, :, WA : WA + 512] = q_ref[:, tall : tall + 512]
+        out_ref[0, h, :, WA + 512 : 1536] = o_ref[:, tall + LOW : tall + 512]
     for z in range(1, 8):
         out_ref[z] = out_ref[0]
 
@@ -141,8 +137,8 @@
     a_refs, out_ref, slab_scr = refs[0:4], refs[4], refs[5]
     x = at_ref[1]
     for d in range(4):
-        slab_scr[:, pl.ds(lax.rem(x - d + 4, 4), 1)] = a_refs[d][...].reshape(8, 1, 8, 768)
-    slab = slab_scr[...].reshape(256, 768)
+        slab_scr[:, pl.ds(lax.rem(x - d + 4, 4), 1)] = a_refs[d][...].reshape(8, 1, 8, WA)
+    slab = slab_scr[...].reshape(256, WA)
     for y in range(4):
         out_ref[y] = slab
 
@@ -158,14 +154,10 @@
     mask, even = block_mask()
     lane = lax.broadcasted_iota(jnp.int32, (8 * BOTH, SEQ), 1)
     for side, rows_ref in enumerate((normed_ref, other_ref)):
-
-        @pl.loop(0, 2)
-        def _(i):
-            src = pl.ds(pl.multiple_of(i * 256, 256), 256)
-            dst = pl.ds(pl.multiple_of(side * ROWS + i * 256, 256), 256)
-            kv = dot(rows_ref[src, :], kv_ref[:, 0:512])
-            kproj_ref[dst, :] = kv[:, 0:256]
-            vcast_ref[dst, :] = kv[:, 256:512].astype(BF16)
+        here = slice(side * ROWS, (side + 1) * ROWS)
+        kv = dot(rows_ref[...], kv_ref[:, 0:512])
+        kproj_ref[here, :] = kv[:, 0:256]
+        vcast_ref[here, :] = kv[:, 256:512].astype(BF16)
 
     q = jnp.zeros((8, 512), F32)
     for d in range(4):
@@ -201,9 +193,11 @@
         ctx_scr[p : p + 1, :] = from_blocks(c, mask, even)
     ctx_ref[...] = ctx_scr[...].astype(BF16)
     for d in range(4):
-        turn_scr[:, pl.ds(lax.rem(x - d + 4, 4), 1)] = q_refs[d][:, 512:768].reshape(32, 1, 8, 256)
-    o_ref[:, 0:256] = kv_ref[:, 512:768]
-    o_ref[:, 256:512] = turn_scr[...].reshape(1024, 256)
+        turn_scr[:, pl.ds(lax.rem(x - d + 4, 4), 1)] = q_refs[d][:, 512:WB].reshape(
+            32, 1, 8, 512 - LOW
+        )
+    o_ref[:, 0:LOW] = kv_ref[:, 512:WA]
+    o_ref[:, LOW:512] = turn_scr[...].reshape(1024, 512 - LOW)
     out_ref[...] = dot(ctx_ref[...], o_ref[...], LAST)
 
 
@@ -295,11 +289,8 @@
     for d in range(4):
         last_ref[:, block_at(at_ref[1], -d, 256)] = dot(gqb, q_refs[d][:, 0:512], LAST)
 
-    @pl.loop(0, 2)
-    def _(i):
-        src = pl.ds(pl.multiple_of(ROWS + i * 256, 256), 256)
-        gn = dot(gkv_ref[src, :].astype(BF16), kv_ref[:, 0:512], LAST)
-        send_ref[pl.ds(pl.multiple_of(i * 256, 256), 256), :] = gn.astype(BF16)
+    gn = dot(gkv_ref[ROWS : 2 * ROWS, :].astype(BF16), kv_ref[:, 0:512], LAST)
+    send_ref[...] = gn.astype(BF16)
 
 
 def weight_body(
@@ -318,52 +309,43 @@
     *refs,
 ):
     out_a, outs_b, loss_ref, skv_ref, g_ref, sr_ref = refs[0], refs[1:5], *refs[5:9]
-    srow_scr, sturn_scr, sq_scr = refs[9:]
+    srow_scr, sturn_scr, sq_scr, b_scr = refs[9:]
     x = at_ref[1]
-    i = pl.program_id(0)
-
-    @pl.when(i == 0)
-    def _():
-        lane = lax.broadcasted_iota(jnp.int32, (1, HW), 1)
-
-        def pick(v, i):
-            return jnp.sum(jnp.where(lane == i, v, 0.0), axis=-1, keepdims=True)
-
-        t = tot_ref[0]
-        for i in range(1, 32):
-            t = t + tot_ref[i]
-        ts, tt, cr = pick(t, 0), pick(t, 1), pick(t, 2)
-        loss_ref[...] = jnp.broadcast_to(cr / tt - jnp.log(tt) + jnp.log(ts), (8, HW))
-        row = lax.broadcasted_iota(jnp.int32, (8, HW), 0)
-        g = GRAD_SCALE * (jnp.exp(score_ref[...]) / ts - jnp.exp(teach_ref[...] / 2.0) / tt)
-        gcol = g[:, 0:1]
-        sr = gr_ref[...] * gcol
-        sr_ref[...] = sr
-        g_ref[...] = g
-        sq_scr[...] = (gq_ref[...] * gcol).astype(BF16)
-        srow_scr[...] = sr.astype(BF16)
-        sturn_scr[...] = (grturn_ref[...] * gcol).astype(BF16)
-        for p in range(BOTH):
-            rows = slice(p * SEQ, (p + 1) * SEQ)
-            skv_ref[rows, :] = (gkv_ref[rows, :] * gcol[p : p + 1, :]).astype(BF16)
-
-    rows = pl.ds(pl.multiple_of(i * 256, 256), 256)
+    lane = lax.broadcasted_iota(jnp.int32, (1, HW), 1)
+
+    def pick(v, i):
+        return jnp.sum(jnp.where(lane == i, v, 0.0), axis=-1, keepdims=True)
+
+    t = tot_ref[0]
+    for i in range(1, 32):
+        t = t + tot_ref[i]
+    ts, tt, cr = pick(t, 0), pick(t, 1), pick(t, 2)
+    loss_ref[...] = jnp.broadcast_to(cr / tt - jnp.log(tt) + jnp.log(ts), (8, HW))
+    row = lax.broadcasted_iota(jnp.int32, (8, HW), 0)
+    g = GRAD_SCALE * (jnp.exp(score_ref[...]) / ts - jnp.exp(teach_ref[...] / 2.0) / tt)
+    gcol = g[:, 0:1]
+    sr = gr_ref[...] * gcol
+    sr_ref[...] = sr
+    g_ref[...] = g
+    sq_scr[...] = (gq_ref[...] * gcol).astype(BF16)
+    srow_scr[...] = sr.astype(BF16)
+    sturn_scr[...] = (grturn_ref[...] * gcol).astype(BF16)
+    for p in range(BOTH):
+        rows = slice(p * SEQ, (p + 1) * SEQ)
+        skv_ref[rows, :] = (gkv_ref[rows, :] * gcol[p : p + 1, :]).astype(BF16)
+
     kv = dot(turned_ref[...], skv_ref[0:ROWS, :]) + dot(
         turned_other_ref[...], skv_ref[ROWS : 2 * ROWS, :]
     )
-    o_low = dot(srow_scr[:, rows], ctx_ref[:, 0:256], FIRST)
-    rows_x = block_at(x, i, 256)
-    q = dot(nlast_ref[:, rows_x], sq_scr[...], FIRST)
-    o_high = dot(sturn_scr[:, rows_x], ctx_ref[:, 256:512], FIRST)
-    out_a[0, :, 0:512] = kv.astype(BF16)
-    out_a[0, :, 512:768] = o_low.astype(BF16)
-    q, o_high = q.astype(BF16), o_high.astype(BF16)
+    out_a[:, :, 0:512] = kv.astype(BF16).reshape(4, 256, 512)
+    o_low = dot(srow_scr[...], ctx_ref[:, 0:LOW], FIRST)
+    out_a[:, :, 512:WA] = o_low.astype(BF16).reshape(4, 256, LOW)
+    q = dot(nlast_ref[...], sq_scr[...], FIRST)
+    b_scr[:, :, 0:512] = q.astype(BF16).reshape(4, 256, 512)
+    o_high = dot(sturn_scr[...], ctx_ref[:, LOW:512], FIRST)
+    b_scr[:, :, 512:WB] = o_high.astype(BF16).reshape(4, 256, 512 - LOW)
     for d in range(4):
-
-        @pl.when(i == d)
-        def _():
-            outs_b[d][:, 0:512] = q
-            outs_b[d][:, 512:768] = o_high
+        outs_b[d][...] = b_scr[lax.rem(x + d, 4)]
 
 
 def middle_body(at_ref, loss_ref, got_a_ref, *refs):
@@ -374,19 +356,19 @@
     for d in range(1, 4):
         total_a = total_a + got_a_ref[d].astype(F32)
         total_b = total_b + b_refs[d][...].astype(F32)
-    out_b[:, 0:64, :] = total_b.reshape(4, 64, 768).astype(BF16)
-    rest = jnp.broadcast_to(loss_ref[0:1, 0:1], (16, 768))
-    lane = lax.broadcasted_iota(jnp.int32, (16, 768), 1)
-    parts = jnp.zeros((16, 768), F32)
+    out_b[:, 0:64, :] = total_b.reshape(4, 64, WB).astype(BF16)
+    rest = jnp.broadcast_to(loss_ref[0:1, 0:1], (16, WB))
+    lane = lax.broadcasted_iota(jnp.int32, (16, WB), 1)
+    parts = jnp.zeros((16, WB), F32)
     for i in range(3):
         part = rest.astype(BF16).astype(F32)
         parts = jnp.where(lane == i, part, parts)
         rest = rest - part
     for y in range(4):
         out_b[y, 64:80, :] = parts.astype(BF16)
-    a_scr[...] = total_a.reshape(8, 4, 8, 768)
+    a_scr[...] = total_a.reshape(8, 4, 8, WA)
     for d in range(4):
-        out_a[d][...] = a_scr[:, pl.ds(lax.rem(x + d, 4), 1)].reshape(64, 768).astype(BF16)
+        out_a[d][...] = a_scr[:, pl.ds(lax.rem(x + d, 4), 1)].reshape(64, WA).astype(BF16)
 
 
 def hidden_body(len_ref, h_ref, gain_ref, skv_ref, g_ref, last_ref, other_ref, sr_ref, kv_ref, got_ref, out_ref):
@@ -414,9 +396,9 @@
             total = total + rec_ref[z, h].astype(F32)
         gk_ref[:, h * 256 : h * 256 + 256] = total[:, 0:256]
         gv_ref[:, h * 256 : h * 256 + 256] = total[:, 256:512]
-        go_ref[:, h * 512 : h * 512 + 256] = total[:, 512:768]
-        gq_ref[:, h * 512 : h * 512 + 512] = total[:, 768:1280]
-        go_ref[:, h * 512 + 256 : h * 512 + 512] = total[:, 1280:1536]
+        go_ref[:, h * 512 : h * 512 + LOW] = total[:, 512:WA]
+        gq_ref[:, h * 512 : h * 512 + 512] = total[:, WA : WA + 512]
+        go_ref[:, h * 512 + LOW : h * 512 + 512] = total[:, WA + 512 : 1536]
 
 
 def everyone(x, axes, count):
@@ -499,16 +481,16 @@
     column, normed, turned, pack = lax.optimization_barrier((column, normed, turned, pack))
     other = swap(normed)
     got = swap(pack)
-    slab_b = everyone(column[:, 768:1536], "pb", 4).reshape(256, 768)
-    ring_a = from_ring(column[:, 0:768], "x")
-    (slab_a,) = call(arrange_body, [at], ring_a, [((4, 256, 768), BF16)], [((8, 4, 8, 768), BF16)])
+    slab_b = everyone(column[:, WA:1536], "pb", 4).reshape(256, WB)
+    ring_a = from_ring(column[:, 0:WA], "x")
+    (slab_a,) = call(arrange_body, [at], ring_a, [((4, 256, WA), BF16)], [((8, 4, 8, WA), BF16)], grant=10)
     slab_a, slab_b, got = lax.optimization_barrier((slab_a, slab_b, got))
     packed = jnp.concatenate([pack, got], axis=0)
     xlast = packed[:, 0:1024]
     nlast = packed[:, 1024:2048].astype(BF16)
     lens_both = packed[:, 2048].astype(jnp.int32)
     teach = packed[:, 2048 + HW :]
-    kvo = lax.all_to_all(slab_a, "pb", 0, 0, tiled=True).reshape(1024, 768)
+    kvo = lax.all_to_all(slab_a, "pb", 0, 0, tiled=True).reshape(1024, WA)
     qo = from_ring(slab_b, "x")
 
     kproj, krot, vcast, qproj, qrot, attn, ctx, attended, oa = call(
@@ -526,7 +508,7 @@
             ((8, D), F32),
             ((D, 512), BF16),
         ],
-        [((8, 512), F32), ((8, 512), F32), ((32, 4, 8, 256), BF16), ((8 * BOTH, SEQ), F32)],
+        [((8, 512), F32), ((8, 512), F32), ((32, 4, 8, 512 - LOW), BF16), ((8 * BOTH, SEQ), F32)],
         flops=1_100_000_000,
     )
     ctx, turned_late = lax.optimization_barrier((ctx, turned))
@@ -553,17 +535,16 @@
     last = chunk_back(last)
     got = swap(send)
 
-    pieces = ((4, 256, 768), BF16)
+    pieces = ((4, 256, WA), BF16)
     chip_a, *rest = call(
         weight_body,
         [at],
         [totals, score, teach, gkv, gq, gr, grturn, turned, turned_other, nlast, ctx],
         [pieces]
-        + [((256, 768), BF16)] * 4
+        + [((256, WB), BF16)] * 4
         + [((8, HW), F32), ((ROWS * 2, 512), BF16), ((8, HW), F32), ((8, D), F32)],
-        [((8, D), BF16), ((8, D), BF16), ((8, 512), BF16)],
+        [((8, D), BF16), ((8, D), BF16), ((8, 512), BF16), ((4, 256, WB), BF16)],
         flops=1_100_000_000,
-        cuts={7: (256, 512), 8: (256, 512), -1: (1, 256, 768)},
     )
     chip_b, (loss, skv, g, sr) = rest[0:4], rest[4:]
     got_a = lax.all_to_all(chip_a, "pb", 0, 0, tiled=True)
@@ -580,8 +561,9 @@
         middle_body,
         [at],
         [loss, got_a, *got_b],
-        [((64, 768), BF16)] * 4 + [((4, 80, 768), BF16)],
-        [((8, 4, 8, 768), F32)],
+        [((64, WA), BF16)] * 4 + [((4, 80, WB), BF16)],
+        [((8, 4, 8, WA), F32)],
+        grant=52,
     )
     done_a = along_ring(mid_a, "x")
     done_b = lax.all_to_all(mid_b, "pb", 0, 0, tiled=True)

time: 161 us -> 162 us (level)
  Pallas kernels: 36.9 us -> 34.4 us
  starting transfers between devices: 61.5 us -> 63.8 us
    ppermute x6, waiting for transfers between devices: 12.1 us -> 4.01 us  [along_ring(): lax.ppermute(pieces[d], axis, [(i, (i + d) % 4) for i in range(4)])]
    all_to_all x1, waiting for transfers between devices: 0.01 us -> 4.64 us  [shards(): done_b = lax.all_to_all(mid_b, 'pb', 0, 0, tiled=True)]
    all_to_all x1, starting transfers between devices: 6.39 us -> 10.2 us  [shards(): lax.all_to_all(part.reshape(16, 4, 1536), ('z', 'c'), 0, 0, tiled=True)]
    all_to_all x1, waiting for transfers between devices: 0.01 us -> 3.61 us  [shards(): kvo = lax.all_to_all(slab_a, 'pb', 0, 0, tiled=True).reshape(1024, WA)]
    all_to_all x1, waiting for transfers between devices: 0.01 us -> 2.44 us  [shards(): got_a = lax.all_to_all(chip_a, 'pb', 0, 0, tiled=True)]
    pallas_call x10, Pallas kernels: 36.9 us -> 34.4 us  [call(): pl.pallas_call(body, grid=(1,), out_shape=[jax.ShapeDtypeStruct(o, d) for...]
    ppermute x6, waiting for transfers between devices: 19.2 us -> 17.2 us  [from_ring(): lax.ppermute(x, axis, [(i, (i + d) % 4) for i in range(4)])]
  transfers between devices with their start and end apart: 25 -> 25, of which waited for: 13 -> 16; matrix products, arithmetic and copies ran while one was open for 5% -> 5% of each run, Pallas kernels for 11% -> 11%
where the time goes in v5:
time: 162 us; the launch traced here: 161 us
  starting transfers between devices  63.8 us (39%)
  waiting for transfers between devices  47.5 us (29%)
  Pallas kernels  34.4 us (21%)
  local copies, waits for them, and re-layouts  10.3 us (6%)
  between operations  4.63 us (3%)
    pallas_call x10, Pallas kernels, call(): pl.pallas_call(body, grid=(1,), out_shape=[jax.ShapeDtypeStruct(o, d) for...  34.4 us
    ppermute x6, waiting for transfers between devices, from_ring(): lax.ppermute(x, axis, [(i, (i + d) % 4) for i in range(4)])  17.2 us
    all_to_all x1, starting transfers between devices, shards(): lax.all_to_all(part.reshape(16, 4, 1536), ('z', 'c'), 0, 0, tiled=True)  10.2 us
    all_to_all x1, starting transfers between devices, shards(): lax.all_to_all(both_halves, ('z', 'c'), 0, 0, tiled=True).reshape(64, 1536)  9.98 us
    ppermute x6, starting transfers between devices, from_ring(): lax.ppermute(x, axis, [(i, (i + d) % 4) for i in range(4)])  9.36 us
    all_to_all x1, waiting for transfers between devices, shards(): lax.all_to_all(part.reshape(16, 4, 1536), ('z', 'c'), 0, 0, tiled=True)  7.02 us
    ppermute x6, starting transfers between devices, along_ring(): lax.ppermute(pieces[d], axis, [(i, (i + d) % 4) for i in range(4)])  6.91 us
    ppermute x6, starting transfers between devices, swap(): return lax.ppermute(x, 'c', [(0, 1), (1, 0)])  6.4 us
  transfers between devices with their start and end apart: 25, of which 16 were waited for; matrix products, arithmetic and copies ran while one was open for 5% of the time, Pallas kernels for 11%

profile of v5, /device:TPU:1, one launch (start us, length us, event | category | flops | bytes accessed | tf_op | source)
XLA Modules:
  0.0 161.2 jit_solution(17091546781562278108)
XLA Ops:
  2.1 10.0 %all-to-all-start = ((bf16[16,4,1536]{2,1,0:T(4,128)(2,1)}), bf16[16,4,1536]{2,1,0:T(4,128)(2,1)S(1)}, u32[]{:S(2)}, u32[]{:S(2)}) async-start(bf16[16,4,1536]{2,1,0:T(4,128)(2,1)} %bitcast.44), calls=%async_computation | async-start | bytes 393216 | tf_op jit(solution)/shard_map/all_to_all | solution.py:462
  13.4 2.9 %shard_map.172 = (bf16[512,1024]{1,0:T(8,128)(2,1)S(1)}, bf16[1024,512]{1,0:T(8,128)(2,1)}, bf16[8,1024]{1,0:T(8,128)(2,1)S(1)}, f32[8,1024]{1,0:T(8,128)S(1)}) custom-call(s32[4]{0:T(128)S(1)} %bitcast.40, bf16[512,1024]{1,0:T(8,128)(2,1)} %bitcast.26, f32[1,1024]{1,0:T(1,128)S(1)} %bitcast.34), custom_call_target="tpu_custom_call" | custom-call | flops 10000000 | bytes 3198976 | tf_op jit(solution)/shard_map/pallas_call | solution.py:50
  17.4 5.1 %all-to-all-done = bf16[16,4,1536]{2,1,0:T(4,128)(2,1)S(1)} async-done(((bf16[16,4,1536]{2,1,0:T(4,128)(2,1)}), bf16[16,4,1536]{2,1,0:T(4,128)(2,1)S(1)}, u32[]{:S(2)}, u32[]{:S(2)}) %all-to-all-start) | async-done | bytes 196640 | tf_op jit(solution)/shard_map/all_to_all | solution.py:462
  23.2 4.2 %all-to-all-start.1 = ((bf16[4,64,640]{2,1,0:T(8,128)(2,1)}), bf16[4,64,640]{2,1,0:T(8,128)(2,1)S(1)}, u32[]{:S(2)}, u32[]{:S(2)}) async-start(bf16[4,64,640]{2,1,0:T(8,128)(2,1)} %broadcast_in_dim.32), calls=%async_computation.1 | async-start | bytes 655360 | tf_op jit(solution)/shard_map/all_to_all | solution.py:405
  28.7 2.5 %collective-permute-start.1 = (bf16[64,896]{1,0:T(8,128)(2,1)S(1)}, bf16[64,896]{1,0:T(8,128)(2,1)S(1)}, u32[]{:S(2)}, u32[]{:S(2)}) collective-permute-start(bf16[64,896]{1,0:T(8,128)(2,1)S(1)} %slice.53.refs_0_), channel_id=1, source_target_pairs={{0,4},{2,6},{4,0},{6,2},{1,5},{3,7},{5,1},{7,3},{8,12},{10,14},{12... | collective-permute-start | bytes 344072 | tf_op jit(solution)/shard_map/ppermute | solution.py:412
  33.5 3.4 %collective-permute-done.1.refs_2_ = bf16[64,896]{1,0:T(8,128)(2,1)S(1)} collective-permute-done((bf16[64,896]{1,0:T(8,128)(2,1)S(1)}, bf16[64,896]{1,0:T(8,128)(2,1)S(1)}, u32[]{:S(2)}, u32[]{:S(2)}) %collective-permute-start.1) | collective-permute-done | bytes 114720 | tf_op jit(solution)/shard_map/ppermute | solution.py:412
  38.9 4.5 %all-to-all-start.2 = ((bf16[4,256,896]{2,1,0:T(8,128)(2,1)}), bf16[4,256,896]{2,1,0:T(8,128)(2,1)}, u32[]{:S(2)}, u32[]{:S(2)}) async-start(bf16[4,256,896]{2,1,0:T(8,128)(2,1)} %shard_map.173), calls=%async_computation.2 | async-start | bytes 3670016 | tf_op jit(solution)/shard_map/all_to_all | solution.py:493
  49.0 6.0 %collective-permute-done.5.refs_1_.refs_2_ = bf16[256,640]{1,0:T(8,128)(2,1)S(1)} collective-permute-done((bf16[256,640]{1,0:T(8,128)(2,1)S(1)}, bf16[256,640]{1,0:T(8,128)(2,1)S(1)}, u32[]{:S(2)}, u32[]{:S(2)}) %collective-permute-start.5) | collective-permute-done | bytes 327712 | tf_op jit(solution)/shard_map/ppermute | solution.py:412
  55.0 7.5 %collective-permute-done.6.refs_2_.refs_3_ = bf16[256,640]{1,0:T(8,128)(2,1)S(1)} collective-permute-done((bf16[256,640]{1,0:T(8,128)(2,1)S(1)}, bf16[256,640]{1,0:T(8,128)(2,1)S(1)}, u32[]{:S(2)}, u32[]{:S(2)}) %collective-permute-start.6) | collective-permute-done | bytes 327712 | tf_op jit(solution)/shard_map/ppermute | solution.py:412
  62.5 3.6 %all-to-all-done.2 = bf16[4,256,896]{2,1,0:T(8,128)(2,1)} async-done(((bf16[4,256,896]{2,1,0:T(8,128)(2,1)}), bf16[4,256,896]{2,1,0:T(8,128)(2,1)}, u32[]{:S(2)}, u32[]{:S(2)}) %all-to-all-start.2) | async-done | bytes 1835040 | tf_op jit(solution)/shard_map/all_to_all | solution.py:493
  66.1 6.2 %shard_map.174 = (f32[1024,256]{1,0:T(8,128)}, bf16[1024,256]{1,0:T(8,128)(2,1)}, bf16[1024,256]{1,0:T(8,128)(2,1)}, f32[8,512]{1,0:T(8,128)S(1)}, bf16[8,512]{1...) custom-call(s32[2]{0:T(128)S(1)} %pad_add_fusion.at_ref, ...), custom_call_target="tpu_custom_call" | custom-call | flops 1100000000 | bytes 8634368 | tf_op jit(solution)/shard_map/pallas_call | solution.py:50
  77.2 4.3 %all-to-all-start.3 = ((f32[32,1,128]{2,1,0:T(1,128)}), f32[32,1,128]{2,1,0:T(1,128)S(1)}, u32[]{:S(2)}, u32[]{:S(2)}) async-start(f32[32,1,128]{2,1,0:T(1,128)} %get-tuple-element.75), calls=%async_computation.3 | async-start | bytes 32768 | tf_op jit(solution)/shard_map/all_to_all | solution.py:524
  81.5 6.7 %shard_map.176 = (f32[1024,512]{1,0:T(8,128)}, f32[8,512]{1,0:T(8,128)S(1)}, f32[8,1024]{1,0:T(8,128)S(1)}, f32[8,1024]{1,0:T(8,128)S(1)}, bf16[512,1024]{1,0:T(8,128)(2,1)}) custom-call(s32[2]{0:T(128)S(1)} %pad_add_fusion.at_ref, s32[8]{0:T(128)S(1)} %convert_reduce_fusion.len_ref, bf16[1024,256]{1,0:T(8,128)(2,1)} %get-tuple-element.77.krot_ref, ...), custom_call_target="tpu_custom_call" | custom-call | flops 200000000 | bytes 9752576 | tf_op jit(solution)/shard_map/pallas_call | solution.py:50
  89.8 5.3 %shard_map.177 = (bf16[4,256,896]{2,1,0:T(8,128)(2,1)}, bf16[256,640]{1,0:T(8,128)(2,1)S(1)}, bf16[256,640]{1,0:T(8,128)(2,1)S(1)}, bf16[256,640]{1,0:T(8,128)(2...) custom-call(s32[2]{0:T(128)S(1)} %pad_add_fusion.at_ref, ...), custom_call_target="tpu_custom_call" | custom-call | flops 1100000000 | bytes 8560640 | tf_op jit(solution)/shard_map/pallas_call | solution.py:50
  95.1 4.4 %all-to-all-start.4 = ((bf16[4,256,896]{2,1,0:T(8,128)(2,1)}), bf16[4,256,896]{2,1,0:T(8,128)(2,1)}, u32[]{:S(2)}, u32[]{:S(2)}) async-start(bf16[4,256,896]{2,1,0:T(8,128)(2,1)} %get-tuple-element.94), calls=%async_computation.4 | async-start | bytes 3670016 | tf_op jit(solution)/shard_map/all_to_all | solution.py:550
  105.6 2.2 %copy.28 = f32[8,32,4,8]{3,2,1,0:T(4,128)} copy(f32[8,32,4,8]{3,1,2,0:T(8,128)} %bitcast.41) | data formatting | bytes 65536 | tf_op jit(solution)/shard_map/transpose | solution.py:427
  111.2 5.6 %shard_map.178 = bf16[512,1024]{1,0:T(8,128)(2,1)} custom-call(s32[8]{0:T(128)S(1)} %convert_reduce_fusion.len_ref, bf16[512,1024]{1,0:T(8,128)(2,1)S(1)} %bitcast.27, f32[1,1024]{1,0:T(1,128)S(1)} %bitcast.35, bf16[1024,512]{1,0:T(8,128)(2,1)} %get-tuple-element.99.skv_ref, f32[8,128]{1,0:T(8,128)S(1)} %get-tuple-element.100.g_ref, ...), custom_call_target="tpu_custom_call" | custom-call | flops 600000000 | bytes 6135808 | tf_op jit(solution)/shard_map/pallas_call | solution.py:50
  119.2 2.4 %all-to-all-done.4.got_a_ref = bf16[4,256,896]{2,1,0:T(8,128)(2,1)} async-done(((bf16[4,256,896]{2,1,0:T(8,128)(2,1)}), bf16[4,256,896]{2,1,0:T(8,128)(2,1)}, u32[]{:S(2)}, u32[]{:S(2)}) %all-to-all-start.4) | async-done | bytes 1835040 | tf_op jit(solution)/shard_map/all_to_all | solution.py:550
  121.6 2.9 %shard_map.179 = (bf16[64,896]{1,0:T(8,128)(2,1)S(1)}, bf16[64,896]{1,0:T(8,128)(2,1)S(1)}, bf16[64,896]{1,0:T(8,128)(2,1)S(1)}, bf16[64,896]{1,0:T(8,128)(2,1)S(1)}, bf16[4,80,640]{2,1,0:T(8,128)(2,1)}) custom-call(s32[2]{0:T(128)S(1)} %pad_add_fusion.at_ref, f32[8,128]{1,0:T(8,128)S(1)} %get-tuple-element.93.loss_ref, ...), custom_call_target="tpu_custom_call" | custom-call | bytes 4018176 | tf_op jit(solution)/shard_map/pallas_call | solution.py:50
  124.5 2.4 %collective-permute-start.17 = (bf16[64,896]{1,0:T(8,128)(2,1)S(1)}, bf16[64,896]{1,0:T(8,128)(2,1)S(1)}, u32[]{:S(2)}, u32[]{:S(2)}) collective-permute-start(bf16[64,896]{1,0:T(8,128)(2,1)S(1)} %get-tuple-element.114), channel_id=1, source_target_pairs={{0,6},{2,0},{4,2},{6,4},{1,7},{3,1},{5,3},{7,5},{8,14},{10,8},{12,... | collective-permute-start | bytes 344072 | tf_op jit(solution)/shard_map/ppermute | solution.py:418
  128.3 3.5 %all-to-all-start.5 = ((bf16[4,80,640]{2,1,0:T(8,128)(2,1)}), bf16[4,80,640]{2,1,0:T(8,128)(2,1)S(1)}, u32[]{:S(2)}, u32[]{:S(2)}) async-start(bf16[4,80,640]{2,1,0:T(8,128)(2,1)} %get-tuple-element.109), calls=%async_computation.5 | async-start | bytes 819200 | tf_op jit(solution)/shard_map/all_to_all | solution.py:569
  133.4 4.6 %all-to-all-done.5 = bf16[4,80,640]{2,1,0:T(8,128)(2,1)S(1)} async-done(((bf16[4,80,640]{2,1,0:T(8,128)(2,1)}), bf16[4,80,640]{2,1,0:T(8,128)(2,1)S(1)}, u32[]{:S(2)}, u32[]{:S(2)}) %all-to-all-start.5) | async-done | bytes 409632 | tf_op jit(solution)/shard_map/all_to_all | solution.py:569
  138.8 10.2 %all-to-all-start.6 = ((bf16[16,4,1536]{2,1,0:T(4,128)(2,1)}), bf16[16,4,1536]{2,1,0:T(4,128)(2,1)S(1)}, u32[]{:S(2)}, u32[]{:S(2)}) async-start(bf16[16,4,1536]{2,1,0:T(4,128)(2,1)} %reshape.88), calls=%async_computation.6 | async-start | bytes 393216 | tf_op jit(solution)/shard_map/all_to_all | solution.py:581
  152.4 7.0 %all-to-all-done.6 = bf16[16,4,1536]{2,1,0:T(4,128)(2,1)S(1)} async-done(((bf16[16,4,1536]{2,1,0:T(4,128)(2,1)}), bf16[16,4,1536]{2,1,0:T(4,128)(2,1)S(1)}, u32[]{:S(2)}, u32[]{:S(2)}) %all-to-all-start.6) | async-done | bytes 196640 | tf_op jit(solution)/shard_map/all_to_all | solution.py:581
  (89 shorter events, 39.1 us)
Async XLA Ops:
  2.1 20.3 %all-to-all-start = ((bf16[16,4,1536]{2,1,0:T(4,128)(2,1)}), bf16[16,4,1536]{2,1,0:T(4,128)(2,1)S(1)}, u32[]{:S(2)}, u32[]{:S(2)}) async-start(bf16[16,4,1536]{2,1,0:T(4,128)(2,1)} %bitcast.44), calls=%async_computation | async-start | bytes 393216 | tf_op jit(solution)/shard_map/all_to_all | solution.py:462
  23.2 15.7 %all-to-all-start.1 = ((bf16[4,64,640]{2,1,0:T(8,128)(2,1)}), bf16[4,64,640]{2,1,0:T(8,128)(2,1)S(1)}, u32[]{:S(2)}, u32[]{:S(2)}) async-start(bf16[4,64,640]{2,1,0:T(8,128)(2,1)} %broadcast_in_dim.32), calls=%async_computation.1 | async-start | bytes 655360 | tf_op jit(solution)/shard_map/all_to_all | solution.py:405
  27.4 6.1 %collective-permute-start = (bf16[64,896]{1,0:T(8,128)(2,1)S(1)}, bf16[64,896]{1,0:T(8,128)(2,1)S(1)}, u32[]{:S(2)}, u32[]{:S(2)}) collective-permute-start(bf16[64,896]{1,0:T(8,128)(2,1)S(1)} %slice.53.refs_0_), channel_id=1, source_target_pairs={{0,2},{2,4},{4,6},{6,0},{1,3},{3,5},{5,7},{7,1},{8,10},{10,12},{12... | collective-permute-start | bytes 344072 | tf_op jit(solution)/shard_map/ppermute | solution.py:412
  28.7 8.2 %collective-permute-start.1 = (bf16[64,896]{1,0:T(8,128)(2,1)S(1)}, bf16[64,896]{1,0:T(8,128)(2,1)S(1)}, u32[]{:S(2)}, u32[]{:S(2)}) collective-permute-start(bf16[64,896]{1,0:T(8,128)(2,1)S(1)} %slice.53.refs_0_), channel_id=1, source_target_pairs={{0,4},{2,6},{4,0},{6,2},{1,5},{3,7},{5,1},{7,3},{8,12},{10,14},{12... | collective-permute-start | bytes 344072 | tf_op jit(solution)/shard_map/ppermute | solution.py:412
  31.2 5.8 %collective-permute-start.2 = (bf16[64,896]{1,0:T(8,128)(2,1)S(1)}, bf16[64,896]{1,0:T(8,128)(2,1)S(1)}, u32[]{:S(2)}, u32[]{:S(2)}) collective-permute-start(bf16[64,896]{1,0:T(8,128)(2,1)S(1)} %slice.53.refs_0_), channel_id=1, source_target_pairs={{0,6},{2,0},{4,2},{6,4},{1,7},{3,1},{5,3},{7,5},{8,14},{10,8},{12,... | collective-permute-start | bytes 344072 | tf_op jit(solution)/shard_map/ppermute | solution.py:412
  32.3 6.6 %collective-permute-start.3 = (f32[4,2304]{1,0:T(4,128)S(1)}, f32[4,2304]{1,0:T(4,128)S(1)}, u32[]{:S(2)}, u32[]{:S(2)}) collective-permute-start(f32[4,2304]{1,0:T(4,128)S(1)} %pad_maximum_fusion.1), channel_id=1, source_target_pairs={{0,1},{1,0},{2,3},{3,2},{4,5},{5,4},{6,7},{7,6},{8,9},{9,8},{10,11... | collective-permute-start | bytes 110600 | tf_op jit(solution)/shard_map/ppermute | solution.py:431
  38.9 27.2 %all-to-all-start.2 = ((bf16[4,256,896]{2,1,0:T(8,128)(2,1)}), bf16[4,256,896]{2,1,0:T(8,128)(2,1)}, u32[]{:S(2)}, u32[]{:S(2)}) async-start(bf16[4,256,896]{2,1,0:T(8,128)(2,1)} %shard_map.173), calls=%async_computation.2 | async-start | bytes 3670016 | tf_op jit(solution)/shard_map/all_to_all | solution.py:493
  43.5 19.0 %collective-permute-start.4 = (bf16[512,1024]{1,0:T(8,128)(2,1)S(1)}, bf16[512,1024]{1,0:T(8,128)(2,1)}, u32[]{:S(2)}, u32[]{:S(2)}) collective-permute-start(bf16[512,1024]{1,0:T(8,128)(2,1)S(1)} %get-tuple-element.70.normed_ref), channel_id=1, source_target_pairs={{0,1},{1,0},{2,3},{3,2},{4,5},{5,4},{6,7},{7,6},{8,9},{9,8},{10,11... | collective-permute-start | bytes 3145736 | tf_op jit(solution)/shard_map/ppermute | solution.py:431
  44.4 10.6 %collective-permute-start.5 = (bf16[256,640]{1,0:T(8,128)(2,1)S(1)}, bf16[256,640]{1,0:T(8,128)(2,1)S(1)}, u32[]{:S(2)}, u32[]{:S(2)}) collective-permute-start(bf16[256,640]{1,0:T(8,128)(2,1)S(1)} %bitcast.28), channel_id=1, source_target_pairs={{0,2},{2,4},{4,6},{6,0},{1,3},{3,5},{5,7},{7,1},{8,10},{10,12},{12... | collective-permute-start | bytes 983048 | tf_op jit(solution)/shard_map/ppermute | solution.py:412
  45.5 17.0 %collective-permute-start.6 = (bf16[256,640]{1,0:T(8,128)(2,1)S(1)}, bf16[256,640]{1,0:T(8,128)(2,1)S(1)}, u32[]{:S(2)}, u32[]{:S(2)}) collective-permute-start(bf16[256,640]{1,0:T(8,128)(2,1)S(1)} %bitcast.29), channel_id=1, source_target_pairs={{0,4},{2,6},{4,0},{6,2},{1,5},{3,7},{5,1},{7,3},{8,12},{10,14},{12... | collective-permute-start | bytes 983048 | tf_op jit(solution)/shard_map/ppermute | solution.py:412
  47.6 14.9 %collective-permute-start.7 = (bf16[256,640]{1,0:T(8,128)(2,1)S(1)}, bf16[256,640]{1,0:T(8,128)(2,1)S(1)}, u32[]{:S(2)}, u32[]{:S(2)}) collective-permute-start(bf16[256,640]{1,0:T(8,128)(2,1)S(1)} %bitcast.30), channel_id=1, source_target_pairs={{0,6},{2,0},{4,2},{6,4},{1,7},{3,1},{5,3},{7,5},{8,14},{10,8},{12,... | collective-permute-start | bytes 983048 | tf_op jit(solution)/shard_map/ppermute | solution.py:412
  72.3 17.5 %collective-permute-start.9 = (bf16[1024,512]{1,0:T(8,128)(2,1)}, bf16[1024,512]{1,0:T(8,128)(2,1)}, u32[]{:S(2)}, u32[]{:S(2)}) collective-permute-start(bf16[1024,512]{1,0:T(8,128)(2,1)} %get-tuple-element.91.turned_ref), channel_id=1, source_target_pairs={{0,1},{1,0},{2,3},{3,2},{4,5},{5,4},{6,7},{7,6},{8,9},{9,8},{10,11... | collective-permute-start | bytes 3145736 | tf_op jit(solution)/shard_map/ppermute | solution.py:431
  74.2 2.2 %collective-permute-start.8 = (f32[8,1024]{1,0:T(8,128)S(1)}, f32[8,1024]{1,0:T(8,128)S(1)}, u32[]{:S(2)}, u32[]{:S(2)}) collective-permute-start(f32[8,1024]{1,0:T(8,128)S(1)} %get-tuple-element.73.mine_ref), channel_id=1, source_target_pairs={{0,1},{1,0},{2,3},{3,2},{4,5},{5,4},{6,7},{7,6},{8,9},{9,8},{10,11... | collective-permute-start | bytes 98312 | tf_op jit(solution)/shard_map/ppermute | solution.py:431
  77.2 12.6 %all-to-all-start.3 = ((f32[32,1,128]{2,1,0:T(1,128)}), f32[32,1,128]{2,1,0:T(1,128)S(1)}, u32[]{:S(2)}, u32[]{:S(2)}) async-start(f32[32,1,128]{2,1,0:T(1,128)} %get-tuple-element.75), calls=%async_computation.3 | async-start | bytes 32768 | tf_op jit(solution)/shard_map/all_to_all | solution.py:524
  95.1 26.5 %all-to-all-start.4 = ((bf16[4,256,896]{2,1,0:T(8,128)(2,1)}), bf16[4,256,896]{2,1,0:T(8,128)(2,1)}, u32[]{:S(2)}, u32[]{:S(2)}) async-start(bf16[4,256,896]{2,1,0:T(8,128)(2,1)} %get-tuple-element.94), calls=%async_computation.4 | async-start | bytes 3670016 | tf_op jit(solution)/shard_map/all_to_all | solution.py:550
  99.6 11.6 %collective-permute-start.14 = (bf16[512,1024]{1,0:T(8,128)(2,1)}, bf16[512,1024]{1,0:T(8,128)(2,1)}, u32[]{:S(2)}, u32[]{:S(2)}) collective-permute-start(bf16[512,1024]{1,0:T(8,128)(2,1)} %get-tuple-element.103), channel_id=1, source_target_pairs={{0,1},{1,0},{2,3},{3,2},{4,5},{5,4},{6,7},{7,6},{8,9},{9,8},{10,11... | collective-permute-start | bytes 3145736 | tf_op jit(solution)/shard_map/ppermute | solution.py:431
  101.3 15.5 %collective-permute-start.10 = (bf16[256,640]{1,0:T(8,128)(2,1)S(1)}, bf16[256,640]{1,0:T(8,128)(2,1)S(1)}, u32[]{:S(2)}, u32[]{:S(2)}) collective-permute-start(bf16[256,640]{1,0:T(8,128)(2,1)S(1)} %get-tuple-element.96), channel_id=1, source_target_pairs={{0,2},{2,4},{4,6},{6,0},{1,3},{3,5},{5,7},{7,1},{8,10},{10,12},{12... | collective-permute-start | bytes 983048 | tf_op jit(solution)/shard_map/ppermute | solution.py:418
  101.6 16.8 %collective-permute-start.11 = (bf16[256,640]{1,0:T(8,128)(2,1)S(1)}, bf16[256,640]{1,0:T(8,128)(2,1)S(1)}, u32[]{:S(2)}, u32[]{:S(2)}) collective-permute-start(bf16[256,640]{1,0:T(8,128)(2,1)S(1)} %get-tuple-element.97), channel_id=1, source_target_pairs={{0,4},{2,6},{4,0},{6,2},{1,5},{3,7},{5,1},{7,3},{8,12},{10,14},{12... | collective-permute-start | bytes 983048 | tf_op jit(solution)/shard_map/ppermute | solution.py:418
  103.4 15.8 %collective-permute-start.12 = (bf16[256,640]{1,0:T(8,128)(2,1)S(1)}, bf16[256,640]{1,0:T(8,128)(2,1)S(1)}, u32[]{:S(2)}, u32[]{:S(2)}) collective-permute-start(bf16[256,640]{1,0:T(8,128)(2,1)S(1)} %get-tuple-element.98), channel_id=1, source_target_pairs={{0,6},{2,0},{4,2},{6,4},{1,7},{3,1},{5,3},{7,5},{8,14},{10,8},{12,... | collective-permute-start | bytes 983048 | tf_op jit(solution)/shard_map/ppermute | solution.py:418
  124.5 7.2 %collective-permute-start.17 = (bf16[64,896]{1,0:T(8,128)(2,1)S(1)}, bf16[64,896]{1,0:T(8,128)(2,1)S(1)}, u32[]{:S(2)}, u32[]{:S(2)}) collective-permute-start(bf16[64,896]{1,0:T(8,128)(2,1)S(1)} %get-tuple-element.114), channel_id=1, source_target_pairs={{0,6},{2,0},{4,2},{6,4},{1,7},{3,1},{5,3},{7,5},{8,14},{10,8},{12,... | collective-permute-start | bytes 344072 | tf_op jit(solution)/shard_map/ppermute | solution.py:418
  126.9 5.3 %collective-permute-start.16 = (bf16[64,896]{1,0:T(8,128)(2,1)S(1)}, bf16[64,896]{1,0:T(8,128)(2,1)S(1)}, u32[]{:S(2)}, u32[]{:S(2)}) collective-permute-start(bf16[64,896]{1,0:T(8,128)(2,1)S(1)} %get-tuple-element.113), channel_id=1, source_target_pairs={{0,4},{2,6},{4,0},{6,2},{1,5},{3,7},{5,1},{7,3},{8,12},{10,14},{12... | collective-permute-start | bytes 344072 | tf_op jit(solution)/shard_map/ppermute | solution.py:418
  127.4 5.9 %collective-permute-start.15 = (bf16[64,896]{1,0:T(8,128)(2,1)S(1)}, bf16[64,896]{1,0:T(8,128)(2,1)S(1)}, u32[]{:S(2)}, u32[]{:S(2)}) collective-permute-start(bf16[64,896]{1,0:T(8,128)(2,1)S(1)} %get-tuple-element.112), channel_id=1, source_target_pairs={{0,2},{2,4},{4,6},{6,0},{1,3},{3,5},{5,7},{7,1},{8,10},{10,12},{12... | collective-permute-start | bytes 344072 | tf_op jit(solution)/shard_map/ppermute | solution.py:418
  128.3 9.8 %all-to-all-start.5 = ((bf16[4,80,640]{2,1,0:T(8,128)(2,1)}), bf16[4,80,640]{2,1,0:T(8,128)(2,1)S(1)}, u32[]{:S(2)}, u32[]{:S(2)}) async-start(bf16[4,80,640]{2,1,0:T(8,128)(2,1)} %get-tuple-element.109), calls=%async_computation.5 | async-start | bytes 819200 | tf_op jit(solution)/shard_map/all_to_all | solution.py:569
  138.8 20.6 %all-to-all-start.6 = ((bf16[16,4,1536]{2,1,0:T(4,128)(2,1)}), bf16[16,4,1536]{2,1,0:T(4,128)(2,1)S(1)}, u32[]{:S(2)}, u32[]{:S(2)}) async-start(bf16[16,4,1536]{2,1,0:T(4,128)(2,1)} %reshape.88), calls=%async_computation.6 | async-start | bytes 393216 | tf_op jit(solution)/shard_map/all_to_all | solution.py:581
  (12 other events, 161.2 us)

commit v6 on v5

--- a/solution.py
+++ b/solution.py
@@ -18,7 +18,7 @@
 D = 1024
 ROWS = PAIRS * SEQ
 BOTH = 2 * PAIRS
-LOW = 384
+LOW = 256
 WA = 512 + LOW
 WB = 1024 - LOW
 F32 = jnp.float32

time: 162 us -> 159 us (0.981)
  starting transfers between devices: 63.8 us -> 61.5 us
    ppermute x6, waiting for transfers between devices: 4.01 us -> 11.7 us  [along_ring(): lax.ppermute(pieces[d], axis, [(i, (i + d) % 4) for i in range(4)])]
    all_to_all x1, waiting for transfers between devices: 4.64 us -> 0.01 us  [shards(): done_b = lax.all_to_all(mid_b, 'pb', 0, 0, tiled=True)]
    all_to_all x1, waiting for transfers between devices: 3.61 us -> 0.01 us  [shards(): kvo = lax.all_to_all(slab_a, 'pb', 0, 0, tiled=True).reshape(1024, WA)]
    all_to_all x1, starting transfers between devices: 10.2 us -> 6.97 us  [shards(): lax.all_to_all(part.reshape(16, 4, 1536), ('z', 'c'), 0, 0, tiled=True)]
    all_to_all x1, waiting for transfers between devices: 2.44 us -> 0.01 us  [shards(): got_a = lax.all_to_all(chip_a, 'pb', 0, 0, tiled=True)]
    ppermute x6, waiting for transfers between devices: 17.2 us -> 19.2 us  [from_ring(): lax.ppermute(x, axis, [(i, (i + d) % 4) for i in range(4)])]
  transfers between devices with their start and end apart: 25 -> 25, of which waited for: 16 -> 13; matrix products, arithmetic and copies ran while one was open for 5% -> 5% of each run, Pallas kernels for 11% -> 11%
where the time goes in v6:
time: 159 us; the launch traced here: 158 us
  starting transfers between devices  61.5 us (39%)
  waiting for transfers between devices  46.5 us (29%)
  Pallas kernels  34.3 us (22%)
  local copies, waits for them, and re-layouts  10.3 us (6%)
  between operations  4.63 us (3%)
    pallas_call x10, Pallas kernels, call(): pl.pallas_call(body, grid=(1,), out_shape=[jax.ShapeDtypeStruct(o, d) for...  34.3 us
    ppermute x6, waiting for transfers between devices, from_ring(): lax.ppermute(x, axis, [(i, (i + d) % 4) for i in range(4)])  19.2 us
    ppermute x6, waiting for transfers between devices, along_ring(): lax.ppermute(pieces[d], axis, [(i, (i + d) % 4) for i in range(4)])  11.7 us
    all_to_all x1, starting transfers between devices, shards(): lax.all_to_all(both_halves, ('z', 'c'), 0, 0, tiled=True).reshape(64, 1536)  9.98 us
    ppermute x6, starting transfers between devices, from_ring(): lax.ppermute(x, axis, [(i, (i + d) % 4) for i in range(4)])  9.28 us
    all_to_all x1, waiting for transfers between devices, shards(): lax.all_to_all(part.reshape(16, 4, 1536), ('z', 'c'), 0, 0, tiled=True)  7.02 us
    all_to_all x1, starting transfers between devices, shards(): lax.all_to_all(part.reshape(16, 4, 1536), ('z', 'c'), 0, 0, tiled=True)  6.97 us
    ppermute x6, starting transfers between devices, along_ring(): lax.ppermute(pieces[d], axis, [(i, (i + d) % 4) for i in range(4)])  6.62 us
  transfers between devices with their start and end apart: 25, of which 13 were waited for; matrix products, arithmetic and copies ran while one was open for 5% of the time, Pallas kernels for 11%

profile of v6, /device:TPU:1, one launch (start us, length us, event | category | flops | bytes accessed | tf_op | source)
XLA Modules:
  0.0 157.7 jit_solution(10172364818365437601)
XLA Ops:
  2.1 10.0 %all-to-all-start = ((bf16[16,4,1536]{2,1,0:T(4,128)(2,1)}), bf16[16,4,1536]{2,1,0:T(4,128)(2,1)S(1)}, u32[]{:S(2)}, u32[]{:S(2)}) async-start(bf16[16,4,1536]{2,1,0:T(4,128)(2,1)} %bitcast.44), calls=%async_computation | async-start | bytes 393216 | tf_op jit(solution)/shard_map/all_to_all | solution.py:462
  13.4 2.9 %shard_map.172 = (bf16[512,1024]{1,0:T(8,128)(2,1)S(1)}, bf16[1024,512]{1,0:T(8,128)(2,1)}, bf16[8,1024]{1,0:T(8,128)(2,1)S(1)}, f32[8,1024]{1,0:T(8,128)S(1)}) custom-call(s32[4]{0:T(128)S(1)} %bitcast.40, bf16[512,1024]{1,0:T(8,128)(2,1)} %bitcast.26, f32[1,1024]{1,0:T(1,128)S(1)} %bitcast.34), custom_call_target="tpu_custom_call" | custom-call | flops 10000000 | bytes 3198976 | tf_op jit(solution)/shard_map/pallas_call | solution.py:50
  17.3 5.1 %all-to-all-done = bf16[16,4,1536]{2,1,0:T(4,128)(2,1)S(1)} async-done(((bf16[16,4,1536]{2,1,0:T(4,128)(2,1)}), bf16[16,4,1536]{2,1,0:T(4,128)(2,1)S(1)}, u32[]{:S(2)}, u32[]{:S(2)}) %all-to-all-start) | async-done | bytes 196640 | tf_op jit(solution)/shard_map/all_to_all | solution.py:462
  23.3 4.2 %all-to-all-start.1 = ((bf16[4,64,768]{2,1,0:T(8,128)(2,1)}), bf16[4,64,768]{2,1,0:T(8,128)(2,1)S(1)}, u32[]{:S(2)}, u32[]{:S(2)}) async-start(bf16[4,64,768]{2,1,0:T(8,128)(2,1)} %broadcast_in_dim.32), calls=%async_computation.1 | async-start | bytes 786432 | tf_op jit(solution)/shard_map/all_to_all | solution.py:405
  28.7 2.5 %collective-permute-start.1 = (bf16[64,768]{1,0:T(8,128)(2,1)S(1)}, bf16[64,768]{1,0:T(8,128)(2,1)S(1)}, u32[]{:S(2)}, u32[]{:S(2)}) collective-permute-start(bf16[64,768]{1,0:T(8,128)(2,1)S(1)} %get-tuple-element.120.refs_0_), channel_id=1, source_target_pairs={{0,4},{2,6},{4,0},{6,2},{1,5},{3,7},{5,1},{7,3},{8,12},{10,14},{12... | collective-permute-start | bytes 294920 | tf_op jit(solution)/shard_map/ppermute | solution.py:412
  33.2 3.0 %collective-permute-done.1.refs_2_ = bf16[64,768]{1,0:T(8,128)(2,1)S(1)} collective-permute-done((bf16[64,768]{1,0:T(8,128)(2,1)S(1)}, bf16[64,768]{1,0:T(8,128)(2,1)S(1)}, u32[]{:S(2)}, u32[]{:S(2)}) %collective-permute-start.1) | collective-permute-done | bytes 98336 | tf_op jit(solution)/shard_map/ppermute | solution.py:412
  38.0 4.5 %all-to-all-start.2 = ((bf16[4,256,768]{2,1,0:T(8,128)(2,1)}), bf16[4,256,768]{2,1,0:T(8,128)(2,1)}, u32[]{:S(2)}, u32[]{:S(2)}) async-start(bf16[4,256,768]{2,1,0:T(8,128)(2,1)} %shard_map.173), calls=%async_computation.2 | async-start | bytes 3145728 | tf_op jit(solution)/shard_map/all_to_all | solution.py:493
  44.6 2.1 %collective-permute-start.6 = (bf16[256,768]{1,0:T(8,128)(2,1)S(1)}, bf16[256,768]{1,0:T(8,128)(2,1)S(1)}, u32[]{:S(2)}, u32[]{:S(2)}) collective-permute-start(bf16[256,768]{1,0:T(8,128)(2,1)S(1)} %bitcast.29), channel_id=1, source_target_pairs={{0,4},{2,6},{4,0},{6,2},{1,5},{3,7},{5,1},{7,3},{8,12},{10,14},{12... | collective-permute-start | bytes 1179656 | tf_op jit(solution)/shard_map/ppermute | solution.py:412
  48.1 7.4 %collective-permute-done.5.refs_1_.refs_2_ = bf16[256,768]{1,0:T(8,128)(2,1)S(1)} collective-permute-done((bf16[256,768]{1,0:T(8,128)(2,1)S(1)}, bf16[256,768]{1,0:T(8,128)(2,1)S(1)}, u32[]{:S(2)}, u32[]{:S(2)}) %collective-permute-start.5) | collective-permute-done | bytes 393248 | tf_op jit(solution)/shard_map/ppermute | solution.py:412
  55.5 8.8 %collective-permute-done.6.refs_2_.refs_3_ = bf16[256,768]{1,0:T(8,128)(2,1)S(1)} collective-permute-done((bf16[256,768]{1,0:T(8,128)(2,1)S(1)}, bf16[256,768]{1,0:T(8,128)(2,1)S(1)}, u32[]{:S(2)}, u32[]{:S(2)}) %collective-permute-start.6) | collective-permute-done | bytes 393248 | tf_op jit(solution)/shard_map/ppermute | solution.py:412
  64.4 6.0 %shard_map.174 = (f32[1024,256]{1,0:T(8,128)}, bf16[1024,256]{1,0:T(8,128)(2,1)}, bf16[1024,256]{1,0:T(8,128)(2,1)}, f32[8,512]{1,0:T(8,128)S(1)}, bf16[8,512]{1...) custom-call(s32[2]{0:T(128)S(1)} %pad_add_fusion.at_ref, ...), custom_call_target="tpu_custom_call" | custom-call | flops 1100000000 | bytes 8634368 | tf_op jit(solution)/shard_map/pallas_call | solution.py:50
  74.4 5.1 %all-to-all-start.3 = ((f32[32,1,128]{2,1,0:T(1,128)}), f32[32,1,128]{2,1,0:T(1,128)S(1)}, u32[]{:S(2)}, u32[]{:S(2)}) async-start(f32[32,1,128]{2,1,0:T(1,128)} %get-tuple-element.75), calls=%async_computation.3 | async-start | bytes 32768 | tf_op jit(solution)/shard_map/all_to_all | solution.py:524
  79.5 6.7 %shard_map.176 = (f32[1024,512]{1,0:T(8,128)}, f32[8,512]{1,0:T(8,128)S(1)}, f32[8,1024]{1,0:T(8,128)S(1)}, f32[8,1024]{1,0:T(8,128)S(1)}, bf16[512,1024]{1,0:T(8,128)(2,1)}) custom-call(s32[2]{0:T(128)S(1)} %pad_add_fusion.at_ref, s32[8]{0:T(128)S(1)} %convert_reduce_fusion.len_ref, bf16[1024,256]{1,0:T(8,128)(2,1)} %get-tuple-element.77.krot_ref, ...), custom_call_target="tpu_custom_call" | custom-call | flops 200000000 | bytes 9752576 | tf_op jit(solution)/shard_map/pallas_call | solution.py:50
  87.8 5.6 %shard_map.177 = (bf16[4,256,768]{2,1,0:T(8,128)(2,1)}, bf16[256,768]{1,0:T(8,128)(2,1)S(1)}, bf16[256,768]{1,0:T(8,128)(2,1)}, bf16[256,768]{1,0:T(8,128)(2,1)}...) custom-call(s32[2]{0:T(128)S(1)} %pad_add_fusion.at_ref, ...), custom_call_target="tpu_custom_call" | custom-call | flops 1100000000 | bytes 8560640 | tf_op jit(solution)/shard_map/pallas_call | solution.py:50
  93.4 4.5 %all-to-all-start.4 = ((bf16[4,256,768]{2,1,0:T(8,128)(2,1)}), bf16[4,256,768]{2,1,0:T(8,128)(2,1)}, u32[]{:S(2)}, u32[]{:S(2)}) async-start(bf16[4,256,768]{2,1,0:T(8,128)(2,1)} %get-tuple-element.94), calls=%async_computation.4 | async-start | bytes 3145728 | tf_op jit(solution)/shard_map/all_to_all | solution.py:550
  104.1 2.2 %copy.28 = f32[8,32,4,8]{3,2,1,0:T(4,128)} copy(f32[8,32,4,8]{3,1,2,0:T(8,128)} %bitcast.41) | data formatting | bytes 65536 | tf_op jit(solution)/shard_map/transpose | solution.py:427
  109.7 5.5 %shard_map.178 = bf16[512,1024]{1,0:T(8,128)(2,1)} custom-call(s32[8]{0:T(128)S(1)} %convert_reduce_fusion.len_ref, bf16[512,1024]{1,0:T(8,128)(2,1)S(1)} %bitcast.27, f32[1,1024]{1,0:T(1,128)S(1)} %bitcast.35, bf16[1024,512]{1,0:T(8,128)(2,1)} %get-tuple-element.99.skv_ref, f32[8,128]{1,0:T(8,128)S(1)} %get-tuple-element.100.g_ref, ...), custom_call_target="tpu_custom_call" | custom-call | flops 600000000 | bytes 5873664 | tf_op jit(solution)/shard_map/pallas_call | solution.py:50
  115.2 4.7 %collective-permute-done.11.refs_2_ = bf16[256,768]{1,0:T(8,128)(2,1)S(1)} collective-permute-done((bf16[256,768]{1,0:T(8,128)(2,1)}, bf16[256,768]{1,0:T(8,128)(2,1)S(1)}, u32[]{:S(2)}, u32[]{:S(2)}) %collective-permute-start.11) | collective-permute-done | bytes 393248 | tf_op jit(solution)/shard_map/ppermute | solution.py:418
  120.7 2.9 %shard_map.179 = (bf16[64,768]{1,0:T(8,128)(2,1)S(1)}, bf16[64,768]{1,0:T(8,128)(2,1)S(1)}, bf16[64,768]{1,0:T(8,128)(2,1)S(1)}, bf16[64,768]{1,0:T(8,128)(2,1)S(1)}, bf16[4,80,768]{2,1,0:T(8,128)(2,1)}) custom-call(s32[2]{0:T(128)S(1)} %pad_add_fusion.at_ref, f32[8,128]{1,0:T(8,128)S(1)} %get-tuple-element.93.loss_ref, ...), custom_call_target="tpu_custom_call" | custom-call | bytes 4034560 | tf_op jit(solution)/shard_map/pallas_call | solution.py:50
  123.5 4.5 %all-to-all-start.5 = ((bf16[4,80,768]{2,1,0:T(8,128)(2,1)}), bf16[4,80,768]{2,1,0:T(8,128)(2,1)S(1)}, u32[]{:S(2)}, u32[]{:S(2)}) async-start(bf16[4,80,768]{2,1,0:T(8,128)(2,1)} %get-tuple-element.109), calls=%async_computation.5 | async-start | bytes 983040 | tf_op jit(solution)/shard_map/all_to_all | solution.py:569
  128.1 2.9 %collective-permute-start.17 = (bf16[64,768]{1,0:T(8,128)(2,1)S(1)}, bf16[64,768]{1,0:T(8,128)(2,1)S(1)}, u32[]{:S(2)}, u32[]{:S(2)}) collective-permute-start(bf16[64,768]{1,0:T(8,128)(2,1)S(1)} %get-tuple-element.114), channel_id=1, source_target_pairs={{0,6},{2,0},{4,2},{6,4},{1,7},{3,1},{5,3},{7,5},{8,14},{10,8},{12,... | collective-permute-start | bytes 294920 | tf_op jit(solution)/shard_map/ppermute | solution.py:418
  133.2 2.8 %collective-permute-done.16 = bf16[64,768]{1,0:T(8,128)(2,1)S(1)} collective-permute-done((bf16[64,768]{1,0:T(8,128)(2,1)S(1)}, bf16[64,768]{1,0:T(8,128)(2,1)S(1)}, u32[]{:S(2)}, u32[]{:S(2)}) %collective-permute-start.16) | collective-permute-done | bytes 98336 | tf_op jit(solution)/shard_map/ppermute | solution.py:418
  138.6 7.0 %all-to-all-start.6 = ((bf16[16,4,1536]{2,1,0:T(4,128)(2,1)}), bf16[16,4,1536]{2,1,0:T(4,128)(2,1)S(1)}, u32[]{:S(2)}, u32[]{:S(2)}) async-start(bf16[16,4,1536]{2,1,0:T(4,128)(2,1)} %reshape.88), calls=%async_computation.6 | async-start | bytes 393216 | tf_op jit(solution)/shard_map/all_to_all | solution.py:581
  148.9 7.0 %all-to-all-done.6 = bf16[16,4,1536]{2,1,0:T(4,128)(2,1)S(1)} async-done(((bf16[16,4,1536]{2,1,0:T(4,128)(2,1)}), bf16[16,4,1536]{2,1,0:T(4,128)(2,1)S(1)}, u32[]{:S(2)}, u32[]{:S(2)}) %all-to-all-start.6) | async-done | bytes 196640 | tf_op jit(solution)/shard_map/all_to_all | solution.py:581
  (88 shorter events, 35.4 us)
Async XLA Ops:
  2.1 20.3 %all-to-all-start = ((bf16[16,4,1536]{2,1,0:T(4,128)(2,1)}), bf16[16,4,1536]{2,1,0:T(4,128)(2,1)S(1)}, u32[]{:S(2)}, u32[]{:S(2)}) async-start(bf16[16,4,1536]{2,1,0:T(4,128)(2,1)} %bitcast.44), calls=%async_computation | async-start | bytes 393216 | tf_op jit(solution)/shard_map/all_to_all | solution.py:462
  23.3 14.7 %all-to-all-start.1 = ((bf16[4,64,768]{2,1,0:T(8,128)(2,1)}), bf16[4,64,768]{2,1,0:T(8,128)(2,1)S(1)}, u32[]{:S(2)}, u32[]{:S(2)}) async-start(bf16[4,64,768]{2,1,0:T(8,128)(2,1)} %broadcast_in_dim.32), calls=%async_computation.1 | async-start | bytes 786432 | tf_op jit(solution)/shard_map/all_to_all | solution.py:405
  27.4 5.7 %collective-permute-start = (bf16[64,768]{1,0:T(8,128)(2,1)S(1)}, bf16[64,768]{1,0:T(8,128)(2,1)S(1)}, u32[]{:S(2)}, u32[]{:S(2)}) collective-permute-start(bf16[64,768]{1,0:T(8,128)(2,1)S(1)} %get-tuple-element.120.refs_0_), channel_id=1, source_target_pairs={{0,2},{2,4},{4,6},{6,0},{1,3},{3,5},{5,7},{7,1},{8,10},{10,12},{12... | collective-permute-start | bytes 294920 | tf_op jit(solution)/shard_map/ppermute | solution.py:412
  28.7 7.5 %collective-permute-start.1 = (bf16[64,768]{1,0:T(8,128)(2,1)S(1)}, bf16[64,768]{1,0:T(8,128)(2,1)S(1)}, u32[]{:S(2)}, u32[]{:S(2)}) collective-permute-start(bf16[64,768]{1,0:T(8,128)(2,1)S(1)} %get-tuple-element.120.refs_0_), channel_id=1, source_target_pairs={{0,4},{2,6},{4,0},{6,2},{1,5},{3,7},{5,1},{7,3},{8,12},{10,14},{12... | collective-permute-start | bytes 294920 | tf_op jit(solution)/shard_map/ppermute | solution.py:412
  31.1 5.1 %collective-permute-start.2 = (bf16[64,768]{1,0:T(8,128)(2,1)S(1)}, bf16[64,768]{1,0:T(8,128)(2,1)S(1)}, u32[]{:S(2)}, u32[]{:S(2)}) collective-permute-start(bf16[64,768]{1,0:T(8,128)(2,1)S(1)} %get-tuple-element.120.refs_0_), channel_id=1, source_target_pairs={{0,6},{2,0},{4,2},{6,4},{1,7},{3,1},{5,3},{7,5},{8,14},{10,8},{12,... | collective-permute-start | bytes 294920 | tf_op jit(solution)/shard_map/ppermute | solution.py:412
  32.3 5.7 %collective-permute-start.3 = (f32[4,2304]{1,0:T(4,128)S(1)}, f32[4,2304]{1,0:T(4,128)S(1)}, u32[]{:S(2)}, u32[]{:S(2)}) collective-permute-start(f32[4,2304]{1,0:T(4,128)S(1)} %pad_maximum_fusion.1), channel_id=1, source_target_pairs={{0,1},{1,0},{2,3},{3,2},{4,5},{5,4},{6,7},{7,6},{8,9},{9,8},{10,11... | collective-permute-start | bytes 110600 | tf_op jit(solution)/shard_map/ppermute | solution.py:431
  38.0 26.3 %all-to-all-start.2 = ((bf16[4,256,768]{2,1,0:T(8,128)(2,1)}), bf16[4,256,768]{2,1,0:T(8,128)(2,1)}, u32[]{:S(2)}, u32[]{:S(2)}) async-start(bf16[4,256,768]{2,1,0:T(8,128)(2,1)} %shard_map.173), calls=%async_computation.2 | async-start | bytes 3145728 | tf_op jit(solution)/shard_map/all_to_all | solution.py:493
  42.5 21.8 %collective-permute-start.4 = (bf16[512,1024]{1,0:T(8,128)(2,1)S(1)}, bf16[512,1024]{1,0:T(8,128)(2,1)}, u32[]{:S(2)}, u32[]{:S(2)}) collective-permute-start(bf16[512,1024]{1,0:T(8,128)(2,1)S(1)} %get-tuple-element.70.normed_ref), channel_id=1, source_target_pairs={{0,1},{1,0},{2,3},{3,2},{4,5},{5,4},{6,7},{7,6},{8,9},{9,8},{10,11... | collective-permute-start | bytes 3145736 | tf_op jit(solution)/shard_map/ppermute | solution.py:431
  43.5 12.0 %collective-permute-start.5 = (bf16[256,768]{1,0:T(8,128)(2,1)S(1)}, bf16[256,768]{1,0:T(8,128)(2,1)S(1)}, u32[]{:S(2)}, u32[]{:S(2)}) collective-permute-start(bf16[256,768]{1,0:T(8,128)(2,1)S(1)} %bitcast.28), channel_id=1, source_target_pairs={{0,2},{2,4},{4,6},{6,0},{1,3},{3,5},{5,7},{7,1},{8,10},{10,12},{12... | collective-permute-start | bytes 1179656 | tf_op jit(solution)/shard_map/ppermute | solution.py:412
  44.6 19.7 %collective-permute-start.6 = (bf16[256,768]{1,0:T(8,128)(2,1)S(1)}, bf16[256,768]{1,0:T(8,128)(2,1)S(1)}, u32[]{:S(2)}, u32[]{:S(2)}) collective-permute-start(bf16[256,768]{1,0:T(8,128)(2,1)S(1)} %bitcast.29), channel_id=1, source_target_pairs={{0,4},{2,6},{4,0},{6,2},{1,5},{3,7},{5,1},{7,3},{8,12},{10,14},{12... | collective-permute-start | bytes 1179656 | tf_op jit(solution)/shard_map/ppermute | solution.py:412
  46.7 17.6 %collective-permute-start.7 = (bf16[256,768]{1,0:T(8,128)(2,1)S(1)}, bf16[256,768]{1,0:T(8,128)(2,1)S(1)}, u32[]{:S(2)}, u32[]{:S(2)}) collective-permute-start(bf16[256,768]{1,0:T(8,128)(2,1)S(1)} %bitcast.30), channel_id=1, source_target_pairs={{0,6},{2,0},{4,2},{6,4},{1,7},{3,1},{5,3},{7,5},{8,14},{10,8},{12,... | collective-permute-start | bytes 1179656 | tf_op jit(solution)/shard_map/ppermute | solution.py:412
  70.4 17.5 %collective-permute-start.9 = (bf16[1024,512]{1,0:T(8,128)(2,1)}, bf16[1024,512]{1,0:T(8,128)(2,1)}, u32[]{:S(2)}, u32[]{:S(2)}) collective-permute-start(bf16[1024,512]{1,0:T(8,128)(2,1)} %get-tuple-element.91.turned_ref), channel_id=1, source_target_pairs={{0,1},{1,0},{2,3},{3,2},{4,5},{5,4},{6,7},{7,6},{8,9},{9,8},{10,11... | collective-permute-start | bytes 3145736 | tf_op jit(solution)/shard_map/ppermute | solution.py:431
  71.4 2.2 %collective-permute-start.8 = (f32[8,1024]{1,0:T(8,128)S(1)}, f32[8,1024]{1,0:T(8,128)S(1)}, u32[]{:S(2)}, u32[]{:S(2)}) collective-permute-start(f32[8,1024]{1,0:T(8,128)S(1)} %get-tuple-element.73.mine_ref), channel_id=1, source_target_pairs={{0,1},{1,0},{2,3},{3,2},{4,5},{5,4},{6,7},{7,6},{8,9},{9,8},{10,11... | collective-permute-start | bytes 98312 | tf_op jit(solution)/shard_map/ppermute | solution.py:431
  74.4 13.5 %all-to-all-start.3 = ((f32[32,1,128]{2,1,0:T(1,128)}), f32[32,1,128]{2,1,0:T(1,128)S(1)}, u32[]{:S(2)}, u32[]{:S(2)}) async-start(f32[32,1,128]{2,1,0:T(1,128)} %get-tuple-element.75), calls=%async_computation.3 | async-start | bytes 32768 | tf_op jit(solution)/shard_map/all_to_all | solution.py:524
  93.4 27.3 %all-to-all-start.4 = ((bf16[4,256,768]{2,1,0:T(8,128)(2,1)}), bf16[4,256,768]{2,1,0:T(8,128)(2,1)}, u32[]{:S(2)}, u32[]{:S(2)}) async-start(bf16[4,256,768]{2,1,0:T(8,128)(2,1)} %get-tuple-element.94), calls=%async_computation.4 | async-start | bytes 3145728 | tf_op jit(solution)/shard_map/all_to_all | solution.py:550
  97.9 11.8 %collective-permute-start.14 = (bf16[512,1024]{1,0:T(8,128)(2,1)}, bf16[512,1024]{1,0:T(8,128)(2,1)}, u32[]{:S(2)}, u32[]{:S(2)}) collective-permute-start(bf16[512,1024]{1,0:T(8,128)(2,1)} %get-tuple-element.103), channel_id=1, source_target_pairs={{0,1},{1,0},{2,3},{3,2},{4,5},{5,4},{6,7},{7,6},{8,9},{9,8},{10,11... | collective-permute-start | bytes 3145736 | tf_op jit(solution)/shard_map/ppermute | solution.py:431
  99.8 15.4 %collective-permute-start.10 = (bf16[256,768]{1,0:T(8,128)(2,1)}, bf16[256,768]{1,0:T(8,128)(2,1)S(1)}, u32[]{:S(2)}, u32[]{:S(2)}) collective-permute-start(bf16[256,768]{1,0:T(8,128)(2,1)} %get-tuple-element.96), channel_id=1, source_target_pairs={{0,2},{2,4},{4,6},{6,0},{1,3},{3,5},{5,7},{7,1},{8,10},{10,12},{12... | collective-permute-start | bytes 1179656 | tf_op jit(solution)/shard_map/ppermute | solution.py:418
  100.1 19.7 %collective-permute-start.11 = (bf16[256,768]{1,0:T(8,128)(2,1)}, bf16[256,768]{1,0:T(8,128)(2,1)S(1)}, u32[]{:S(2)}, u32[]{:S(2)}) collective-permute-start(bf16[256,768]{1,0:T(8,128)(2,1)} %get-tuple-element.97), channel_id=1, source_target_pairs={{0,4},{2,6},{4,0},{6,2},{1,5},{3,7},{5,1},{7,3},{8,12},{10,14},{12... | collective-permute-start | bytes 1179656 | tf_op jit(solution)/shard_map/ppermute | solution.py:418
  102.0 18.7 %collective-permute-start.12 = (bf16[256,768]{1,0:T(8,128)(2,1)S(1)}, bf16[256,768]{1,0:T(8,128)(2,1)S(1)}, u32[]{:S(2)}, u32[]{:S(2)}) collective-permute-start(bf16[256,768]{1,0:T(8,128)(2,1)S(1)} %get-tuple-element.98), channel_id=1, source_target_pairs={{0,6},{2,0},{4,2},{6,4},{1,7},{3,1},{5,3},{7,5},{8,14},{10,8},{12,... | collective-permute-start | bytes 1179656 | tf_op jit(solution)/shard_map/ppermute | solution.py:418
  123.5 14.3 %all-to-all-start.5 = ((bf16[4,80,768]{2,1,0:T(8,128)(2,1)}), bf16[4,80,768]{2,1,0:T(8,128)(2,1)S(1)}, u32[]{:S(2)}, u32[]{:S(2)}) async-start(bf16[4,80,768]{2,1,0:T(8,128)(2,1)} %get-tuple-element.109), calls=%async_computation.5 | async-start | bytes 983040 | tf_op jit(solution)/shard_map/all_to_all | solution.py:569
  128.1 5.2 %collective-permute-start.17 = (bf16[64,768]{1,0:T(8,128)(2,1)S(1)}, bf16[64,768]{1,0:T(8,128)(2,1)S(1)}, u32[]{:S(2)}, u32[]{:S(2)}) collective-permute-start(bf16[64,768]{1,0:T(8,128)(2,1)S(1)} %get-tuple-element.114), channel_id=1, source_target_pairs={{0,6},{2,0},{4,2},{6,4},{1,7},{3,1},{5,3},{7,5},{8,14},{10,8},{12,... | collective-permute-start | bytes 294920 | tf_op jit(solution)/shard_map/ppermute | solution.py:418
  131.0 5.1 %collective-permute-start.16 = (bf16[64,768]{1,0:T(8,128)(2,1)S(1)}, bf16[64,768]{1,0:T(8,128)(2,1)S(1)}, u32[]{:S(2)}, u32[]{:S(2)}) collective-permute-start(bf16[64,768]{1,0:T(8,128)(2,1)S(1)} %get-tuple-element.113), channel_id=1, source_target_pairs={{0,4},{2,6},{4,0},{6,2},{1,5},{3,7},{5,1},{7,3},{8,12},{10,14},{12... | collective-permute-start | bytes 294920 | tf_op jit(solution)/shard_map/ppermute | solution.py:418
  131.0 6.8 %collective-permute-start.15 = (bf16[64,768]{1,0:T(8,128)(2,1)S(1)}, bf16[64,768]{1,0:T(8,128)(2,1)S(1)}, u32[]{:S(2)}, u32[]{:S(2)}) collective-permute-start(bf16[64,768]{1,0:T(8,128)(2,1)S(1)} %get-tuple-element.112), channel_id=1, source_target_pairs={{0,2},{2,4},{4,6},{6,0},{1,3},{3,5},{5,7},{7,1},{8,10},{10,12},{12... | collective-permute-start | bytes 294920 | tf_op jit(solution)/shard_map/ppermute | solution.py:418
  138.6 17.3 %all-to-all-start.6 = ((bf16[16,4,1536]{2,1,0:T(4,128)(2,1)}), bf16[16,4,1536]{2,1,0:T(4,128)(2,1)S(1)}, u32[]{:S(2)}, u32[]{:S(2)}) async-start(bf16[16,4,1536]{2,1,0:T(4,128)(2,1)} %reshape.88), calls=%async_computation.6 | async-start | bytes 393216 | tf_op jit(solution)/shard_map/all_to_all | solution.py:581
  (12 other events, 156.8 us)

commit v7 on v6

--- a/solution.py
+++ b/solution.py
@@ -348,15 +348,24 @@
         outs_b[d][...] = b_scr[lax.rem(x + d, 4)]
 
 
-def middle_body(at_ref, loss_ref, got_a_ref, *refs):
-    b_refs, out_a, out_b, a_scr = refs[0:4], refs[4:8], refs[8], refs[9]
-    x = at_ref[1]
-    total_a = got_a_ref[0].astype(F32)
-    total_b = b_refs[0][...].astype(F32)
+def middle_a_body(at_ref, got_a_ref, *refs):
+    outs, a_scr = refs[0:4], refs[4]
+    total = got_a_ref[0].astype(F32)
     for d in range(1, 4):
-        total_a = total_a + got_a_ref[d].astype(F32)
-        total_b = total_b + b_refs[d][...].astype(F32)
-    out_b[:, 0:64, :] = total_b.reshape(4, 64, WB).astype(BF16)
+        total = total + got_a_ref[d].astype(F32)
+    a_scr[...] = total.reshape(8, 4, 8, WA)
+    for d in range(4):
+        outs[d][...] = (
+            a_scr[:, pl.ds(lax.rem(at_ref[1] + d, 4), 1)].reshape(64, WA).astype(BF16)
+        )
+
+
+def middle_b_body(loss_ref, *refs):
+    b_refs, out_b = refs[0:4], refs[4]
+    total = b_refs[0][...].astype(F32)
+    for d in range(1, 4):
+        total = total + b_refs[d][...].astype(F32)
+    out_b[:, 0:64, :] = total.reshape(4, 64, WB).astype(BF16)
     rest = jnp.broadcast_to(loss_ref[0:1, 0:1], (16, WB))
     lane = lax.broadcasted_iota(jnp.int32, (16, WB), 1)
     parts = jnp.zeros((16, WB), F32)
@@ -366,9 +375,6 @@
         rest = rest - part
     for y in range(4):
         out_b[y, 64:80, :] = parts.astype(BF16)
-    a_scr[...] = total_a.reshape(8, 4, 8, WA)
-    for d in range(4):
-        out_a[d][...] = a_scr[:, pl.ds(lax.rem(x + d, 4), 1)].reshape(64, WA).astype(BF16)
 
 
 def hidden_body(len_ref, h_ref, gain_ref, skv_ref, g_ref, last_ref, other_ref, sr_ref, kv_ref, got_ref, out_ref):
@@ -556,15 +562,17 @@
         [((ROWS, D), BF16)],
         flops=600_000_000,
     )
-    got_a, got_b, grad_hidden = lax.optimization_barrier((got_a, got_b, grad_hidden))
-    *mid_a, mid_b = call(
-        middle_body,
+    got_a, grad_hidden = lax.optimization_barrier((got_a, grad_hidden))
+    mid_a = call(
+        middle_a_body,
         [at],
-        [loss, got_a, *got_b],
-        [((64, WA), BF16)] * 4 + [((4, 80, WB), BF16)],
+        [got_a],
+        [((64, WA), BF16)] * 4,
         [((8, 4, 8, WA), F32)],
-        grant=52,
-    )
+        grant=62,
+    )
+    got_b, _ = lax.optimization_barrier((got_b, mid_a[0]))
+    (mid_b,) = call(middle_b_body, [], [loss, *got_b], [((4, 80, WB), BF16)])
     done_a = along_ring(mid_a, "x")
     done_b = lax.all_to_all(mid_b, "pb", 0, 0, tiled=True)
     loss = jnp.sum(done_b[:, 64, 0:3].astype(F32), axis=1)

time: 159 us -> 157 us (0.987)
  waiting for transfers between devices: 46.5 us -> 44.7 us
    ppermute x6, waiting for transfers between devices: 11.7 us -> 7.95 us  [along_ring(): lax.ppermute(pieces[d], axis, [(i, (i + d) % 4) for i in range(4)])]
    all_to_all x1, waiting for transfers between devices: 0.01 us -> 1.85 us  [shards(): got_a = lax.all_to_all(chip_a, 'pb', 0, 0, tiled=True)]
    pallas_call x10 -> x11, Pallas kernels: 34.3 us -> 35 us  [call(): pl.pallas_call(body, grid=(1,), out_shape=[jax.ShapeDtypeStruct(o, d) for...]
  transfers between devices with their start and end apart: 25 -> 25, of which waited for: 13 -> 14; matrix products, arithmetic and copies ran while one was open for 5% -> 5% of each run, Pallas kernels for 11% -> 13%
where the time goes in v7:
time: 157 us; the launch traced here: 156 us
  starting transfers between devices  60.9 us (39%)
  waiting for transfers between devices  44.7 us (28%)
  Pallas kernels  35 us (22%)
  local copies, waits for them, and re-layouts  10.3 us (7%)
  between operations  4.65 us (3%)
    pallas_call x11, Pallas kernels, call(): pl.pallas_call(body, grid=(1,), out_shape=[jax.ShapeDtypeStruct(o, d) for...  35 us
    ppermute x6, waiting for transfers between devices, from_ring(): lax.ppermute(x, axis, [(i, (i + d) % 4) for i in range(4)])  19.2 us
    all_to_all x1, starting transfers between devices, shards(): lax.all_to_all(both_halves, ('z', 'c'), 0, 0, tiled=True).reshape(64, 1536)  9.98 us
    ppermute x6, starting transfers between devices, from_ring(): lax.ppermute(x, axis, [(i, (i + d) % 4) for i in range(4)])  9.28 us
    ppermute x6, waiting for transfers between devices, along_ring(): lax.ppermute(pieces[d], axis, [(i, (i + d) % 4) for i in range(4)])  7.95 us
    all_to_all x1, waiting for transfers between devices, shards(): lax.all_to_all(part.reshape(16, 4, 1536), ('z', 'c'), 0, 0, tiled=True)  7.02 us
    ppermute x6, starting transfers between devices, along_ring(): lax.ppermute(pieces[d], axis, [(i, (i + d) % 4) for i in range(4)])  6.58 us
    all_to_all x1, starting transfers between devices, shards(): lax.all_to_all(part.reshape(16, 4, 1536), ('z', 'c'), 0, 0, tiled=True)  6.42 us
  transfers between devices with their start and end apart: 25, of which 14 were waited for; matrix products, arithmetic and copies ran while one was open for 5% of the time, Pallas kernels for 13%

profile of v7, /device:TPU:1, one launch (start us, length us, event | category | flops | bytes accessed | tf_op | source)
XLA Modules:
  0.0 156.0 jit_solution(13839750178199730)
XLA Ops:
  2.1 10.0 %all-to-all-start = ((bf16[16,4,1536]{2,1,0:T(4,128)(2,1)}), bf16[16,4,1536]{2,1,0:T(4,128)(2,1)S(1)}, u32[]{:S(2)}, u32[]{:S(2)}) async-start(bf16[16,4,1536]{2,1,0:T(4,128)(2,1)} %bitcast.44), calls=%async_computation | async-start | bytes 393216 | tf_op jit(solution)/shard_map/all_to_all | solution.py:468
  13.4 2.9 %shard_map.172 = (bf16[512,1024]{1,0:T(8,128)(2,1)S(1)}, bf16[1024,512]{1,0:T(8,128)(2,1)}, bf16[8,1024]{1,0:T(8,128)(2,1)S(1)}, f32[8,1024]{1,0:T(8,128)S(1)}) custom-call(s32[4]{0:T(128)S(1)} %bitcast.40, bf16[512,1024]{1,0:T(8,128)(2,1)} %bitcast.26, f32[1,1024]{1,0:T(1,128)S(1)} %bitcast.34), custom_call_target="tpu_custom_call" | custom-call | flops 10000000 | bytes 3198976 | tf_op jit(solution)/shard_map/pallas_call | solution.py:50
  17.4 5.1 %all-to-all-done = bf16[16,4,1536]{2,1,0:T(4,128)(2,1)S(1)} async-done(((bf16[16,4,1536]{2,1,0:T(4,128)(2,1)}), bf16[16,4,1536]{2,1,0:T(4,128)(2,1)S(1)}, u32[]{:S(2)}, u32[]{:S(2)}) %all-to-all-start) | async-done | bytes 196640 | tf_op jit(solution)/shard_map/all_to_all | solution.py:468
  23.3 4.2 %all-to-all-start.1 = ((bf16[4,64,768]{2,1,0:T(8,128)(2,1)}), bf16[4,64,768]{2,1,0:T(8,128)(2,1)S(1)}, u32[]{:S(2)}, u32[]{:S(2)}) async-start(bf16[4,64,768]{2,1,0:T(8,128)(2,1)} %broadcast_in_dim.32), calls=%async_computation.1 | async-start | bytes 786432 | tf_op jit(solution)/shard_map/all_to_all | solution.py:411
  28.7 2.5 %collective-permute-start.1 = (bf16[64,768]{1,0:T(8,128)(2,1)S(1)}, bf16[64,768]{1,0:T(8,128)(2,1)S(1)}, u32[]{:S(2)}, u32[]{:S(2)}) collective-permute-start(bf16[64,768]{1,0:T(8,128)(2,1)S(1)} %get-tuple-element.118.refs_0_), channel_id=1, source_target_pairs={{0,4},{2,6},{4,0},{6,2},{1,5},{3,7},{5,1},{7,3},{8,12},{10,14},{12... | collective-permute-start | bytes 294920 | tf_op jit(solution)/shard_map/ppermute | solution.py:418
  33.2 3.0 %collective-permute-done.1.refs_2_ = bf16[64,768]{1,0:T(8,128)(2,1)S(1)} collective-permute-done((bf16[64,768]{1,0:T(8,128)(2,1)S(1)}, bf16[64,768]{1,0:T(8,128)(2,1)S(1)}, u32[]{:S(2)}, u32[]{:S(2)}) %collective-permute-start.1) | collective-permute-done | bytes 98336 | tf_op jit(solution)/shard_map/ppermute | solution.py:418
  38.1 4.5 %all-to-all-start.2 = ((bf16[4,256,768]{2,1,0:T(8,128)(2,1)}), bf16[4,256,768]{2,1,0:T(8,128)(2,1)}, u32[]{:S(2)}, u32[]{:S(2)}) async-start(bf16[4,256,768]{2,1,0:T(8,128)(2,1)} %shard_map.173), calls=%async_computation.2 | async-start | bytes 3145728 | tf_op jit(solution)/shard_map/all_to_all | solution.py:499
  44.6 2.1 %collective-permute-start.6 = (bf16[256,768]{1,0:T(8,128)(2,1)S(1)}, bf16[256,768]{1,0:T(8,128)(2,1)S(1)}, u32[]{:S(2)}, u32[]{:S(2)}) collective-permute-start(bf16[256,768]{1,0:T(8,128)(2,1)S(1)} %bitcast.29), channel_id=1, source_target_pairs={{0,4},{2,6},{4,0},{6,2},{1,5},{3,7},{5,1},{7,3},{8,12},{10,14},{12... | collective-permute-start | bytes 1179656 | tf_op jit(solution)/shard_map/ppermute | solution.py:418
  48.2 7.4 %collective-permute-done.5.refs_1_.refs_2_ = bf16[256,768]{1,0:T(8,128)(2,1)S(1)} collective-permute-done((bf16[256,768]{1,0:T(8,128)(2,1)S(1)}, bf16[256,768]{1,0:T(8,128)(2,1)S(1)}, u32[]{:S(2)}, u32[]{:S(2)}) %collective-permute-start.5) | collective-permute-done | bytes 393248 | tf_op jit(solution)/shard_map/ppermute | solution.py:418
  55.6 8.8 %collective-permute-done.6.refs_2_.refs_3_ = bf16[256,768]{1,0:T(8,128)(2,1)S(1)} collective-permute-done((bf16[256,768]{1,0:T(8,128)(2,1)S(1)}, bf16[256,768]{1,0:T(8,128)(2,1)S(1)}, u32[]{:S(2)}, u32[]{:S(2)}) %collective-permute-start.6) | collective-permute-done | bytes 393248 | tf_op jit(solution)/shard_map/ppermute | solution.py:418
  64.4 6.0 %shard_map.174 = (f32[1024,256]{1,0:T(8,128)}, bf16[1024,256]{1,0:T(8,128)(2,1)}, bf16[1024,256]{1,0:T(8,128)(2,1)}, f32[8,512]{1,0:T(8,128)S(1)}, bf16[8,512]{1...) custom-call(s32[2]{0:T(128)S(1)} %pad_add_fusion.at_ref, ...), custom_call_target="tpu_custom_call" | custom-call | flops 1100000000 | bytes 8634368 | tf_op jit(solution)/shard_map/pallas_call | solution.py:50
  74.4 5.1 %all-to-all-start.3 = ((f32[32,1,128]{2,1,0:T(1,128)}), f32[32,1,128]{2,1,0:T(1,128)S(1)}, u32[]{:S(2)}, u32[]{:S(2)}) async-start(f32[32,1,128]{2,1,0:T(1,128)} %get-tuple-element.74), calls=%async_computation.3 | async-start | bytes 32768 | tf_op jit(solution)/shard_map/all_to_all | solution.py:530
  79.6 6.6 %shard_map.176 = (f32[1024,512]{1,0:T(8,128)}, f32[8,512]{1,0:T(8,128)S(1)}, f32[8,1024]{1,0:T(8,128)S(1)}, f32[8,1024]{1,0:T(8,128)S(1)}, bf16[512,1024]{1,0:T(8,128)(2,1)}) custom-call(s32[2]{0:T(128)S(1)} %pad_add_fusion.at_ref, s32[8]{0:T(128)S(1)} %convert_reduce_fusion.len_ref, bf16[1024,256]{1,0:T(8,128)(2,1)} %get-tuple-element.76.krot_ref, ...), custom_call_target="tpu_custom_call" | custom-call | flops 200000000 | bytes 9752576 | tf_op jit(solution)/shard_map/pallas_call | solution.py:50
  87.9 5.5 %shard_map.177 = (bf16[4,256,768]{2,1,0:T(8,128)(2,1)}, bf16[256,768]{1,0:T(8,128)(2,1)S(1)}, bf16[256,768]{1,0:T(8,128)(2,1)}, bf16[256,768]{1,0:T(8,128)(2,1)}...) custom-call(s32[2]{0:T(128)S(1)} %pad_add_fusion.at_ref, ...), custom_call_target="tpu_custom_call" | custom-call | flops 1100000000 | bytes 8560640 | tf_op jit(solution)/shard_map/pallas_call | solution.py:50
  93.4 4.5 %all-to-all-start.4 = ((bf16[4,256,768]{2,1,0:T(8,128)(2,1)}), bf16[4,256,768]{2,1,0:T(8,128)(2,1)}, u32[]{:S(2)}, u32[]{:S(2)}) async-start(bf16[4,256,768]{2,1,0:T(8,128)(2,1)} %get-tuple-element.97), calls=%async_computation.4 | async-start | bytes 3145728 | tf_op jit(solution)/shard_map/all_to_all | solution.py:556
  104.0 2.2 %copy.28 = f32[8,32,4,8]{3,2,1,0:T(4,128)} copy(f32[8,32,4,8]{3,1,2,0:T(8,128)} %bitcast.41) | data formatting | bytes 65536 | tf_op jit(solution)/shard_map/transpose | solution.py:433
  109.6 5.5 %shard_map.178 = bf16[512,1024]{1,0:T(8,128)(2,1)} custom-call(s32[8]{0:T(128)S(1)} %convert_reduce_fusion.len_ref, bf16[512,1024]{1,0:T(8,128)(2,1)S(1)} %bitcast.27, f32[1,1024]{1,0:T(1,128)S(1)} %bitcast.35, bf16[1024,512]{1,0:T(8,128)(2,1)} %get-tuple-element.98.skv_ref, f32[8,128]{1,0:T(8,128)S(1)} %get-tuple-element.99.g_ref, ...), custom_call_target="tpu_custom_call" | custom-call | flops 600000000 | bytes 5873664 | tf_op jit(solution)/shard_map/pallas_call | solution.py:50
  116.9 2.5 %shard_map.179 = (bf16[64,768]{1,0:T(8,128)(2,1)}, bf16[64,768]{1,0:T(8,128)(2,1)}, bf16[64,768]{1,0:T(8,128)(2,1)}, bf16[64,768]{1,0:T(8,128)(2,1)}) custom-call(s32[2]{0:T(128)} %copy-done.8, bf16[4,256,768]{2,1,0:T(8,128)(2,1)} %all-to-all-done.4.got_a_ref), custom_call_target="tpu_custom_call" | custom-call | bytes 1966080 | tf_op jit(solution)/shard_map/pallas_call | solution.py:50
  121.8 4.5 %all-to-all-start.5 = ((bf16[4,80,768]{2,1,0:T(8,128)(2,1)}), bf16[4,80,768]{2,1,0:T(8,128)(2,1)S(1)}, u32[]{:S(2)}, u32[]{:S(2)}) async-start(bf16[4,80,768]{2,1,0:T(8,128)(2,1)} %shard_map.180), calls=%async_computation.5 | async-start | bytes 983040 | tf_op jit(solution)/shard_map/all_to_all | solution.py:577
  126.3 2.8 %collective-permute-start.17 = (bf16[64,768]{1,0:T(8,128)(2,1)S(1)}, bf16[64,768]{1,0:T(8,128)(2,1)S(1)}, u32[]{:S(2)}, u32[]{:S(2)}) collective-permute-start(bf16[64,768]{1,0:T(8,128)(2,1)S(1)} %copy-done.15), channel_id=1, source_target_pairs={{0,6},{2,0},{4,2},{6,4},{1,7},{3,1},{5,3},{7,5},{8,14},{10,8},{12,... | collective-permute-start | bytes 294920 | tf_op jit(solution)/shard_map/ppermute | solution.py:424
  131.2 3.0 %collective-permute-done.16 = bf16[64,768]{1,0:T(8,128)(2,1)S(1)} collective-permute-done((bf16[64,768]{1,0:T(8,128)(2,1)S(1)}, bf16[64,768]{1,0:T(8,128)(2,1)S(1)}, u32[]{:S(2)}, u32[]{:S(2)}) %collective-permute-start.16) | collective-permute-done | bytes 98336 | tf_op jit(solution)/shard_map/ppermute | solution.py:424
  134.2 2.4 %collective-permute-done.15 = bf16[64,768]{1,0:T(8,128)(2,1)S(1)} collective-permute-done((bf16[64,768]{1,0:T(8,128)(2,1)S(1)}, bf16[64,768]{1,0:T(8,128)(2,1)S(1)}, u32[]{:S(2)}, u32[]{:S(2)}) %collective-permute-start.15) | collective-permute-done | bytes 98336 | tf_op jit(solution)/shard_map/ppermute | solution.py:424
  137.5 6.4 %all-to-all-start.6 = ((bf16[16,4,1536]{2,1,0:T(4,128)(2,1)}), bf16[16,4,1536]{2,1,0:T(4,128)(2,1)S(1)}, u32[]{:S(2)}, u32[]{:S(2)}) async-start(bf16[16,4,1536]{2,1,0:T(4,128)(2,1)} %reshape.88), calls=%async_computation.6 | async-start | bytes 393216 | tf_op jit(solution)/shard_map/all_to_all | solution.py:589
  147.3 7.0 %all-to-all-done.6 = bf16[16,4,1536]{2,1,0:T(4,128)(2,1)S(1)} async-done(((bf16[16,4,1536]{2,1,0:T(4,128)(2,1)}), bf16[16,4,1536]{2,1,0:T(4,128)(2,1)S(1)}, u32[]{:S(2)}, u32[]{:S(2)}) %all-to-all-start.6) | async-done | bytes 196640 | tf_op jit(solution)/shard_map/all_to_all | solution.py:589
  (99 shorter events, 37.0 us)
Async XLA Ops:
  2.1 20.3 %all-to-all-start = ((bf16[16,4,1536]{2,1,0:T(4,128)(2,1)}), bf16[16,4,1536]{2,1,0:T(4,128)(2,1)S(1)}, u32[]{:S(2)}, u32[]{:S(2)}) async-start(bf16[16,4,1536]{2,1,0:T(4,128)(2,1)} %bitcast.44), calls=%async_computation | async-start | bytes 393216 | tf_op jit(solution)/shard_map/all_to_all | solution.py:468
  23.3 14.8 %all-to-all-start.1 = ((bf16[4,64,768]{2,1,0:T(8,128)(2,1)}), bf16[4,64,768]{2,1,0:T(8,128)(2,1)S(1)}, u32[]{:S(2)}, u32[]{:S(2)}) async-start(bf16[4,64,768]{2,1,0:T(8,128)(2,1)} %broadcast_in_dim.32), calls=%async_computation.1 | async-start | bytes 786432 | tf_op jit(solution)/shard_map/all_to_all | solution.py:411
  27.5 5.7 %collective-permute-start = (bf16[64,768]{1,0:T(8,128)(2,1)S(1)}, bf16[64,768]{1,0:T(8,128)(2,1)S(1)}, u32[]{:S(2)}, u32[]{:S(2)}) collective-permute-start(bf16[64,768]{1,0:T(8,128)(2,1)S(1)} %get-tuple-element.118.refs_0_), channel_id=1, source_target_pairs={{0,2},{2,4},{4,6},{6,0},{1,3},{3,5},{5,7},{7,1},{8,10},{10,12},{12... | collective-permute-start | bytes 294920 | tf_op jit(solution)/shard_map/ppermute | solution.py:418
  28.7 7.5 %collective-permute-start.1 = (bf16[64,768]{1,0:T(8,128)(2,1)S(1)}, bf16[64,768]{1,0:T(8,128)(2,1)S(1)}, u32[]{:S(2)}, u32[]{:S(2)}) collective-permute-start(bf16[64,768]{1,0:T(8,128)(2,1)S(1)} %get-tuple-element.118.refs_0_), channel_id=1, source_target_pairs={{0,4},{2,6},{4,0},{6,2},{1,5},{3,7},{5,1},{7,3},{8,12},{10,14},{12... | collective-permute-start | bytes 294920 | tf_op jit(solution)/shard_map/ppermute | solution.py:418
  31.1 5.1 %collective-permute-start.2 = (bf16[64,768]{1,0:T(8,128)(2,1)S(1)}, bf16[64,768]{1,0:T(8,128)(2,1)S(1)}, u32[]{:S(2)}, u32[]{:S(2)}) collective-permute-start(bf16[64,768]{1,0:T(8,128)(2,1)S(1)} %get-tuple-element.118.refs_0_), channel_id=1, source_target_pairs={{0,6},{2,0},{4,2},{6,4},{1,7},{3,1},{5,3},{7,5},{8,14},{10,8},{12,... | collective-permute-start | bytes 294920 | tf_op jit(solution)/shard_map/ppermute | solution.py:418
  32.3 5.8 %collective-permute-start.3 = (f32[4,2304]{1,0:T(4,128)S(1)}, f32[4,2304]{1,0:T(4,128)S(1)}, u32[]{:S(2)}, u32[]{:S(2)}) collective-permute-start(f32[4,2304]{1,0:T(4,128)S(1)} %pad_maximum_fusion.1), channel_id=1, source_target_pairs={{0,1},{1,0},{2,3},{3,2},{4,5},{5,4},{6,7},{7,6},{8,9},{9,8},{10,11... | collective-permute-start | bytes 110600 | tf_op jit(solution)/shard_map/ppermute | solution.py:437
  38.1 26.3 %all-to-all-start.2 = ((bf16[4,256,768]{2,1,0:T(8,128)(2,1)}), bf16[4,256,768]{2,1,0:T(8,128)(2,1)}, u32[]{:S(2)}, u32[]{:S(2)}) async-start(bf16[4,256,768]{2,1,0:T(8,128)(2,1)} %shard_map.173), calls=%async_computation.2 | async-start | bytes 3145728 | tf_op jit(solution)/shard_map/all_to_all | solution.py:499
  42.6 21.8 %collective-permute-start.4 = (bf16[512,1024]{1,0:T(8,128)(2,1)S(1)}, bf16[512,1024]{1,0:T(8,128)(2,1)}, u32[]{:S(2)}, u32[]{:S(2)}) collective-permute-start(bf16[512,1024]{1,0:T(8,128)(2,1)S(1)} %get-tuple-element.69.normed_ref), channel_id=1, source_target_pairs={{0,1},{1,0},{2,3},{3,2},{4,5},{5,4},{6,7},{7,6},{8,9},{9,8},{10,11... | collective-permute-start | bytes 3145736 | tf_op jit(solution)/shard_map/ppermute | solution.py:437
  43.6 12.0 %collective-permute-start.5 = (bf16[256,768]{1,0:T(8,128)(2,1)S(1)}, bf16[256,768]{1,0:T(8,128)(2,1)S(1)}, u32[]{:S(2)}, u32[]{:S(2)}) collective-permute-start(bf16[256,768]{1,0:T(8,128)(2,1)S(1)} %bitcast.28), channel_id=1, source_target_pairs={{0,2},{2,4},{4,6},{6,0},{1,3},{3,5},{5,7},{7,1},{8,10},{10,12},{12... | collective-permute-start | bytes 1179656 | tf_op jit(solution)/shard_map/ppermute | solution.py:418
  44.6 19.7 %collective-permute-start.6 = (bf16[256,768]{1,0:T(8,128)(2,1)S(1)}, bf16[256,768]{1,0:T(8,128)(2,1)S(1)}, u32[]{:S(2)}, u32[]{:S(2)}) collective-permute-start(bf16[256,768]{1,0:T(8,128)(2,1)S(1)} %bitcast.29), channel_id=1, source_target_pairs={{0,4},{2,6},{4,0},{6,2},{1,5},{3,7},{5,1},{7,3},{8,12},{10,14},{12... | collective-permute-start | bytes 1179656 | tf_op jit(solution)/shard_map/ppermute | solution.py:418
  46.8 17.6 %collective-permute-start.7 = (bf16[256,768]{1,0:T(8,128)(2,1)S(1)}, bf16[256,768]{1,0:T(8,128)(2,1)S(1)}, u32[]{:S(2)}, u32[]{:S(2)}) collective-permute-start(bf16[256,768]{1,0:T(8,128)(2,1)S(1)} %bitcast.30), channel_id=1, source_target_pairs={{0,6},{2,0},{4,2},{6,4},{1,7},{3,1},{5,3},{7,5},{8,14},{10,8},{12,... | collective-permute-start | bytes 1179656 | tf_op jit(solution)/shard_map/ppermute | solution.py:418
  70.4 17.5 %collective-permute-start.9 = (bf16[1024,512]{1,0:T(8,128)(2,1)}, bf16[1024,512]{1,0:T(8,128)(2,1)}, u32[]{:S(2)}, u32[]{:S(2)}) collective-permute-start(bf16[1024,512]{1,0:T(8,128)(2,1)} %get-tuple-element.90.turned_ref), channel_id=1, source_target_pairs={{0,1},{1,0},{2,3},{3,2},{4,5},{5,4},{6,7},{7,6},{8,9},{9,8},{10,11... | collective-permute-start | bytes 3145736 | tf_op jit(solution)/shard_map/ppermute | solution.py:437
  71.4 2.2 %collective-permute-start.8 = (f32[8,1024]{1,0:T(8,128)S(1)}, f32[8,1024]{1,0:T(8,128)S(1)}, u32[]{:S(2)}, u32[]{:S(2)}) collective-permute-start(f32[8,1024]{1,0:T(8,128)S(1)} %get-tuple-element.72.mine_ref), channel_id=1, source_target_pairs={{0,1},{1,0},{2,3},{3,2},{4,5},{5,4},{6,7},{7,6},{8,9},{9,8},{10,11... | collective-permute-start | bytes 98312 | tf_op jit(solution)/shard_map/ppermute | solution.py:437
  74.4 13.5 %all-to-all-start.3 = ((f32[32,1,128]{2,1,0:T(1,128)}), f32[32,1,128]{2,1,0:T(1,128)S(1)}, u32[]{:S(2)}, u32[]{:S(2)}) async-start(f32[32,1,128]{2,1,0:T(1,128)} %get-tuple-element.74), calls=%async_computation.3 | async-start | bytes 32768 | tf_op jit(solution)/shard_map/all_to_all | solution.py:530
  93.4 23.6 %all-to-all-start.4 = ((bf16[4,256,768]{2,1,0:T(8,128)(2,1)}), bf16[4,256,768]{2,1,0:T(8,128)(2,1)}, u32[]{:S(2)}, u32[]{:S(2)}) async-start(bf16[4,256,768]{2,1,0:T(8,128)(2,1)} %get-tuple-element.97), calls=%async_computation.4 | async-start | bytes 3145728 | tf_op jit(solution)/shard_map/all_to_all | solution.py:556
  97.9 11.7 %collective-permute-start.14 = (bf16[512,1024]{1,0:T(8,128)(2,1)}, bf16[512,1024]{1,0:T(8,128)(2,1)}, u32[]{:S(2)}, u32[]{:S(2)}) collective-permute-start(bf16[512,1024]{1,0:T(8,128)(2,1)} %get-tuple-element.102), channel_id=1, source_target_pairs={{0,1},{1,0},{2,3},{3,2},{4,5},{5,4},{6,7},{7,6},{8,9},{9,8},{10,11... | collective-permute-start | bytes 3145736 | tf_op jit(solution)/shard_map/ppermute | solution.py:437
  99.8 19.7 %collective-permute-start.10 = (bf16[256,768]{1,0:T(8,128)(2,1)}, bf16[256,768]{1,0:T(8,128)(2,1)S(1)}, u32[]{:S(2)}, u32[]{:S(2)}) collective-permute-start(bf16[256,768]{1,0:T(8,128)(2,1)} %get-tuple-element.94), channel_id=1, source_target_pairs={{0,2},{2,4},{4,6},{6,0},{1,3},{3,5},{5,7},{7,1},{8,10},{10,12},{12... | collective-permute-start | bytes 1179656 | tf_op jit(solution)/shard_map/ppermute | solution.py:424
  100.1 19.7 %collective-permute-start.11 = (bf16[256,768]{1,0:T(8,128)(2,1)}, bf16[256,768]{1,0:T(8,128)(2,1)S(1)}, u32[]{:S(2)}, u32[]{:S(2)}) collective-permute-start(bf16[256,768]{1,0:T(8,128)(2,1)} %get-tuple-element.95), channel_id=1, source_target_pairs={{0,4},{2,6},{4,0},{6,2},{1,5},{3,7},{5,1},{7,3},{8,12},{10,14},{12... | collective-permute-start | bytes 1179656 | tf_op jit(solution)/shard_map/ppermute | solution.py:424
  102.0 18.7 %collective-permute-start.12 = (bf16[256,768]{1,0:T(8,128)(2,1)S(1)}, bf16[256,768]{1,0:T(8,128)(2,1)S(1)}, u32[]{:S(2)}, u32[]{:S(2)}) collective-permute-start(bf16[256,768]{1,0:T(8,128)(2,1)S(1)} %get-tuple-element.96), channel_id=1, source_target_pairs={{0,6},{2,0},{4,2},{6,4},{1,7},{3,1},{5,3},{7,5},{8,14},{10,8},{12,... | collective-permute-start | bytes 1179656 | tf_op jit(solution)/shard_map/ppermute | solution.py:424
  121.8 14.9 %all-to-all-start.5 = ((bf16[4,80,768]{2,1,0:T(8,128)(2,1)}), bf16[4,80,768]{2,1,0:T(8,128)(2,1)S(1)}, u32[]{:S(2)}, u32[]{:S(2)}) async-start(bf16[4,80,768]{2,1,0:T(8,128)(2,1)} %shard_map.180), calls=%async_computation.5 | async-start | bytes 983040 | tf_op jit(solution)/shard_map/all_to_all | solution.py:577
  126.3 4.9 %collective-permute-start.17 = (bf16[64,768]{1,0:T(8,128)(2,1)S(1)}, bf16[64,768]{1,0:T(8,128)(2,1)S(1)}, u32[]{:S(2)}, u32[]{:S(2)}) collective-permute-start(bf16[64,768]{1,0:T(8,128)(2,1)S(1)} %copy-done.15), channel_id=1, source_target_pairs={{0,6},{2,0},{4,2},{6,4},{1,7},{3,1},{5,3},{7,5},{8,14},{10,8},{12,... | collective-permute-start | bytes 294920 | tf_op jit(solution)/shard_map/ppermute | solution.py:424
  129.2 5.1 %collective-permute-start.16 = (bf16[64,768]{1,0:T(8,128)(2,1)S(1)}, bf16[64,768]{1,0:T(8,128)(2,1)S(1)}, u32[]{:S(2)}, u32[]{:S(2)}) collective-permute-start(bf16[64,768]{1,0:T(8,128)(2,1)S(1)} %copy-done.14), channel_id=1, source_target_pairs={{0,4},{2,6},{4,0},{6,2},{1,5},{3,7},{5,1},{7,3},{8,12},{10,14},{12... | collective-permute-start | bytes 294920 | tf_op jit(solution)/shard_map/ppermute | solution.py:424
  129.2 7.5 %collective-permute-start.15 = (bf16[64,768]{1,0:T(8,128)(2,1)S(1)}, bf16[64,768]{1,0:T(8,128)(2,1)S(1)}, u32[]{:S(2)}, u32[]{:S(2)}) collective-permute-start(bf16[64,768]{1,0:T(8,128)(2,1)S(1)} %copy-done.13), channel_id=1, source_target_pairs={{0,2},{2,4},{4,6},{6,0},{1,3},{3,5},{5,7},{7,1},{8,10},{10,12},{12... | collective-permute-start | bytes 294920 | tf_op jit(solution)/shard_map/ppermute | solution.py:424
  137.5 16.7 %all-to-all-start.6 = ((bf16[16,4,1536]{2,1,0:T(4,128)(2,1)}), bf16[16,4,1536]{2,1,0:T(4,128)(2,1)S(1)}, u32[]{:S(2)}, u32[]{:S(2)}) async-start(bf16[16,4,1536]{2,1,0:T(4,128)(2,1)} %reshape.88), calls=%async_computation.6 | async-start | bytes 393216 | tf_op jit(solution)/shard_map/all_to_all | solution.py:589
  (17 other events, 254.8 us)
